TPU v7x, 32 devices: a whole 2x2x4 slice. The times are simulated.
32 devices in a mesh: dp: 16 (over z, y, x), tensor: 2 (over core).
Axes of the slice: x: 2, y: 2, z: 4, core: 2. Of those that a mesh axis runs over, the one named last changes fastest.
Arguments:
- tokens: bfloat16 [16, 256, 2048], P('dp', 'tensor'), may hold values from -6 to 6
- doc_lengths: int32 [16, 4], P('dp'), may hold values from 0 to 255, as said below
- recurrent_norm_gain: bfloat16 [2048], P('dp'), may hold values from 0.25 to 1.75
- w_branch: bfloat16 [2048, 2560], P('dp', 'tensor'), may hold values from -0.125 to 0.125
- w_input: bfloat16 [2048, 2560], P('dp', 'tensor'), may hold values from -0.125 to 0.125
- w_rgate: bfloat16 [10, 256, 256], P('tensor', 'dp'), may hold values from -0.375 to 0.375
- w_igate: bfloat16 [10, 256, 256], P('tensor', 'dp'), may hold values from -0.375 to 0.375
- rgate_bias: bfloat16 [10, 256], P('tensor', 'dp'), may hold values from -3 to 3
- igate_bias: bfloat16 [10, 256], P('tensor', 'dp'), may hold values from -3 to 3
- decay_param: bfloat16 [10, 256], P('tensor', 'dp'), may hold values from 4.1875 to 8.5
- conv_weight: bfloat16 [4, 10, 256], P(None, 'tensor', 'dp'), may hold values from -3 to 3
- conv_bias: bfloat16 [10, 256], P('tensor', 'dp'), may hold values from -2 to 2
- w_output: bfloat16 [2560, 2048], P('tensor', 'dp'), may hold values from -0.25 to 0.25
- perceptron_norm_gain: bfloat16 [2048], P('dp'), may hold values from 0.25 to 1.75
- w_gate: bfloat16 [2048, 6144], P('dp', 'tensor'), may hold values from -0.125 to 0.125
- w_up: bfloat16 [2048, 6144], P('dp', 'tensor'), may hold values from -0.125 to 0.125
- w_down: bfloat16 [6144, 2048], P('tensor', 'dp'), may hold values from -0.078125 to 0.078125
- cotangent: float32 [16, 256, 2048], P('dp', 'tensor'), may hold values from -6 to 6
Outputs:
- result: bfloat16 [16, 256, 2048], P('dp', 'tensor')
- token_input_gradient: float32 [16, 256, 2048], P('dp', 'tensor')
- grad_rec_gain: float32 [2048], P('dp')
- grad_w_branch: float32 [2048, 2560], P('dp', 'tensor')
- grad_w_input: float32 [2048, 2560], P('dp', 'tensor')
- grad_w_rgate: float32 [10, 256, 256], P('tensor', 'dp')
- grad_w_igate: float32 [10, 256, 256], P('tensor', 'dp')
- grad_rgate_bias: float32 [10, 256], P('tensor', 'dp')
- grad_igate_bias: float32 [10, 256], P('tensor', 'dp')
- grad_decay_param: float32 [10, 256], P('tensor', 'dp')
- grad_conv_weight: float32 [4, 10, 256], P(None, 'tensor', 'dp')
- grad_conv_bias: float32 [10, 256], P('tensor', 'dp')
- grad_w_output: float32 [2560, 2048], P('tensor', 'dp')
- grad_mlp_gain: float32 [2048], P('dp')
- grad_w_gate: float32 [2048, 6144], P('dp', 'tensor')
- grad_w_up: float32 [2048, 6144], P('dp', 'tensor')
- grad_w_down: float32 [6144, 2048], P('tensor', 'dp')
Inputs may be any that keep to these rules, and one draw needn't show every extreme that they name: `doc_lengths`: in each row the 4 lengths are documents placed one after another from the row's first position, the first at least one token long; together they cover more than 128 positions and the positions after them are padding.
All inputs are finite; a program needn't handle non-finite values.
Results may differ from a plain program's by a relative error of at most 0.015.
Values may be sent and summed in bfloat16 or wider, within the bound.
A program may use at most 256 MiB of HBM per device.

v0:
```python
import jax
import jax.numpy as jnp
from jax import lax
from jax.sharding import PartitionSpec as P

norm_epsilon = 1e-06
decay_scale = 8.0


def gelu_tanh(values):
    return jax.nn.gelu(values, approximate=True)


def combine(first, second):
    return (first[0] * second[0], second[0] * first[1] + second[1])


def doc_layout(doc_lengths, length):
    ends = jnp.cumsum(doc_lengths, axis=-1)
    places = jnp.arange(length, dtype=jnp.int32)
    segment = jnp.sum((places[None, :, None] >= ends[:, None, :]).astype(jnp.int32), axis=-1)
    valid = places[None, :] < ends[:, -1:]
    earlier = jnp.pad(segment, ((0, 0), (1, 0)), constant_values=-1)[:, :-1]
    start = earlier != segment
    return (segment, valid, start)


def conv_mix(values, weights, bias, segment):
    total = values * weights[0] + bias
    for shift in range(1, weights.shape[0]):
        moved = jnp.pad(values, ((0, 0), (shift, 0), (0, 0)))[:, :-shift]
        earlier = jnp.pad(segment, ((0, 0), (shift, 0)), constant_values=-1)[:, :-shift]
        total = total + jnp.where((earlier == segment)[..., None], moved, 0.0) * weights[shift]
    return total


def gate_terms(pre_r, pre_i, conv_out, decay_row, start_col):
    rate = jax.nn.sigmoid(pre_r)
    entry = jax.nn.sigmoid(pre_i)
    log_decay = -decay_scale * rate * jax.nn.softplus(-decay_row)
    a_eff = jnp.where(start_col, 0.0, jnp.exp(log_decay))
    scaling = jnp.where(start_col, 1.0, jnp.sqrt(-jnp.expm1(2.0 * log_decay)))
    return (a_eff, scaling * entry * conv_out)


def rows_product(left, right):
    return lax.dot_general(
        left, right, (((0,), (0,)), ((), ())), preferred_element_type=jnp.float32
    )


def back_product(left, right):
    return lax.dot_general(
        left, right, (((1,), (1,)), ((), ())), preferred_element_type=jnp.float32
    )


def norm_scale(values):
    return lax.rsqrt(jnp.mean(values * values, axis=-1, keepdims=True) + norm_epsilon)


def norm_backward_pass(grad, normalized_rows, inverse):
    return inverse * (
        grad - normalized_rows * jnp.mean(grad * normalized_rows, axis=-1, keepdims=True)
    )


def local(
    tokens,
    doc_lengths,
    recurrent_norm_gain,
    w_branch,
    w_input,
    w_rgate,
    w_igate,
    rgate_bias,
    igate_bias,
    decay_param,
    conv_weight,
    conv_bias,
    w_output,
    perceptron_norm_gain,
    w_gate,
    w_up,
    w_down,
    cotangent,
):
    (
        rec_gain_all,
        w_branch_all,
        w_input_all,
        w_rgate_all,
        w_igate_all,
        rbias_all,
        ibias_all,
        decay_all,
        conv_w_all,
        conv_b_all,
        w_output_all,
    ) = (
        lax.all_gather(recurrent_norm_gain, "dp", axis=0, tiled=True),
        lax.all_gather(w_branch, "dp", axis=0, tiled=True),
        lax.all_gather(w_input, "dp", axis=0, tiled=True),
        lax.all_gather(w_rgate, "dp", axis=1, tiled=True),
        lax.all_gather(w_igate, "dp", axis=1, tiled=True),
        lax.all_gather(rgate_bias, "dp", axis=1, tiled=True),
        lax.all_gather(igate_bias, "dp", axis=1, tiled=True),
        lax.all_gather(decay_param, "dp", axis=1, tiled=True),
        lax.all_gather(conv_weight, "dp", axis=2, tiled=True),
        lax.all_gather(conv_bias, "dp", axis=1, tiled=True),
        lax.all_gather(w_output, "dp", axis=1, tiled=True),
    )
    mlp_gain_all, w_gate_all, w_up_all, w_down_all = (
        lax.all_gather(perceptron_norm_gain, "dp", axis=0, tiled=True),
        lax.all_gather(w_gate, "dp", axis=0, tiled=True),
        lax.all_gather(w_up, "dp", axis=0, tiled=True),
        lax.all_gather(w_down, "dp", axis=1, tiled=True),
    )
    row_count, half_len, width = tokens.shape
    full_len = half_len * lax.axis_size("tensor")
    head_count, block_size = rbias_all.shape
    channels = head_count * block_size
    conv_taps = conv_w_all.shape[0]
    segment, valid, start = doc_layout(doc_lengths, full_len)
    offset = lax.axis_index("tensor") * half_len
    valid_own = lax.dynamic_slice_in_dim(valid, offset, half_len, 1)[..., None]
    start_col = start.reshape(-1, 1)
    first_gain_vector = rec_gain_all.astype(jnp.float32)
    second_gain_vector = mlp_gain_all.astype(jnp.float32)
    layer_input_rows = tokens.astype(jnp.float32)
    first_norm_scale = norm_scale(layer_input_rows)
    first_unit_rows = layer_input_rows * first_norm_scale
    normalized_input_rows = lax.all_gather(
        (first_unit_rows * first_gain_vector).astype(jnp.bfloat16), "tensor", axis=1, tiled=True
    ).reshape(-1, width)
    branch_pre = jnp.dot(normalized_input_rows, w_branch_all, preferred_element_type=jnp.float32)
    conv_in = jnp.dot(normalized_input_rows, w_input_all, preferred_element_type=jnp.float32)
    conv_flat = conv_w_all.astype(jnp.float32).reshape(conv_taps, channels)
    conv_shift = conv_b_all.astype(jnp.float32).reshape(channels)

    def conv_local(values, weights, bias):
        return conv_mix(
            values.reshape(row_count, full_len, channels), weights, bias, segment
        ).reshape(-1, channels)

    conv_out, conv_back = jax.vjp(conv_local, conv_in, conv_flat, conv_shift)
    conv_low = conv_out.astype(jnp.bfloat16).reshape(-1, head_count, block_size)
    pre_r = jnp.einsum(
        "phi,hij->phj", conv_low, w_rgate_all, preferred_element_type=jnp.float32
    ).reshape(-1, channels)
    pre_r = pre_r + rbias_all.astype(jnp.float32).reshape(channels)
    pre_i = jnp.einsum(
        "phi,hij->phj", conv_low, w_igate_all, preferred_element_type=jnp.float32
    ).reshape(-1, channels)
    pre_i = pre_i + ibias_all.astype(jnp.float32).reshape(channels)
    decay_row = decay_all.astype(jnp.float32).reshape(channels)

    def gate_local(rate_pre, entry_pre, values, decay_vals):
        return gate_terms(rate_pre, entry_pre, values, decay_vals, start_col)

    (a_eff, drive), gate_back = jax.vjp(gate_local, pre_r, pre_i, conv_out, decay_row)
    state = lax.associative_scan(combine, (a_eff, drive), axis=0)[1]
    branch_act, branch_back = jax.vjp(gelu_tanh, branch_pre)
    mixed = (state * branch_act).astype(jnp.bfloat16)
    rec_part = jnp.dot(mixed, w_output_all, preferred_element_type=jnp.float32).reshape(
        row_count, full_len, width
    )
    residual_stream = layer_input_rows + lax.psum_scatter(
        rec_part.astype(jnp.bfloat16), "tensor", scatter_dimension=1, tiled=True
    ).astype(jnp.float32)
    second_norm_scale = norm_scale(residual_stream)
    second_unit_rows = residual_stream * second_norm_scale
    normalized_rows = lax.all_gather(
        (second_unit_rows * second_gain_vector).astype(jnp.bfloat16), "tensor", axis=1, tiled=True
    ).reshape(-1, width)
    gate_pre = jnp.dot(normalized_rows, w_gate_all, preferred_element_type=jnp.float32)
    up_pre = jnp.dot(normalized_rows, w_up_all, preferred_element_type=jnp.float32)
    gate_act, gate_back_fn = jax.vjp(gelu_tanh, gate_pre)
    hidden = (gate_act * up_pre).astype(jnp.bfloat16)
    mlp_part = jnp.dot(hidden, w_down_all, preferred_element_type=jnp.float32).reshape(
        row_count, full_len, width
    )
    mlp_out = lax.psum_scatter(
        mlp_part.astype(jnp.bfloat16), "tensor", scatter_dimension=1, tiled=True
    ).astype(jnp.float32)
    result = jnp.where(valid_own, residual_stream + mlp_out, 0.0).astype(jnp.bfloat16)
    output_gradient = jnp.where(valid_own, cotangent, 0.0)
    mlp_grad = lax.all_gather(
        output_gradient.astype(jnp.bfloat16), "tensor", axis=1, tiled=True
    ).reshape(-1, width)
    grad_w_down = rows_product(hidden, mlp_grad)
    hidden_grad = back_product(mlp_grad, w_down_all)
    gate_grad = gate_back_fn(hidden_grad * up_pre)[0].astype(jnp.bfloat16)
    up_grad = (hidden_grad * gate_act).astype(jnp.bfloat16)
    grad_w_gate = rows_product(normalized_rows, gate_grad)
    grad_w_up = rows_product(normalized_rows, up_grad)
    normed_part = (back_product(gate_grad, w_gate_all) + back_product(up_grad, w_up_all)).reshape(
        row_count, full_len, width
    )
    normalized_rows_gradient = lax.psum_scatter(
        normed_part.astype(jnp.bfloat16), "tensor", scatter_dimension=1, tiled=True
    ).astype(jnp.float32)
    second_gain_portion = jnp.sum(normalized_rows_gradient * second_unit_rows, axis=(0, 1))
    residual_stream_gradient = output_gradient + norm_backward_pass(
        normalized_rows_gradient * second_gain_vector, second_unit_rows, second_norm_scale
    )
    rec_grad = lax.all_gather(
        residual_stream_gradient.astype(jnp.bfloat16), "tensor", axis=1, tiled=True
    ).reshape(-1, width)
    grad_w_output = rows_product(mixed, rec_grad)
    mixed_grad = back_product(rec_grad, w_output_all)
    state_grad = mixed_grad * branch_act
    branch_grad = branch_back(mixed_grad * state)[0].astype(jnp.bfloat16)
    a_next = jnp.concatenate([a_eff[1:], jnp.zeros_like(a_eff[:1])], axis=0)
    carried = lax.associative_scan(combine, (a_next, state_grad), reverse=True, axis=0)[1]
    state_prev = jnp.concatenate([jnp.zeros_like(state[:1]), state[:-1]], axis=0)
    rate_grad, entry_grad, conv_direct, decay_grad = gate_back((carried * state_prev, carried))
    rate_low = rate_grad.astype(jnp.bfloat16).reshape(-1, head_count, block_size)
    entry_low = entry_grad.astype(jnp.bfloat16).reshape(-1, head_count, block_size)
    grad_w_rgate = jnp.einsum(
        "phi,phj->hij", conv_low, rate_low, preferred_element_type=jnp.float32
    )
    grad_w_igate = jnp.einsum(
        "phi,phj->hij", conv_low, entry_low, preferred_element_type=jnp.float32
    )
    conv_grad = conv_direct + (
        jnp.einsum("phj,hij->phi", rate_low, w_rgate_all, preferred_element_type=jnp.float32)
        + jnp.einsum("phj,hij->phi", entry_low, w_igate_all, preferred_element_type=jnp.float32)
    ).reshape(-1, channels)
    input_grad_f, conv_w_grad, conv_b_grad = conv_back(conv_grad)
    input_grad = input_grad_f.astype(jnp.bfloat16)
    grad_w_branch = rows_product(normalized_input_rows, branch_grad)
    grad_w_input = rows_product(normalized_input_rows, input_grad)
    input_part = (
        back_product(branch_grad, w_branch_all) + back_product(input_grad, w_input_all)
    ).reshape(row_count, full_len, width)
    normalized_input_gradient = lax.psum_scatter(
        input_part.astype(jnp.bfloat16), "tensor", scatter_dimension=1, tiled=True
    ).astype(jnp.float32)
    first_gain_portion = jnp.sum(normalized_input_gradient * first_unit_rows, axis=(0, 1))
    token_input_gradient = residual_stream_gradient + norm_backward_pass(
        normalized_input_gradient * first_gain_vector, first_unit_rows, first_norm_scale
    )
    gain_one_sum, gain_two_sum = lax.psum((first_gain_portion, second_gain_portion), "tensor")
    grad_rbias = jnp.sum(rate_grad, axis=0).reshape(head_count, block_size)
    grad_ibias = jnp.sum(entry_grad, axis=0).reshape(head_count, block_size)
    grad_decay = decay_grad.reshape(head_count, block_size)
    grad_conv_w = conv_w_grad.reshape(conv_taps, head_count, block_size)
    grad_conv_b = conv_b_grad.reshape(head_count, block_size)
    summed = (
        lax.psum_scatter(gain_one_sum, "dp", scatter_dimension=0, tiled=True),
        lax.psum_scatter(grad_w_branch, "dp", scatter_dimension=0, tiled=True),
        lax.psum_scatter(grad_w_input, "dp", scatter_dimension=0, tiled=True),
        lax.psum_scatter(grad_w_rgate, "dp", scatter_dimension=1, tiled=True),
        lax.psum_scatter(grad_w_igate, "dp", scatter_dimension=1, tiled=True),
        lax.psum_scatter(grad_rbias, "dp", scatter_dimension=1, tiled=True),
        lax.psum_scatter(grad_ibias, "dp", scatter_dimension=1, tiled=True),
        lax.psum_scatter(grad_decay, "dp", scatter_dimension=1, tiled=True),
        lax.psum_scatter(grad_conv_w, "dp", scatter_dimension=2, tiled=True),
        lax.psum_scatter(grad_conv_b, "dp", scatter_dimension=1, tiled=True),
        lax.psum_scatter(grad_w_output, "dp", scatter_dimension=1, tiled=True),
        lax.psum_scatter(gain_two_sum, "dp", scatter_dimension=0, tiled=True),
        lax.psum_scatter(grad_w_gate, "dp", scatter_dimension=0, tiled=True),
        lax.psum_scatter(grad_w_up, "dp", scatter_dimension=0, tiled=True),
        lax.psum_scatter(grad_w_down, "dp", scatter_dimension=1, tiled=True),
    )
    return (
        result,
        token_input_gradient,
        summed[0],
        summed[1],
        summed[2],
        summed[3],
        summed[4],
        summed[5],
        summed[6],
        summed[7],
        summed[8],
        summed[9],
        summed[10],
        summed[11],
        summed[12],
        summed[13],
        summed[14],
    )


def solution(mesh):
    return jax.shard_map(
        local,
        mesh=mesh,
        in_specs=(
            P("dp", "tensor", None),
            P("dp", None),
            P("dp"),
            P("dp", "tensor"),
            P("dp", "tensor"),
            P("tensor", "dp", None),
            P("tensor", "dp", None),
            P("tensor", "dp"),
            P("tensor", "dp"),
            P("tensor", "dp"),
            P(None, "tensor", "dp"),
            P("tensor", "dp"),
            P("tensor", "dp"),
            P("dp"),
            P("dp", "tensor"),
            P("dp", "tensor"),
            P("tensor", "dp"),
            P("dp", "tensor", None),
        ),
        out_specs=(
            P("dp", "tensor", None),
            P("dp", "tensor", None),
            P("dp"),
            P("dp", "tensor"),
            P("dp", "tensor"),
            P("tensor", "dp", None),
            P("tensor", "dp", None),
            P("tensor", "dp"),
            P("tensor", "dp"),
            P("tensor", "dp"),
            P(None, "tensor", "dp"),
            P("tensor", "dp"),
            P("tensor", "dp"),
            P("dp"),
            P("dp", "tensor"),
            P("dp", "tensor"),
            P("tensor", "dp"),
        ),
        check_vma=False,
    )
```

profile of v0, /device:TPU:0, one launch (start us, length us, event | category | flops | bytes accessed | tf_op | source)
XLA Modules:
  0.0 3565.5 jit_solution(3201103686632250252)
XLA Ops:
  8.5 42.4 %all-gather = bf16[16,1,128]{2,1,0:T(2,128)(2,1)S(1)} all-gather(bf16[1,1,128]{2,1,0:T(2,128)(2,1)} %bitcast.215), channel_id=1, replica_groups=mesh['dp'=16,'tensor'=2] {'dp'}, dimensions={0}, use_global_device_ids=true | all-gather | bytes 4352 | tf_op jit(solution)/shard_map/all_gather | solution.py:101
  55.8 35.8 %all-gather.2 = bf16[16,16,5]{1,2,0:T(8,128)(2,1)S(1)} all-gather(bf16[1,16,5]{1,2,0:T(8,128)(2,1)S(1)} %bitcast.210), channel_id=1, replica_groups=mesh['dp'=16,'tensor'=2] {'dp'}, dimensions={0}, use_global_device_ids=true | all-gather | bytes 2720 | tf_op jit(solution)/shard_map/all_gather | solution.py:106
  91.7 38.4 %all-gather.4 = bf16[16,16,5]{1,2,0:T(8,128)(2,1)S(1)} all-gather(bf16[1,16,5]{1,2,0:T(8,128)(2,1)S(1)} %bitcast.211), channel_id=1, replica_groups=mesh['dp'=16,'tensor'=2] {'dp'}, dimensions={0}, use_global_device_ids=true | all-gather | bytes 2720 | tf_op jit(solution)/shard_map/all_gather | solution.py:107
  130.2 35.8 %all-gather.3 = bf16[16,16,5]{1,2,0:T(8,128)(2,1)S(1)} all-gather(bf16[1,16,5]{1,2,0:T(8,128)(2,1)S(1)} %bitcast.212), channel_id=1, replica_groups=mesh['dp'=16,'tensor'=2] {'dp'}, dimensions={0}, use_global_device_ids=true | all-gather | bytes 2720 | tf_op jit(solution)/shard_map/all_gather | solution.py:108
  167.3 38.2 %all-gather.1 = bf16[16,16,5]{1,2,0:T(8,128)(2,1)S(1)} all-gather(bf16[1,16,5]{1,2,0:T(8,128)(2,1)S(1)} %bitcast.213), channel_id=1, replica_groups=mesh['dp'=16,'tensor'=2] {'dp'}, dimensions={0}, use_global_device_ids=true | all-gather | bytes 2720 | tf_op jit(solution)/shard_map/all_gather | solution.py:110
  205.6 39.2 %all_gather.60 = bf16[4,5,256]{1,0,2:T(4,128)(2,1)S(1)} all-gather(bf16[4,5,16]{1,0,2:T(4,128)(2,1)S(1)} %copy.104), channel_id=1, replica_groups=mesh['dp'=16,'tensor'=2] {'dp'}, dimensions={2}, use_global_device_ids=true | all-gather | bytes 10880 | tf_op jit(solution)/shard_map/all_gather | solution.py:109
  245.5 46.0 %all_gather.62 = bf16[5,256,256]{2,1,0:T(8,128)(2,1)S(1)} all-gather(bf16[5,16,256]{2,1,0:T(8,128)(2,1)S(1)} %copy-done.59), channel_id=1, replica_groups=mesh['dp'=16,'tensor'=2] {'dp'}, dimensions={1}, use_global_device_ids=true | all-gather | bytes 696320 | tf_op jit(solution)/shard_map/all_gather | solution.py:104
  291.5 46.8 %all_gather.65 = bf16[5,256,256]{2,1,0:T(8,128)(2,1)} all-gather(bf16[5,16,256]{2,1,0:T(8,128)(2,1)S(1)} %copy-done.60), channel_id=1, replica_groups=mesh['dp'=16,'tensor'=2] {'dp'}, dimensions={1}, use_global_device_ids=true | all-gather | bytes 696320 | tf_op jit(solution)/shard_map/all_gather | solution.py:105
  447.8 37.2 %all-gather.5 = bf16[16,1,128]{2,1,0:T(2,128)(2,1)S(1)} all-gather(bf16[1,1,128]{2,1,0:T(2,128)(2,1)S(1)} %bitcast.216), channel_id=1, replica_groups=mesh['dp'=16,'tensor'=2] {'dp'}, dimensions={0}, use_global_device_ids=true | all-gather | bytes 4352 | tf_op jit(solution)/shard_map/all_gather | solution.py:114
  493.5 155.6 %all-gather.29.cloned.1.call-done = bf16[2048,3072]{1,0:T(8,128)(2,1)} async-done(((bf16[128,3072]{1,0:T(8,128)(2,1)}), bf16[2048,3072]{1,0:T(8,128)(2,1)}) %all-gather.29.cloned.1.call-update) | async-done | bytes 12582928 | tf_op jit(solution)/shard_map/all_gather | solution.py:116
  649.1 10.0 fusion.64
  659.1 143.4 %all-gather.27.cloned.1.call-done = bf16[2048,3072]{1,0:T(8,128)(2,1)} async-done(((bf16[128,3072]{1,0:T(8,128)(2,1)}), bf16[2048,3072]{1,0:T(8,128)(2,1)}) %all-gather.27.cloned.1.call-update) | async-done | bytes 12582928 | tf_op jit(solution)/shard_map/all_gather | solution.py:115
  802.5 9.9 fusion.66
  812.4 199.6 %all-gather.31.cloned.1.call-done = bf16[3072,2048]{1,0:T(8,128)(2,1)} async-done(((bf16[3072,128]{1,0:T(8,128)(2,1)}), bf16[3072,2048]{1,0:T(8,128)(2,1)}) %all-gather.31.cloned.1.call-update) | async-done | bytes 12582928 | tf_op jit(solution)/shard_map/all_gather | solution.py:117
  1012.0 11.5 multiply_convert_fusion
  1205.8 10.8 rev.2
  1300.4 10.3 fusion.60
  1312.1 10.2 fusion.62
  1324.0 10.3 fusion.56
  1337.5 37.4 %reduce-scatter.52.cloned.1.call-done = f32[16,5]{1,0:T(8,128)} async-done(((f32[256,5]{1,0:T(8,128)}), f32[16,5]{1,0:T(8,128)}) %reduce-scatter.52.cloned.1.call-update) | async-done | bytes 336
  1376.3 72.9 %reduce-scatter.54.cloned.1.call-done = f32[16,5]{1,0:T(8,128)} async-done(((f32[256,5]{1,0:T(8,128)}), f32[16,5]{1,0:T(8,128)}) %reduce-scatter.54.cloned.1.call-update) | async-done | bytes 336
  1450.6 73.0 %reduce-scatter.60.cloned.1.call-done = f32[16,5]{1,0:T(8,128)} async-done(((f32[256,5]{1,0:T(8,128)}), f32[16,5]{1,0:T(8,128)}) %reduce-scatter.60.cloned.1.call-update) | async-done | bytes 336
  1524.9 72.9 %reduce-scatter.58.cloned.1.call-done = f32[16,20]{1,0:T(8,128)} async-done(((f32[256,20]{1,0:T(8,128)}), f32[16,20]{1,0:T(8,128)}) %reduce-scatter.58.cloned.1.call-update) | async-done | bytes 1296
  1607.0 77.1 %all-reduce.49 = (f32[2048]{0:T(1024)S(1)}, f32[2048]{0:T(1024)S(1)}) all-reduce(f32[2048]{0:T(1024)S(1)} %get-tuple-element.26, f32[2048]{0:T(1024)S(1)} %copy-done.61), channel_id=6, replica_groups=mesh['dp'=16,'tensor'=2] {'dp'}, use_global_device_ids=true, to_apply=%region_12.13.clone | all-reduce | flops 4096 | bytes 32768
  1690.5 9.6 reduce-scatter.40.cloned.1.call-done
  1700.0 78.0 %reduce-scatter.42.cloned.1.call-done = f32[5,16,256]{2,1,0:T(8,128)} async-done(((f32[5,256,256]{2,1,0:T(8,128)}), f32[5,16,256]{2,1,0:T(8,128)}) %reduce-scatter.42.cloned.1.call-update) | async-done | bytes 81936 | tf_op jit(solution)/shard_map/reduce_scatter | solution.py:255
  1778.1 219.1 %reduce-scatter.44.cloned.1.call-done = f32[1280,128]{1,0:T(8,128)} async-done(((f32[1280,2048]{1,0:T(8,128)}), f32[1280,128]{1,0:T(8,128)}) %reduce-scatter.44.cloned.1.call-update) | async-done | bytes 655376 | tf_op jit(solution)/shard_map/reduce_scatter | solution.py:261
  1997.2 226.4 %reduce-scatter.38.cloned.1.call-done = f32[128,1280]{1,0:T(8,128)} async-done(((f32[2048,1280]{1,0:T(8,128)}), f32[128,1280]{1,0:T(8,128)}) %reduce-scatter.38.cloned.1.call-update) | async-done | bytes 655376 | tf_op jit(solution)/shard_map/reduce_scatter | solution.py:253
  2223.6 226.3 %reduce-scatter.36.cloned.1.call-done = f32[128,1280]{1,0:T(8,128)} async-done(((f32[2048,1280]{1,0:T(8,128)}), f32[128,1280]{1,0:T(8,128)}) %reduce-scatter.36.cloned.1.call-update) | async-done | bytes 655376 | tf_op jit(solution)/shard_map/reduce_scatter | solution.py:252
  2449.8 372.5 %reduce-scatter.48.cloned.1.call-done = f32[128,3072]{1,0:T(8,128)} async-done(((f32[2048,3072]{1,0:T(8,128)}), f32[128,3072]{1,0:T(8,128)}) %reduce-scatter.48.cloned.1.call-update) | async-done | bytes 1572880 | tf_op jit(solution)/shard_map/reduce_scatter | solution.py:264
  2822.3 367.7 %reduce-scatter.46.cloned.1.call-done = f32[128,3072]{1,0:T(8,128)} async-done(((f32[2048,3072]{1,0:T(8,128)}), f32[128,3072]{1,0:T(8,128)}) %reduce-scatter.46.cloned.1.call-update) | async-done | bytes 1572880 | tf_op jit(solution)/shard_map/reduce_scatter | solution.py:263
  3190.1 368.1 %reduce-scatter.50.cloned.1.call-done = f32[3072,128]{1,0:T(8,128)} async-done(((f32[3072,2048]{1,0:T(8,128)}), f32[3072,128]{1,0:T(8,128)}) %reduce-scatter.50.cloned.1.call-update) | async-done | bytes 1572880 | tf_op jit(solution)/shard_map/reduce_scatter | solution.py:265
  (551 shorter events, 416.1 us)
Async XLA Ops:
  7.2 331.2 %all-gather.17.cloned.1.call-start = ((), (), s32[]{:S(2)}) async-start(), calls=%async_computation.17 | async-start | bytes 1572864 | tf_op jit(solution)/shard_map/all_gather | solution.py:133
  53.0 285.4 %all-gather.19.cloned.1.call-start = ((), (), s32[]{:S(2)}) async-start(), calls=%async_computation.18 | async-start | bytes 5570560 | tf_op jit(solution)/shard_map/all_gather | solution.py:103
  53.7 381.9 %all-gather.21.cloned.1.call-start = ((), (), s32[]{:S(2)}) async-start(), calls=%async_computation.19 | async-start | bytes 5570560 | tf_op jit(solution)/shard_map/all_gather | solution.py:102
  54.4 388.1 %all-gather.23.cloned.1.call-start = ((), (), s32[]{:S(2)}) async-start(), calls=%async_computation.20 | async-start | bytes 5570560 | tf_op jit(solution)/shard_map/all_gather | solution.py:111
  55.0 430.0 %reduce-scatter.28.cloned.1.call-start = ((), (), s32[]{:S(2)}) async-start(), calls=%async_computation.21 | async-start | bytes 1572864 | tf_op jit(solution)/shard_map/reduce_scatter | solution.py:168
  447.8 45.7 %all-gather.25.cloned.1.call-start = ((), (), s32[]{:S(2)}) async-start(), calls=%async_computation.22 | async-start | bytes 1572864 | tf_op jit(solution)/shard_map/all_gather | solution.py:173
  485.0 564.4 %copy-start.37 = (f32[16,1,128]{2,1,0:T(1,128)}, f32[16,1,128]{2,1,0:T(1,128)S(1)}, u32[]{:S(2)}) copy-start(f32[16,1,128]{2,1,0:T(1,128)S(1)} %convert_element_type.157) | copy-start | bytes 24580
  486.5 563.0 %copy-start.70 = (f32[128]{0:T(128)}, f32[128]{0:T(128)S(1)}, u32[]{:S(2)}) copy-start(f32[128]{0:T(128)S(1)} %add_rsqrt_fusion) | copy-start | bytes 1540
  487.5 161.6 %all-gather.29.cloned.1.call-start = ((), (), s32[]{:S(2)}) async-start(), calls=%async_computation.24 | async-start | bytes 13369344 | tf_op jit(solution)/shard_map/all_gather | solution.py:116
  488.3 314.2 %all-gather.27.cloned.1.call-start = ((), (), s32[]{:S(2)}) async-start(), calls=%async_computation.23 | async-start | bytes 13369344 | tf_op jit(solution)/shard_map/all_gather | solution.py:115
  489.0 323.4 %all-gather.33.cloned.1.call-start = ((), (), s32[]{:S(2)}) async-start(), calls=%async_computation.27 | async-start | bytes 1572864 | tf_op jit(solution)/shard_map/all_gather | solution.py:188
  490.3 559.2 %copy-start.83 = (pred[128]{0:T(512)(128)(4,1)}, pred[128]{0:T(512)(128)(4,1)S(1)}, u32[]{:S(2)}) copy-start(pred[128]{0:T(512)(128)(4,1)S(1)} %compare_bitcast_fusion) | copy-start | bytes 388
  492.5 519.5 %all-gather.31.cloned.1.call-start = ((), (), s32[]{:S(2)}) async-start(), calls=%async_computation.25 | async-start | bytes 13369344 | tf_op jit(solution)/shard_map/all_gather | solution.py:117
  493.1 553.9 %reduce-scatter.32.cloned.1.call-start = ((), (), s32[]{:S(2)}) async-start(), calls=%async_computation.28 | async-start | bytes 1572864 | tf_op jit(solution)/shard_map/reduce_scatter | solution.py:200
  1040.2 48.4 %all-gather.35.cloned.1.call-start = ((), (), s32[]{:S(2)}) async-start(), calls=%async_computation.29 | async-start | bytes 1572864 | tf_op jit(solution)/shard_map/all_gather | solution.py:207
  1052.2 283.9 %reduce-scatter.56.cloned.1.call-start = ((), (), s32[]{:S(2)}) async-start(), calls=%async_computation.41 | async-start | bytes 139264
  1222.9 152.0 %reduce-scatter.52.cloned.1.call-start = ((), (), s32[]{:S(2)}) async-start(), calls=%async_computation.39 | async-start | bytes 139264
  1239.6 209.7 %reduce-scatter.54.cloned.1.call-start = ((), (), s32[]{:S(2)}) async-start(), calls=%async_computation.40 | async-start | bytes 139264
  1246.1 277.5 %reduce-scatter.60.cloned.1.call-start = ((), (), s32[]{:S(2)}) async-start(), calls=%async_computation.43 | async-start | bytes 139264
  1250.9 346.9 %reduce-scatter.58.cloned.1.call-start = ((), (), s32[]{:S(2)}) async-start(), calls=%async_computation.42 | async-start | bytes 139264
  1254.4 351.1 %reduce-scatter.34.cloned.1.call-start = ((), (), s32[]{:S(2)}) async-start(), calls=%async_computation.30 | async-start | bytes 1572864 | tf_op jit(solution)/shard_map/reduce_scatter | solution.py:237
  1263.8 423.4 %reduce-scatter.30.cloned.1.call-start = ((), (), s32[]{:S(2)}) async-start(), calls=%async_computation.26 | async-start | bytes 1572864 | tf_op jit(solution)/shard_map/reduce_scatter | solution.py:183
  1273.5 426.6 %reduce-scatter.40.cloned.1.call-start = ((), (), s32[]{:S(2)}) async-start(), calls=%async_computation.33 | async-start | bytes 1392640 | tf_op jit(solution)/shard_map/reduce_scatter | solution.py:254
  1276.0 502.1 %reduce-scatter.42.cloned.1.call-start = ((), (), s32[]{:S(2)}) async-start(), calls=%async_computation.34 | async-start | bytes 1392640 | tf_op jit(solution)/shard_map/reduce_scatter | solution.py:255
  1278.6 718.6 %reduce-scatter.44.cloned.1.call-start = ((), (), s32[]{:S(2)}) async-start(), calls=%async_computation.35 | async-start | bytes 11141120 | tf_op jit(solution)/shard_map/reduce_scatter | solution.py:261
  1285.2 938.4 %reduce-scatter.38.cloned.1.call-start = ((), (), s32[]{:S(2)}) async-start(), calls=%async_computation.32 | async-start | bytes 11141120 | tf_op jit(solution)/shard_map/reduce_scatter | solution.py:253
  1292.0 1157.8 %reduce-scatter.36.cloned.1.call-start = ((), (), s32[]{:S(2)}) async-start(), calls=%async_computation.31 | async-start | bytes 11141120 | tf_op jit(solution)/shard_map/reduce_scatter | solution.py:252
  1298.7 1523.6 %reduce-scatter.48.cloned.1.call-start = ((), (), s32[]{:S(2)}) async-start(), calls=%async_computation.37 | async-start | bytes 26738688 | tf_op jit(solution)/shard_map/reduce_scatter | solution.py:264
  1310.7 1879.4 %reduce-scatter.46.cloned.1.call-start = ((), (), s32[]{:S(2)}) async-start(), calls=%async_computation.36 | async-start | bytes 26738688 | tf_op jit(solution)/shard_map/reduce_scatter | solution.py:263
  1322.3 2235.9 %reduce-scatter.50.cloned.1.call-start = ((), (), s32[]{:S(2)}) async-start(), calls=%async_computation.38 | async-start | bytes 26738688 | tf_op jit(solution)/shard_map/reduce_scatter | solution.py:265
  1334.3 352.9 %copy-start.10 = (f32[1,128,2048]{2,1,0:T(8,128)S(1)}, f32[1,128,2048]{2,1,0:T(8,128)}, u32[]{:S(2)}) copy-start(f32[1,128,2048]{2,1,0:T(8,128)} %param.35) | copy-start | bytes 3145732
  1334.3 352.9 %copy-start.6 = (bf16[1,128,2048]{2,1,0:T(8,128)(2,1)S(1)}, bf16[1,128,2048]{2,1,0:T(8,128)(2,1)}, u32[]{:S(2)}) copy-start(bf16[1,128,2048]{2,1,0:T(8,128)(2,1)} %reduce-scatter.28.cloned.1.call-done) | copy-start | bytes 1572868
  (93 other events, 5739.8 us)
Sparse Core Ops, SparseCore 0:
  53.1 4.8 all-gather.16
  60.8 86.9 all-gather.18
  150.5 91.5 all-gather.20
  244.6 108.4 all-gather.22
  447.9 6.0 reduce-scatter.27
  487.6 5.0 all-gather.24
  495.9 153.1 all-gather.28
  652.2 150.1 all-gather.26
  804.7 7.2 all-gather.32
  814.8 197.1 all-gather.30
  1040.3 6.7 reduce-scatter.31
  1052.4 10.1 all-gather.34
  1223.0 76.9 reduce-scatter.55
  1302.8 72.1 reduce-scatter.51
  1377.0 72.1 reduce-scatter.53
  1451.4 72.1 reduce-scatter.59
  1525.7 72.1 reduce-scatter.57
  1600.6 4.8 reduce-scatter.33
  1607.8 9.6 reduce-scatter.29
  1620.3 79.7 reduce-scatter.39
  1703.0 75.0 reduce-scatter.41
  1781.1 216.0 reduce-scatter.43
  2000.2 223.3 reduce-scatter.37
  2226.4 223.3 reduce-scatter.35
  2457.1 365.1 reduce-scatter.47
  2829.5 360.5 reduce-scatter.45
  3197.2 360.9 reduce-scatter.49
where the time goes:
time: 3580 us; the launch traced here: 3570 us
  waiting for transfers between devices  2640 us (74%)
  blocking collectives  440 us (12%)
  local copies, waits for them, and re-layouts  234 us (7%)
  matrix products  147 us (4%)
  other arithmetic  86.6 us (2%)
    reduce_scatter x1, waiting for transfers between devices, local(): lax.psum_scatter(grad_w_up, 'dp', scatter_dimension=0, tiled=True)  372 us
    reduce_scatter x1, waiting for transfers between devices, local(): lax.psum_scatter(grad_w_down, 'dp', scatter_dimension=1, tiled=True)  368 us
    reduce_scatter x1, waiting for transfers between devices, local(): lax.psum_scatter(grad_w_gate, 'dp', scatter_dimension=0, tiled=True)  368 us
    unnamed x32, waiting for transfers between devices  260 us
    reduce_scatter x1, waiting for transfers between devices, local(): lax.psum_scatter(grad_w_input, 'dp', scatter_dimension=0, tiled=True)  226 us
    reduce_scatter x1, waiting for transfers between devices, local(): lax.psum_scatter(grad_w_branch, 'dp', scatter_dimension=0, tiled=True)  226 us
    reduce_scatter x1, waiting for transfers between devices, local(): lax.psum_scatter(grad_w_output, 'dp', scatter_dimension=1, tiled=True)  219 us
    all_gather x1, waiting for transfers between devices, local(): lax.all_gather(w_down, 'dp', axis=1, tiled=True)  200 us
  transfers between devices with their start and end apart: 27, of which 17 were waited for; matrix products, arithmetic and copies ran while one was open for 8% of the time, Pallas kernels for 0%

commit v1 on v0

v1 whole, which is shorter than its diff:
```python
import functools

import jax
import jax.numpy as jnp
from jax import lax
from jax.experimental import pallas as pl
from jax.experimental.pallas import tpu as pltpu
from jax.sharding import PartitionSpec as P

MESH = pl.DeviceIdType.MESH
BF = jnp.bfloat16
F32 = jnp.float32
EPS = 1e-06
DECAY = 8.0
GC = 0.7978845608028654
GK = 0.044715
VMEM_LIMIT = 60 * 1024 * 1024


def dp_at(zh, zl, y, x):
    return ((zh * 2 + zl) * 2 + y) * 2 + x


def place():
    dp = lax.axis_index("dp")
    return dp // 8, (dp // 4) % 2, (dp // 2) % 2, dp % 2, lax.axis_index("tensor")


def dev(dp, core):
    return {"dp": dp, "tensor": core}


def greet(devices):
    sem = pltpu.get_barrier_semaphore()
    for d in devices:
        pl.semaphore_signal(sem, inc=1, device_id=d, device_id_type=MESH)
    pl.semaphore_wait(sem, len(devices))


def remote(src, dst, ssem, rsem, d):
    return pltpu.make_async_remote_copy(
        src_ref=src, dst_ref=dst, send_sem=ssem, recv_sem=rsem, device_id=d, device_id_type=MESH
    )


def peers_of_group(zh, zl, y, x):
    out = []
    for kl, kx in ((0, 1), (1, 0), (1, 1)):
        pz, px = (zl + kl) % 2, (x + kx) % 2
        out.append((pz * 2 + px, dp_at(zh, pz, y, px)))
    return out


def act_gather_kernel(x_ref, out_ref, send, recv, fsend, frecv, local):
    zh, zl, y, x, c = place()
    q, me = zl * 2 + x, dp_at(zh, zl, y, x)
    sib = dev(me, 1 - c)
    peers = peers_of_group(zh, zl, y, x)
    greet([sib] + [dev(d, c) for _, d in peers])
    own = pltpu.make_async_copy(x_ref, out_ref.at[q, c], local)
    own.start()
    copies = []
    for k, (pq, d) in enumerate(peers):
        cp = remote(x_ref, out_ref.at[q, c], send.at[k], recv.at[q], dev(d, c))
        cp.start()
        copies.append(cp)
    fwd = [remote(x_ref, out_ref.at[q, c], fsend.at[3], frecv.at[q], sib)]
    fwd[0].start()
    for k, (pq, d) in enumerate(peers):
        land = out_ref.at[pq, c]
        remote(land, land, send.at[k], recv.at[pq], dev(d, c)).wait_recv()
        cp = remote(land, land, fsend.at[k], frecv.at[pq], sib)
        cp.start()
        fwd.append(cp)
    for j in range(4):
        land = out_ref.at[j, 1 - c]
        remote(land, land, fsend.at[0], frecv.at[j], sib).wait_recv()
    for cp in copies + fwd:
        cp.wait_send()
    own.wait()


def act_gather(x, cid):
    half, width = x.shape
    return pl.pallas_call(
        act_gather_kernel,
        out_shape=jax.ShapeDtypeStruct((4, 2, half, width), x.dtype),
        in_specs=[pl.BlockSpec(memory_space=pl.ANY)],
        out_specs=pl.BlockSpec(memory_space=pl.ANY),
        scratch_shapes=[
            pltpu.SemaphoreType.DMA((3,)),
            pltpu.SemaphoreType.DMA((4,)),
            pltpu.SemaphoreType.DMA((4,)),
            pltpu.SemaphoreType.DMA((4,)),
            pltpu.SemaphoreType.DMA,
        ],
        compiler_params=pltpu.CompilerParams(collective_id=cid, has_side_effects=True),
        name="act_gather",
    )(x)


def act_reduce_kernel(p_ref, out_ref, sbuf, tbuf, rbuf, ssend, srecv, send, recv):
    zh, zl, y, x, c = place()
    q, me = zl * 2 + x, dp_at(zh, zl, y, x)
    sib = dev(me, 1 - c)
    peers = peers_of_group(zh, zl, y, x)
    greet([sib] + [dev(d, c) for _, d in peers])
    order = [peers[2], peers[1], peers[0], (q, me)]
    half = []
    for k, (pq, d) in enumerate(order):
        cp = remote(p_ref.at[pq, 1 - c], sbuf.at[pq], ssend.at[k], srecv.at[pq], sib)
        cp.start()
        half.append(cp)
    out = []
    for k, (pq, d) in enumerate(order):
        remote(sbuf.at[pq], sbuf.at[pq], ssend.at[k], srecv.at[pq], sib).wait_recv()
        total = p_ref[pq, c].astype(F32) + sbuf[pq].astype(F32)
        if k < 3:
            tbuf[k] = total.astype(BF)
            cp = remote(tbuf.at[k], rbuf.at[q], send.at[k], recv.at[q], dev(d, c))
            cp.start()
            out.append(cp)
        else:
            out_ref[...] = total
    for pq, d in peers:
        remote(rbuf.at[pq], rbuf.at[pq], send.at[0], recv.at[pq], dev(d, c)).wait_recv()
        out_ref[...] += rbuf[pq].astype(F32)
    for cp in half + out:
        cp.wait_send()


def act_reduce(parts, cid):
    _, _, half, width = parts.shape
    vm = pl.BlockSpec(memory_space=pltpu.VMEM)
    return pl.pallas_call(
        act_reduce_kernel,
        out_shape=jax.ShapeDtypeStruct((half, width), F32),
        in_specs=[vm],
        out_specs=vm,
        scratch_shapes=[
            pltpu.VMEM((4, half, width), BF),
            pltpu.VMEM((3, half, width), BF),
            pltpu.VMEM((4, half, width), BF),
            pltpu.SemaphoreType.DMA((4,)),
            pltpu.SemaphoreType.DMA((4,)),
            pltpu.SemaphoreType.DMA((3,)),
            pltpu.SemaphoreType.DMA((4,)),
        ],
        compiler_params=pltpu.CompilerParams(
            collective_id=cid, has_side_effects=True, vmem_limit_bytes=VMEM_LIMIT
        ),
        name="act_reduce",
    )(parts)


def plane(zh, zl, y, x, high):
    out = []
    for kh in range(high):
        for kl in range(2):
            for kx in range(2):
                ph, pz, px = (zh + kh) % high, (zl + kl) % 2, (x + kx) % 2
                out.append((ph, pz, px))
    return out


def weight_gather_kernel(high, narr, picked, *refs):
    src, dst = refs[:narr], refs[narr : 2 * narr]
    send, recv, fsend, local = refs[2 * narr :]
    zh, zl, y, x, c = place()
    me = dp_at(zh, zl, y, x)
    there = plane(zh, zl, y, x, high)
    other = dev(dp_at(zh, zl, 1 - y, x), c)
    greet([dev(dp_at(h, z, y, w), c) for h, z, w in there[1:]] + [other])
    pend = []
    for a in range(narr):
        for k, (h, z, w) in enumerate(there):
            piece = src[a].at[z * 2 + w] if picked[a] else src[a]
            if k == 0:
                cp = pltpu.make_async_copy(piece, dst[a].at[me], local.at[a])
            else:
                cp = remote(piece, dst[a].at[me], send.at[a, k], recv.at[a, me], dev(dp_at(h, z, y, w), c))
            cp.start()
            pend.append((k, cp))
    for a in range(narr):
        for k, (h, z, w) in enumerate(there):
            s = dp_at(h, z, y, w)
            land = dst[a].at[s]
            if k == 0:
                pend[a * len(there)][1].wait()
            else:
                remote(land, land, send.at[a, k], recv.at[a, s], other).wait_recv()
            cp = remote(land, land, fsend.at[a, k], recv.at[a, s], other)
            cp.start()
            pend.append((1, cp))
    for a in range(narr):
        for k, (h, z, w) in enumerate(there):
            s = dp_at(h, z, 1 - y, w)
            land = dst[a].at[s]
            remote(land, land, fsend.at[a, k], recv.at[a, s], other).wait_recv()
    for k, cp in pend:
        if k:
            cp.wait_send()


def weight_gather(arrays, picked, n, cid):
    high = n // 8
    narr = len(arrays)
    shapes = tuple(
        jax.ShapeDtypeStruct((n,) + (a.shape[1:] if p else a.shape), a.dtype) for a, p in zip(arrays, picked)
    )
    anyspec = pl.BlockSpec(memory_space=pl.ANY)
    return pl.pallas_call(
        functools.partial(weight_gather_kernel, high, narr, picked),
        out_shape=shapes,
        in_specs=[anyspec] * narr,
        out_specs=[anyspec] * narr,
        scratch_shapes=[
            pltpu.SemaphoreType.DMA((narr, high * 4)),
            pltpu.SemaphoreType.DMA((narr, n)),
            pltpu.SemaphoreType.DMA((narr, high * 4)),
            pltpu.SemaphoreType.DMA((narr,)),
        ],
        compiler_params=pltpu.CompilerParams(collective_id=cid, has_side_effects=True),
        name="weight_gather",
    )(*arrays)


def grad_reduce_kernel(high, narr, picked, *refs):
    src, dst = refs[:narr], refs[narr : 2 * narr]
    ybuf, tbuf, rbuf = (refs[(2 + i) * narr : (3 + i) * narr] for i in range(3))
    ysend, yrecv, send, recv = refs[5 * narr :]
    zh, zl, y, x, c = place()
    q = zl * 2 + x
    there = plane(zh, zl, y, x, high)
    other = dev(dp_at(zh, zl, 1 - y, x), c)
    greet([dev(dp_at(h, z, y, w), c) for h, z, w in there[1:]] + [other])
    mine = zh * 4 + q
    order = there[1:] + there[:1]
    pend = []
    for a in range(narr):
        for h, z, w in order:
            j = h * 4 + z * 2 + w
            cp = remote(src[a].at[dp_at(h, z, 1 - y, w)], ybuf[a].at[j], ysend.at[a, j], yrecv.at[a, j], other)
            cp.start()
            pend.append(cp)
    for a in range(narr):
        for k, (h, z, w) in enumerate(order):
            j = h * 4 + z * 2 + w
            remote(ybuf[a].at[j], ybuf[a].at[j], ysend.at[a, j], yrecv.at[a, j], other).wait_recv()
            total = src[a][dp_at(h, z, y, w)].astype(F32) + ybuf[a][j].astype(F32)
            if k < len(order) - 1:
                tbuf[a][j] = total.astype(tbuf[a].dtype)
                cp = remote(
                    tbuf[a].at[j], rbuf[a].at[mine], send.at[a, j], recv.at[a, mine], dev(dp_at(h, z, y, w), c)
                )
                cp.start()
                pend.append(cp)
            elif picked[a]:
                dst[a][...] = jnp.zeros(dst[a].shape, F32)
                dst[a][q] = total
            else:
                dst[a][...] = total
    for a in range(narr):
        for h, z, w in there[1:]:
            j = h * 4 + z * 2 + w
            remote(rbuf[a].at[j], rbuf[a].at[j], send.at[a, j], recv.at[a, j], other).wait_recv()
            if picked[a]:
                dst[a][z * 2 + w] += rbuf[a][j].astype(F32)
            else:
                dst[a][...] += rbuf[a][j].astype(F32)
    for cp in pend:
        cp.wait_send()


def grad_reduce(arrays, picked, n, cid):
    high = n // 8
    narr = len(arrays)
    vm = pl.BlockSpec(memory_space=pltpu.VMEM)
    shapes = tuple(
        jax.ShapeDtypeStruct(((4,) if p else ()) + a.shape[1:], F32) for a, p in zip(arrays, picked)
    )
    bufs = [pltpu.VMEM((high * 4,) + a.shape[1:], a.dtype) for a in arrays]
    return pl.pallas_call(
        functools.partial(grad_reduce_kernel, high, narr, picked),
        out_shape=shapes,
        in_specs=[vm] * narr,
        out_specs=[vm] * narr,
        scratch_shapes=bufs * 3 + [pltpu.SemaphoreType.DMA((narr, high * 4))] * 4,
        compiler_params=pltpu.CompilerParams(
            collective_id=cid, has_side_effects=True, vmem_limit_bytes=VMEM_LIMIT
        ),
        name="grad_reduce",
    )(*arrays)


def gelu_parts(v):
    t = jnp.tanh(GC * (v + GK * v * v * v))
    act = 0.5 * v * (1.0 + t)
    der = 0.5 * (1.0 + t) + 0.5 * v * (1.0 - t * t) * GC * (1.0 + 3.0 * GK * v * v)
    return act, der


def segments(ends, length, width, taps):
    t = lax.broadcasted_iota(jnp.int32, (length, width), 0).astype(F32)

    def seg(at):
        total = jnp.zeros((length, width), F32)
        for j in range(4):
            total = total + jnp.where(at >= ends[:, j : j + 1], 1.0, 0.0)
        return total

    here = seg(t)
    same = []
    for k in range(1, taps):
        same.append(jnp.where((t >= float(k)) & (seg(t - float(k)) == here), 1.0, 0.0))
    return same


def scan8(a, b, reverse):
    length, width = a.shape
    row = lax.broadcasted_iota(jnp.int32, (length, width), 0) % 8
    for d in (1, 2, 4):
        if reverse:
            ash, bsh = pltpu.roll(a, length - d, 0), pltpu.roll(b, length - d, 0)
            ok = row < 8 - d
        else:
            ash, bsh = pltpu.roll(a, d, 0), pltpu.roll(b, d, 0)
            ok = row >= d
        b = b + a * jnp.where(ok, bsh, 0.0)
        a = a * jnp.where(ok, ash, 1.0)
    return a, b


def full_scan(a, b, out_ref, a_ref, reverse):
    length, width = a.shape
    a8, b8 = scan8(a, b, reverse)
    a_ref[...] = a8
    out_ref[...] = b8
    blocks = length // 8

    def step(i, carry):
        at = (blocks - 1 - i if reverse else i) * 8
        at = pl.multiple_of(at, 8)
        now = out_ref[pl.ds(at, 8), :] + a_ref[pl.ds(at, 8), :] * carry
        out_ref[pl.ds(at, 8), :] = now
        return now[0:1, :] if reverse else now[7:8, :]

    lax.fori_loop(0, blocks, step, jnp.zeros((1, width), F32))


def rec_forward_kernel(taps, p_ref, g_ref, v_ref, e_ref, mixed_ref, conv_ref, r_ref, i_ref, state_ref, a_ref):
    length, two = p_ref.shape[1:]
    blk = two // 2
    branch, conv_in = p_ref[0, :, :blk], p_ref[0, :, blk:]
    vec = v_ref[0]
    same = segments(e_ref[0, 0:1, :], length, blk, taps)
    conv = conv_in * vec[4:5] + vec[4 + taps : 5 + taps]
    for k in range(1, taps):
        conv = conv + pltpu.roll(conv_in, k, 0) * same[k - 1] * vec[4 + k : 5 + k]
    pre = jnp.dot(conv.astype(BF), g_ref[0], preferred_element_type=F32)
    r = jax.nn.sigmoid(pre[:, :blk] + vec[0:1])
    gate = jax.nn.sigmoid(pre[:, blk:] + vec[1:2])
    log_a = (-DECAY * r) * vec[2:3]
    a = jnp.exp(log_a)
    start = same[0] == 0.0
    a_eff = jnp.where(start, 0.0, a)
    mult = jnp.where(start, 1.0, jnp.sqrt(-jnp.tanh(log_a) * (1.0 + a * a)))
    full_scan(a_eff, mult * gate * conv, state_ref.at[0], a_ref, False)
    act, _ = gelu_parts(branch)
    mixed_ref[0] = (state_ref[0] * act).astype(BF)
    conv_ref[0] = conv
    r_ref[0] = r
    i_ref[0] = gate


def rec_backward_kernel(
    taps, p_ref, g_ref, v_ref, e_ref, conv_ref, r_ref, i_ref, state_ref, m_ref,
    low_ref, gg_ref, vg_ref, carry_ref, a_ref,
):
    unit = pl.program_id(0)
    length, two = p_ref.shape[1:]
    blk = two // 2
    branch, conv_in = p_ref[0, :, :blk], p_ref[0, :, blk:]
    vec = v_ref[0]
    same = segments(e_ref[0, 0:1, :], length, blk, taps)
    start = same[0] == 0.0
    r, gate, conv, state, mg = r_ref[0], i_ref[0], conv_ref[0], state_ref[0], m_ref[0]
    act, der = gelu_parts(branch)
    low_ref[0, :, :blk] = (mg * state * der).astype(BF)
    log_a = (-DECAY * r) * vec[2:3]
    a = jnp.exp(log_a)
    a_eff = jnp.where(start, 0.0, a)
    row = lax.broadcasted_iota(jnp.int32, (length, blk), 0)
    a_next = jnp.where(row < length - 1, pltpu.roll(a_eff, length - 1, 0), 0.0)
    full_scan(a_next, mg * act, carry_ref, a_ref, True)
    carry = carry_ref[...]
    prev = jnp.where(row > 0, pltpu.roll(state, 1, 0), 0.0)
    raw = jnp.sqrt(-jnp.tanh(log_a) * (1.0 + a * a))
    mult = jnp.where(start, 1.0, raw)
    log_grad = jnp.where(start, 0.0, carry * prev * a - carry * gate * conv * (a * a) / raw)
    r_grad = log_grad * (-DECAY * vec[2:3]) * (r * (1.0 - r))
    i_grad = carry * mult * conv * (gate * (1.0 - gate))
    pre_low = jnp.concatenate([r_grad.astype(BF), i_grad.astype(BF)], axis=1)
    conv_grad = carry * mult * gate + lax.dot_general(
        pre_low, g_ref[0], (((1,), (1,)), ((), ())), preferred_element_type=F32
    )
    gg = lax.dot_general(conv.astype(BF), pre_low, (((0,), (0,)), ((), ())), preferred_element_type=F32)

    def total(v):
        return jnp.sum(v, axis=0, keepdims=True)

    rows = [total(r_grad), total(i_grad), total(log_grad * (DECAY * r) * vec[3:4]), total(conv_grad)]
    inp = conv_grad * vec[4:5]
    rows.append(total(conv_grad * conv_in))
    for k in range(1, taps):
        masked = conv_grad * same[k - 1]
        rows.append(total(masked * pltpu.roll(conv_in, k, 0)))
        inp = inp + pltpu.roll(masked, length - k, 0) * vec[4 + k : 5 + k]
    low_ref[0, :, blk:] = inp.astype(BF)
    vg = jnp.concatenate(rows, axis=0)

    @pl.when((unit == 0) | (unit == 4))
    def _():
        gg_ref[0] = gg
        vg_ref[0] = vg

    @pl.when((unit != 0) & (unit != 4))
    def _():
        gg_ref[0] += gg
        vg_ref[0] += vg


def unit_spec(a):
    return pl.BlockSpec((1,) + a.shape[1:], lambda u: (u, 0, 0))


def head_spec(a):
    return pl.BlockSpec((1,) + a.shape[1:], lambda u: (u // 4, 0, 0))


def rec_forward(taps, pre, gates, vec, ends):
    units, length, two = pre.shape
    blk = two // 2
    block = pl.BlockSpec((1, length, blk), lambda u: (u, 0, 0))
    f32 = jax.ShapeDtypeStruct((units, length, blk), F32)
    return pl.pallas_call(
        functools.partial(rec_forward_kernel, taps),
        grid=(units,),
        out_shape=(jax.ShapeDtypeStruct((units, length, blk), BF), f32, f32, f32, f32),
        in_specs=[unit_spec(pre), head_spec(gates), head_spec(vec), unit_spec(ends)],
        out_specs=[block] * 5,
        scratch_shapes=[pltpu.VMEM((length, blk), F32)],
        compiler_params=pltpu.CompilerParams(vmem_limit_bytes=VMEM_LIMIT),
        name="rec_forward",
    )(pre, gates, vec, ends)


def rec_backward(taps, pre, gates, vec, ends, conv, r, gate, state, mixed_grad):
    units, length, two = pre.shape
    blk = two // 2
    vrows = 4 + taps
    return pl.pallas_call(
        functools.partial(rec_backward_kernel, taps),
        grid=(units,),
        out_shape=(
            jax.ShapeDtypeStruct((units, length, two), BF),
            jax.ShapeDtypeStruct((2, blk, two), F32),
            jax.ShapeDtypeStruct((2, vrows, blk), F32),
        ),
        in_specs=[unit_spec(pre), head_spec(gates), head_spec(vec), unit_spec(ends)]
        + [unit_spec(conv)] * 5,
        out_specs=[
            unit_spec(pre),
            pl.BlockSpec((1, blk, two), lambda u: (u // 4, 0, 0)),
            pl.BlockSpec((1, vrows, blk), lambda u: (u // 4, 0, 0)),
        ],
        scratch_shapes=[pltpu.VMEM((length, blk), F32)] * 2,
        compiler_params=pltpu.CompilerParams(vmem_limit_bytes=VMEM_LIMIT),
        name="rec_backward",
    )(pre, gates, vec, ends, conv, r, gate, state, mixed_grad)


def mm(a, b):
    return jnp.dot(a, b, preferred_element_type=F32)


def mm_t(a, b):
    return lax.dot_general(a, b, (((1,), (1,)), ((), ())), preferred_element_type=F32)


def t_mm(a, b):
    return lax.dot_general(a, b, (((0,), (0,)), ((), ())), preferred_element_type=F32)


def gelu_tanh(values):
    return jax.nn.gelu(values, approximate=True)


def norm_scale(values):
    return lax.rsqrt(jnp.mean(values * values, axis=-1, keepdims=True) + EPS)


def norm_back(grad, unit, inverse):
    return inverse * (grad - unit * jnp.mean(grad * unit, axis=-1, keepdims=True))


def local(
    tokens, doc_lengths, rec_gain, w_branch, w_input, w_rgate, w_igate, rgate_bias, igate_bias,
    decay_param, conv_weight, conv_bias, w_output, mlp_gain, w_gate, w_up, w_down, cotangent,
):
    n = lax.axis_size("dp")
    zh, zl, y, x, c = place()
    q = zl * 2 + x
    _, half, width = tokens.shape
    length = half * 2
    heads, rb, blk = w_rgate.shape
    taps = conv_weight.shape[0]
    rows = w_branch.shape[0]
    ff = w_gate.shape[1] // 4

    def by_head(w):
        return w.reshape(rows, heads, blk)

    rec_piece = jnp.concatenate([by_head(w_branch), by_head(w_input), by_head(w_output.T)], axis=2)
    rec_piece = rec_piece.transpose(1, 0, 2)

    def by_quarter(w):
        return w.reshape(rows, 4, ff)

    mlp_piece = jnp.concatenate([by_quarter(w_gate), by_quarter(w_up), by_quarter(w_down.T)], axis=2)
    mlp_piece = mlp_piece.transpose(1, 0, 2)
    gate_piece = jnp.concatenate([w_rgate, w_igate], axis=2)
    d32 = decay_param.astype(F32)
    vecs = jnp.stack(
        [rgate_bias.astype(F32), igate_bias.astype(F32), jax.nn.softplus(-d32), jax.nn.sigmoid(-d32)]
        + [conv_weight[k].astype(F32) for k in range(taps)]
        + [conv_bias.astype(F32)]
    )
    nv = vecs.shape[0]
    vecs = jnp.pad(vecs.reshape(nv, heads * rb), ((0, 0), (0, 128 - heads * rb)))
    lens = doc_lengths.reshape(4).astype(F32)
    e0 = lens[0]
    e1 = e0 + lens[1]
    e2 = e1 + lens[2]
    e3 = e2 + lens[3]
    ends_own = jnp.stack([e0, e1, e2, e3])

    def line(v):
        v = v.astype(F32).reshape(1, -1)
        return jnp.pad(v, ((0, 0), (0, 128 - v.shape[1])))

    smalls = jnp.concatenate([vecs, line(rec_gain), line(mlp_gain), line(ends_own)], axis=0)
    smalls = jnp.pad(smalls, ((0, 16 - smalls.shape[0]), (0, 0)))

    recq, rec4, gq, g4, small, mlp = weight_gather(
        (rec_piece[:4], rec_piece[4], gate_piece[:4], gate_piece[4], smalls, mlp_piece),
        (True, False, True, False, False, True), n, 1,
    )
    recq, rec4, mlp = recq.reshape(width, -1), rec4.reshape(width, -1), mlp.reshape(width, -1)
    gates = jnp.stack([gq.reshape(blk, 2 * blk), g4.reshape(blk, 2 * blk)])
    vec_all = small[:, :nv, : heads * rb].reshape(n, nv, heads, rb).transpose(2, 1, 0, 3).reshape(heads, nv, blk)
    vec = jnp.stack([lax.dynamic_index_in_dim(vec_all, q, 0, False), vec_all[4]])
    vec = jnp.pad(vec, ((0, 0), (0, 16 - nv), (0, 0)))
    gain1 = small[:, nv, :rows].reshape(1, width)
    gain2 = small[:, nv + 1, :rows].reshape(1, width)
    group_ends = small[:, nv + 2].reshape(n // 8, 2, 2, 2, 128)
    group_ends = lax.dynamic_index_in_dim(group_ends, zh, 0, False)
    group_ends = lax.dynamic_index_in_dim(group_ends, y, 1, False).reshape(4, 128)
    own_ends = lax.dynamic_index_in_dim(group_ends, q, 0, True)
    ends = jnp.concatenate([group_ends, own_ends], axis=0)[:, None, :]
    ends = jnp.broadcast_to(ends, (5, 8, 128))
    valid_own = ((lax.broadcasted_iota(jnp.int32, (half, 1), 0) + c * half).astype(F32)) < e3

    x_in = tokens[0].astype(F32)
    scale1 = norm_scale(x_in)
    unit1 = x_in * scale1
    u = act_gather((unit1 * gain1).astype(BF), 2)
    u_all = u.reshape(4 * length, width)
    u_own = lax.dynamic_index_in_dim(u, q, 0, False).reshape(length, width)
    pre = jnp.concatenate(
        [
            mm(u_all, recq[:, : 2 * blk]).reshape(4, length, 2 * blk),
            mm(u_own, rec4[:, : 2 * blk]).reshape(1, length, 2 * blk),
        ],
        axis=0,
    )
    mixed, conv, rate, gate, state = rec_forward(taps, pre, gates, vec, ends)
    mixed_a, mixed_b = mixed[:4].reshape(4 * length, blk), mixed[4]

    def with_own(a, b):
        a = a.reshape(4, length, -1)
        own = lax.dynamic_index_in_dim(a, q, 0, False) + b
        return lax.dynamic_update_index_in_dim(a, own, q, 0)

    def by_half(a):
        return a.astype(BF).reshape(4, 2, half, width)

    rec_part = with_own(mm_t(mixed_a, recq[:, 2 * blk :]), mm_t(mixed_b, rec4[:, 2 * blk :]))
    resid = x_in + act_reduce(by_half(rec_part), 3)
    scale2 = norm_scale(resid)
    unit2 = resid * scale2
    normed = act_gather((unit2 * gain2).astype(BF), 4).reshape(4 * length, width)
    w_g, w_u, w_d = mlp[:, :ff], mlp[:, ff : 2 * ff], mlp[:, 2 * ff :]
    gate_pre = mm(normed, w_g)
    up_pre = mm(normed, w_u)
    gate_act, gate_back = jax.vjp(gelu_tanh, gate_pre)
    hidden = (gate_act * up_pre).astype(BF)
    mlp_out = act_reduce(by_half(mm_t(hidden, w_d)), 5)
    result = jnp.where(valid_own, resid + mlp_out, 0.0).astype(BF)
    out_grad = jnp.where(valid_own, cotangent[0], 0.0)
    mlp_grad = act_gather(out_grad.astype(BF), 6).reshape(4 * length, width)
    hidden_grad = mm(mlp_grad, w_d)
    gate_grad = gate_back(hidden_grad * up_pre)[0].astype(BF)
    up_grad = (hidden_grad * gate_act).astype(BF)
    normed_grad = act_reduce(by_half(mm_t(gate_grad, w_g) + mm_t(up_grad, w_u)), 7)
    grad_mlp = jnp.concatenate(
        [t_mm(normed, gate_grad).astype(BF), t_mm(normed, up_grad).astype(BF), t_mm(mlp_grad, hidden).astype(BF)],
        axis=1,
    )
    gain2_part = jnp.sum(normed_grad * unit2, axis=0)
    resid_grad = out_grad + norm_back(normed_grad * gain2, unit2, scale2)
    rg = act_gather(resid_grad.astype(BF), 8)
    rec_grad = rg.reshape(4 * length, width)
    rec_grad_own = lax.dynamic_index_in_dim(rg, q, 0, False).reshape(length, width)
    mixed_grad = jnp.concatenate(
        [
            mm(rec_grad, recq[:, 2 * blk :]).reshape(4, length, blk),
            mm(rec_grad_own, rec4[:, 2 * blk :]).reshape(1, length, blk),
        ],
        axis=0,
    )
    low, gate_w_grad, vec_grad = rec_backward(taps, pre, gates, vec, ends, conv, rate, gate, state, mixed_grad)
    low_a, low_b = low[:4].reshape(4 * length, 2 * blk), low[4]
    u_part = with_own(mm_t(low_a, recq[:, : 2 * blk]), mm_t(low_b, rec4[:, : 2 * blk]))
    u_grad = act_reduce(by_half(u_part), 9)
    grad_q = jnp.concatenate([t_mm(u_all, low_a).astype(BF), t_mm(rec_grad, mixed_a).astype(BF)], axis=1)
    grad_4 = jnp.concatenate([t_mm(u_own, low_b).astype(BF), t_mm(rec_grad_own, mixed_b).astype(BF)], axis=1)
    gain1_part = jnp.sum(u_grad * unit1, axis=0)
    token_grad = resid_grad + norm_back(u_grad * gain1, unit1, scale1)
    gains = lax.psum(jnp.stack([gain1_part, gain2_part]), "tensor")

    nvg = vec_grad.shape[1]
    depth = -(-(rb + nvg + 2) // 8) * 8

    def small_grads(h, extra):
        v = vec_grad[h].reshape(nvg, n, rb).transpose(1, 0, 2)
        v = jnp.pad(v, ((0, 0), (0, 0), (0, 2 * blk - rb)))
        g = extra.reshape(2, n, rows).transpose(1, 0, 2)
        g = jnp.pad(g, ((0, 0), (0, 0), (0, 2 * blk - rows)))
        s = jnp.concatenate([gate_w_grad[h].reshape(n, rb, 2 * blk), v, g], axis=1)
        return jnp.pad(s, ((0, 0), (0, depth - s.shape[1]), (0, 0)))

    sq = small_grads(0, jnp.zeros_like(gains))
    s4 = small_grads(1, gains)

    def slots(a):
        return a.reshape(n, rows, a.shape[1])

    o_mlp, o_q, o_4, o_sq, o_s4 = grad_reduce(
        (slots(grad_mlp), slots(grad_q), slots(grad_4), sq, s4), (True, True, False, True, False), n, 10
    )
    rec_out = jnp.concatenate([o_q, o_4[None]], axis=0)
    so = jnp.concatenate([o_sq, o_s4[None]], axis=0)

    def heads_cols(a):
        return a.transpose(1, 0, 2).reshape(rows, heads * blk)

    def quarter_cols(a):
        return a.transpose(1, 0, 2).reshape(rows, 4 * ff)

    def vec_out(i):
        return so[:, rb + i, :rb]

    return (
        result[None],
        token_grad[None],
        o_s4[rb + nvg, :rows],
        heads_cols(rec_out[:, :, :blk]),
        heads_cols(rec_out[:, :, blk : 2 * blk]),
        so[:, :rb, :blk],
        so[:, :rb, blk:],
        vec_out(0),
        vec_out(1),
        vec_out(2),
        jnp.stack([vec_out(4 + k) for k in range(taps)]),
        vec_out(3),
        rec_out[:, :, 2 * blk :].transpose(0, 2, 1).reshape(heads * blk, rows),
        o_s4[rb + nvg + 1, :rows],
        quarter_cols(o_mlp[:, :, :ff]),
        quarter_cols(o_mlp[:, :, ff : 2 * ff]),
        o_mlp[:, :, 2 * ff :].transpose(0, 2, 1).reshape(4 * ff, rows),
    )


def solution(mesh):
    return jax.shard_map(
        local,
        mesh=mesh,
        in_specs=(
            P("dp", "tensor", None),
            P("dp", None),
            P("dp"),
            P("dp", "tensor"),
            P("dp", "tensor"),
            P("tensor", "dp", None),
            P("tensor", "dp", None),
            P("tensor", "dp"),
            P("tensor", "dp"),
            P("tensor", "dp"),
            P(None, "tensor", "dp"),
            P("tensor", "dp"),
            P("tensor", "dp"),
            P("dp"),
            P("dp", "tensor"),
            P("dp", "tensor"),
            P("tensor", "dp"),
            P("dp", "tensor", None),
        ),
        out_specs=(
            P("dp", "tensor", None),
            P("dp", "tensor", None),
            P("dp"),
            P("dp", "tensor"),
            P("dp", "tensor"),
            P("tensor", "dp", None),
            P("tensor", "dp", None),
            P("tensor", "dp"),
            P("tensor", "dp"),
            P("tensor", "dp"),
            P(None, "tensor", "dp"),
            P("tensor", "dp"),
            P("tensor", "dp"),
            P("dp"),
            P("dp", "tensor"),
            P("dp", "tensor"),
            P("tensor", "dp"),
        ),
        check_vma=False,
    )
```

time: 3580 us -> 939 us (0.26)
  waiting for transfers between devices: 2640 us -> 0 us
  Pallas kernels: 0 us -> 725 us
  blocking collectives: 440 us -> 3.36 us
  local copies, waits for them, and re-layouts: 234 us -> 69.8 us
  matrix products: 147 us -> 84.7 us
  other arithmetic: 86.6 us -> 43.7 us
    reduce_scatter x12 -> x0, waiting for transfers between devices: 1880 us -> none  [the longest x1 372 us: local(): lax.psum_scatter(grad_w_up, 'dp', scatter_dimension=0, tiled=True)]
    pallas_call x0 -> x12, Pallas kernels: none -> 725 us  [the longest x1 259 us: grad_reduce(): pl.pallas_call(functools.partial(grad_reduce_kernel, high, narr, picked),...]
    all_gather x10 -> x0, waiting for transfers between devices: 499 us -> none  [the longest x1 200 us: local(): lax.all_gather(w_down, 'dp', axis=1, tiled=True)]
    all_gather x9 -> x0, blocking collectives: 360 us -> none  [the longest x1 46.8 us: local(): lax.all_gather(w_igate, 'dp', axis=1, tiled=True)]
    unnamed x32 -> x0, waiting for transfers between devices: 260 us -> none
    slice x105 -> x11, local copies, waits for them, and re-layouts: 148 us -> 8.32 us  [the longest x1 2.06 us: small_grads(): s = jnp.concatenate([gate_w_grad[h].reshape(n, rb, 2 * blk), v, g], axis=1)]
    unnamed x1 -> x0, blocking collectives: 77.1 us -> none
    dot_general x24 -> x21, matrix products: 147 us -> 84.7 us  [the longest x7 30 us: mm_t(): lax.dot_general(a, b, (((1,), (1,)), ((), ())), preferred_element_type=F32)]
  transfers between devices with their start and end apart: 27 -> 0, of which waited for: 17 -> 0; matrix products, arithmetic and copies ran while one was open for 8% -> 0% of each run, Pallas kernels for 0% -> 0%
where the time goes in v1:
time: 939 us; the launch traced here: 931 us
  Pallas kernels  725 us (77%)
  matrix products  84.7 us (9%)
  local copies, waits for them, and re-layouts  69.8 us (7%)
  other arithmetic  43.7 us (5%)
    pallas_call x1, Pallas kernels, grad_reduce(): pl.pallas_call(functools.partial(grad_reduce_kernel, high, narr, picked),...  259 us
    pallas_call x1, Pallas kernels, weight_gather(): pl.pallas_call(functools.partial(weight_gather_kernel, high, narr, picked...  200 us
    pallas_call x4, Pallas kernels, act_reduce(): pl.pallas_call(act_reduce_kernel, out_shape=jax.ShapeDtypeStruct((half, w...  128 us
    pallas_call x4, Pallas kernels, act_gather(): pl.pallas_call(act_gather_kernel, out_shape=jax.ShapeDtypeStruct((4, 2, h...  115 us
    dot_general x7, matrix products, mm_t(): lax.dot_general(a, b, (((1,), (1,)), ((), ())), preferred_element_type=F32)  30 us
    dot_general x7, matrix products, mm(): return jnp.dot(a, b, preferred_element_type=F32)  29.7 us
    dot_general x7, matrix products, t_mm(): lax.dot_general(a, b, (((0,), (0,)), ((), ())), preferred_element_type=F32)  25 us

profile of v1, /device:TPU:0, one launch (start us, length us, event | category | flops | bytes accessed | tf_op | source)
XLA Modules:
  0.0 931.1 jit_solution(5247138332981227758)
XLA Ops:
  25.2 30.2 %act_gather.6 = bf16[4,2,128,2048]{3,2,1,0:T(8,128)(2,1)} custom-call(bf16[128,2048]{1,0:T(8,128)(2,1)} %fusion.43.x_ref), custom_call_target="tpu_custom_call" | custom-call | tf_op jit(solution)/shard_map/act_gather/pallas_call | solution.py:85
  55.3 200.5 %weight_gather.1 = (bf16[16,128,768]{2,1,0:T(8,128)(2,1)}, bf16[16,128,768]{2,1,0:T(8,128)(2,1)}, bf16[16,16,512]{2,1,0:T(8,128)(2,1)}, bf16[16,16,512]{2,1,0:T(...) custom-call(bf16[4,128,768]{2,1,0:T(8,128)(2,1)} %slice.219.refs_0_, ...), custom_call_target="tpu_custom_call" | custom-call | tf_op jit(solution)/shard_map/weight_gather/pallas_call | solution.py:212
  262.6 27.6 %act_gather.4 = bf16[4,2,128,2048]{3,2,1,0:T(8,128)(2,1)} custom-call(bf16[128,2048]{1,0:T(8,128)(2,1)} %fusion.33.x_ref), custom_call_target="tpu_custom_call" | custom-call | tf_op jit(solution)/shard_map/act_gather/pallas_call | solution.py:85
  294.1 3.9 fusion.25
  299.7 9.3 %rec_forward.1 = (bf16[5,256,256]{2,1,0:T(8,128)(2,1)}, f32[5,256,256]{2,1,0:T(8,128)}, f32[5,256,256]{2,1,0:T(8,128)}, f32[5,256,256]{2,1,0:T(8,128)}, f32[5,256,256]{2,1,0:T(8,128)}) custom-call(f32[5,256,512]{2,1,0:T(8,128)} %pad_maximum_fusion.3.p_ref, bf16[2,256,512]{2,1,0:T(8,128)(2,1)} %pad_maximum_fusion.6.g_ref, ...), custom_call_target="tpu_custom_call" | custom-call | tf_op jit(solution)/shard_map/rec_forward/pallas_call | solution.py:446
  317.5 31.9 %act_reduce.4 = f32[128,2048]{1,0:T(8,128)} custom-call(bf16[4,2,128,2048]{3,2,1,0:T(8,128)(2,1)} %bitcast.202), custom_call_target="tpu_custom_call" | custom-call | tf_op jit(solution)/shard_map/act_reduce/pallas_call | solution.py:135
  351.8 28.4 %act_gather.5 = bf16[4,2,128,2048]{3,2,1,0:T(8,128)(2,1)} custom-call(bf16[128,2048]{1,0:T(8,128)(2,1)} %multiply_convert_fusion.2.x_ref), custom_call_target="tpu_custom_call" | custom-call | tf_op jit(solution)/shard_map/act_gather/pallas_call | solution.py:85
  380.3 6.5 fusion.11
  386.8 5.5 fusion.15
  392.3 7.3 multiply_convert_fusion
  399.7 3.9 convolution_convert_fusion.1
  403.6 3.9 convolution_convert_fusion.2
  407.4 3.9 convolution_convert_fusion.3
  411.3 4.7 pad_maximum_fusion
  416.0 12.4 %copy.53 = bf16[2048,2304]{1,0:T(8,128)(2,1)} copy(bf16[2048,2304]{0,1:T(8,128)(2,1)} %pad_maximum_fusion) | data formatting | bytes 18874368 | tf_op jit(solution)/shard_map/concatenate | solution.py:616
  428.4 7.8 convolution_convert_fusion
  436.3 31.9 %act_reduce.5 = f32[128,2048]{1,0:T(8,128)} custom-call(bf16[4,2,128,2048]{3,2,1,0:T(8,128)(2,1)} %bitcast.213), custom_call_target="tpu_custom_call" | custom-call | tf_op jit(solution)/shard_map/act_reduce/pallas_call | solution.py:135
  468.2 5.9 fusion.13
  474.1 7.1 add_convert_fusion
  481.2 31.9 %act_reduce.6 = f32[128,2048]{1,0:T(8,128)} custom-call(bf16[4,2,128,2048]{3,2,1,0:T(8,128)(2,1)} %bitcast.212), custom_call_target="tpu_custom_call" | custom-call | tf_op jit(solution)/shard_map/act_reduce/pallas_call | solution.py:135
  514.6 3.6 fusion.84
  518.2 28.5 %act_gather.7 = bf16[4,2,128,2048]{3,2,1,0:T(8,128)(2,1)} custom-call(bf16[128,2048]{1,0:T(8,128)(2,1)} %get-tuple-element.80.x_ref), custom_call_target="tpu_custom_call" | custom-call | tf_op jit(solution)/shard_map/act_gather/pallas_call | solution.py:85
  546.7 4.6 convolution_convert_fusion.7
  559.1 14.3 %rec_backward.1 = (bf16[5,256,512]{2,1,0:T(8,128)(2,1)}, f32[2,256,512]{2,1,0:T(8,128)}, f32[2,8,256]{2,1,0:T(8,128)}) custom-call(f32[5,256,512]{2,1,0:T(8,128)} %pad_maximum_fusion.3.p_ref, bf16[2,256,512]{2,1,0:T(8,128)(2,1)} %pad_maximum_fusion.6.g_ref, f32[2,16,256]{2,1,0:T(8,128)} %select_maximum_fusion.3.v_ref, f32[5,8,128]{2,1,0:T(8,128)} %broadcast_in_dim.46.e_ref, ...), custom_call_target="tpu_custom_call" | custom-call | tf_op jit(solution)/shard_map/rec_backward/pallas_call | solution.py:462
  582.2 4.8 copy.55
  587.1 4.7 convolution_convert_fusion.5
  593.7 4.8 copy.54
  598.5 4.0 fusion.24
  607.8 32.0 %act_reduce.7 = f32[128,2048]{1,0:T(8,128)} custom-call(bf16[4,2,128,2048]{3,2,1,0:T(8,128)(2,1)} %bitcast.203), custom_call_target="tpu_custom_call" | custom-call | tf_op jit(solution)/shard_map/act_reduce/pallas_call | solution.py:135
  641.4 3.4 psum.7
  648.5 258.9 %grad_reduce.1 = (f32[4,128,2304]{2,1,0:T(8,128)}, f32[4,128,768]{2,1,0:T(8,128)}, f32[128,768]{1,0:T(8,128)}, f32[4,32,512]{2,1,0:T(8,128)}, f32[32,512]{1,0:T(8,128)}) custom-call(bf16[16,128,2304]{2,1,0:T(8,128)(2,1)} %bitcast.201, bf16[16,128,768]{2,1,0:T(8,128)(2,1)} %bitcast.205, bf16[16,128,768]{2,1,0:T(8,128)(2,1)} %bitcast.204, ...), custom_call_target="tpu_custom_call" | custom-call | tf_op jit(solution)/shard_map/grad_reduce/pallas_call | solution.py:283
  917.2 4.0 slice_bitcast_fusion.3
  (156 shorter events, 95.0 us)
Async XLA Ops:
  0.7 17.3 %copy-start.14 = (bf16[1280,128]{1,0:T(8,128)(2,1)S(1)}, bf16[1280,128]{1,0:T(8,128)(2,1)}, u32[]{:S(2)}) copy-start(bf16[1280,128]{1,0:T(8,128)(2,1)} %param.30) | copy-start | bytes 983044
  16.3 3.6 copy-start.5
  18.0 2.8 copy-start.12
  21.2 2.1 copy-start.13
  55.3 206.3 %copy-start = (bf16[1,128,2048]{2,1,0:T(8,128)(2,1)S(1)}, bf16[1,128,2048]{2,1,0:T(8,128)(2,1)}, u32[]{:S(2)}) copy-start(bf16[1,128,2048]{2,1,0:T(8,128)(2,1)} %param.18) | copy-start | bytes 1572868
  290.2 3.9 copy-start.1
  380.3 6.5 copy-start.4
  386.8 5.5 copy-start.3
  399.6 3.9 copy-start.19
  399.6 3.9 copy-start.17
  399.7 7.8 copy-start.16
  468.1 5.9 copy-start.18
  546.7 4.6 copy-start.2
  577.5 2.8 copy-start.6
  582.2 4.8 copy-start.9
  587.1 4.7 copy-start.11
  602.4 1.9 copy-start.8
  607.8 37.0 %copy-start.7 = (f32[128,2048]{1,0:T(8,128)S(1)}, f32[128,2048]{1,0:T(8,128)}, u32[]{:S(2)}) copy-start(f32[128,2048]{1,0:T(8,128)} %get-tuple-element.81) | copy-start | bytes 3145732
  907.5 2.9 copy-start.15
  907.5 3.4 copy-start.10

commit v2 on v1

--- a/solution.py
+++ b/solution.py
@@ -480,6 +480,620 @@
     )(pre, gates, vec, ends, conv, r, gate, state, mixed_grad)
 
 
+class Gather:
+    def __init__(self, slot, parts, sems, here, there, core):
+        self.slot, self.parts, (self.send, self.recv, self.fsend) = slot, parts, sems
+        zh, zl, y, x = here
+        self.q = zl * 2 + x
+        self.me = dp_at(zh, zl, y, x)
+        self.near = [dp_at(h, z, y, w) for h, z, w in there]
+        self.far = [dp_at(h, z, 1 - y, w) for h, z, w in there]
+        self.pick = [z * 2 + w for _, z, w in there]
+        self.core = core
+        self.other = dev(dp_at(zh, zl, 1 - y, x), core)
+
+    def ks(self, far):
+        count = len(self.near)
+        return range(4, count) if far else range(4)
+
+    def start(self, far):
+        for k in self.ks(far):
+            for piece, part in self.parts:
+                src = piece(self.pick[k])
+                dst = part(self.slot(self.me, self.pick[k]))
+                if k == 0:
+                    pltpu.make_async_copy(src, dst, self.send.at[0]).start()
+                else:
+                    d = dev(self.near[k], self.core)
+                    remote(src, dst, self.send.at[k], self.recv.at[self.me], d).start()
+
+    def forward(self, k):
+        land = self.slot(self.near[k], self.q)
+        if k == 0:
+            pltpu.make_async_copy(land, land, self.send.at[0]).wait()
+        else:
+            remote(land, land, self.send.at[k], self.recv.at[self.near[k]], self.other).wait_recv()
+        remote(land, land, self.fsend.at[k], self.recv.at[self.near[k]], self.other).start()
+
+    def forward_all(self, far):
+        for k in self.ks(far):
+            self.forward(k)
+
+    def arrive_all(self):
+        for k in range(len(self.far)):
+            land = self.slot(self.far[k], self.q)
+            remote(land, land, self.fsend.at[k], self.recv.at[self.far[k]], self.other).wait_recv()
+
+    def finish(self):
+        for k in range(len(self.near)):
+            land = self.slot(self.near[k], self.q)
+            remote(land, land, self.fsend.at[k], self.recv.at[self.near[k]], self.other).wait_send()
+            if k:
+                remote(land, land, self.send.at[k], self.recv.at[self.near[k]], self.other).wait_send()
+
+
+class Rows:
+    def __init__(self, buf, sems, here, core):
+        self.buf, (self.send, self.recv, self.fsend, self.frecv) = buf, sems
+        self.here, self.core = here, core
+        zh, zl, y, x = here
+        self.q = zl * 2 + x
+        self.sib = dev(dp_at(zh, zl, y, x), 1 - core)
+
+    def at(self, k):
+        zh, zl, y, x = self.here
+        pz, px = (zl + k // 2) % 2, (x + k % 2) % 2
+        return pz * 2 + px, dev(dp_at(zh, pz, y, px), self.core)
+
+    def start(self):
+        own = self.buf.at[self.q, self.core]
+        remote(own, own, self.fsend.at[0], self.frecv.at[self.q], self.sib).start()
+        for k in (1, 2, 3):
+            _, d = self.at(k)
+            remote(own, own, self.send.at[k], self.recv.at[self.q], d).start()
+
+    def forward(self, k):
+        pq, d = self.at(k)
+        land = self.buf.at[pq, self.core]
+        remote(land, land, self.send.at[k], self.recv.at[pq], d).wait_recv()
+        remote(land, land, self.fsend.at[k], self.frecv.at[pq], self.sib).start()
+
+    def arrive(self, k):
+        pq, _ = self.at(k)
+        land = self.buf.at[pq, 1 - self.core]
+        remote(land, land, self.fsend.at[k], self.frecv.at[pq], self.sib).wait_recv()
+
+    def finish(self):
+        own = self.buf.at[self.q, self.core]
+        for k in range(4):
+            remote(own, own, self.fsend.at[k], self.frecv.at[self.q], self.sib).wait_send()
+            if k:
+                remote(own, own, self.send.at[k], self.recv.at[self.q], self.sib).wait_send()
+
+
+def row_sems():
+    return [pltpu.SemaphoreType.DMA((4,))] * 4
+
+
+class Sums:
+    def __init__(self, part, sib, got, sems, rows):
+        self.part, self.sib_buf, self.got = part, sib, got
+        self.ssend, self.srecv, self.send, self.recv = sems
+        self.rows = rows
+
+    def push(self, k):
+        r = self.rows
+        pq, _ = r.at(k)
+        remote(
+            self.part.at[pq, 1 - r.core], self.sib_buf.at[pq], self.ssend.at[k], self.srecv.at[pq], r.sib
+        ).start()
+
+    def pair(self, k):
+        r = self.rows
+        pq, _ = r.at(k)
+        land = self.sib_buf.at[pq]
+        remote(land, land, self.ssend.at[k], self.srecv.at[pq], r.sib).wait_recv()
+        return self.part[pq, r.core].astype(F32) + self.sib_buf[pq].astype(F32)
+
+    def pass_on(self, k):
+        r = self.rows
+        pq, d = r.at(k)
+        self.part[pq, r.core] = self.pair(k).astype(BF)
+        remote(self.part.at[pq, r.core], self.got.at[r.q], self.send.at[k], self.recv.at[r.q], d).start()
+
+    def take(self, k):
+        r = self.rows
+        pq, _ = r.at(k)
+        land = self.got.at[pq]
+        remote(land, land, self.send.at[k], self.recv.at[pq], r.sib).wait_recv()
+        return self.got[pq].astype(F32)
+
+    def finish(self):
+        r = self.rows
+        land = self.got.at[r.q]
+        for k in range(4):
+            remote(land, land, self.ssend.at[k], self.srecv.at[r.q], r.sib).wait_send()
+            if k:
+                remote(land, land, self.send.at[k], self.recv.at[r.q], r.sib).wait_send()
+
+
+def rec_unit(taps, branch, conv_in, vec, gates, ends, state_ref, a_ref):
+    length, blk = branch.shape
+    same = segments(ends, length, blk, taps)
+    conv = conv_in * vec[4:5] + vec[4 + taps : 5 + taps]
+    for k in range(1, taps):
+        conv = conv + pltpu.roll(conv_in, k, 0) * same[k - 1] * vec[4 + k : 5 + k]
+    pre = jnp.dot(conv.astype(BF), gates, preferred_element_type=F32)
+    r = jax.nn.sigmoid(pre[:, :blk] + vec[0:1])
+    gate = jax.nn.sigmoid(pre[:, blk:] + vec[1:2])
+    log_a = (-DECAY * r) * vec[2:3]
+    a = jnp.exp(log_a)
+    start = same[0] == 0.0
+    a_eff = jnp.where(start, 0.0, a)
+    mult = jnp.where(start, 1.0, jnp.sqrt(-jnp.tanh(log_a) * (1.0 + a * a)))
+    full_scan(a_eff, mult * gate * conv, state_ref, a_ref, False)
+    act, _ = gelu_parts(branch)
+    return conv, r, gate, (state_ref[...] * act).astype(BF)
+
+
+SMALL_ROWS = 96
+
+
+def forward_kernel(n, taps, heads, *refs):
+    (tok, cot, wb, wi, wo, wg, wu, wd, wr, wig, small) = refs[:11]
+    (o_rec, o_mlp, o_gate, o_vec, o_gain, o_ends, o_u, o_grad, pre, conv, rate, gate, state, mixed, resid, o_norm) = refs[11:27]
+    (rec, gat, sml, u_buf, og, part, sibb, got, extra, a_scr, gfull) = refs[27:38]
+    sems = refs[38:]
+    g_sems, r1, r2, s1, (fin, h_send, h_recv) = sems[:48], sems[48:52], sems[52:56], sems[56:60], sems[60:]
+    zh, zl, y, x, c = place()
+    here = (zh, zl, y, x)
+    q, me = zl * 2 + x, dp_at(zh, zl, y, x)
+    high = n // 8
+    there = plane(zh, zl, y, x, high)
+    half, width = tok.shape
+    length, blk = pre.shape[1], pre.shape[2] // 2
+    ff = wg.shape[1] // 4
+    rb, rr = wr.shape[1], wb.shape[0]
+    greet(
+        [dev(dp_at(h, z, y, w), c) for h, z, w in there[1:]]
+        + [dev(dp_at(zh, zl, 1 - y, x), c), dev(me, 1 - c)]
+    )
+
+    def whole(ref):
+        return ref
+
+    def head_cols(ref):
+        return lambda p: ref.at[:, pl.ds(pl.multiple_of(p * blk, 128), blk)]
+
+    def make(i, slot, parts):
+        return Gather(slot, parts, g_sems[3 * i : 3 * i + 3], here, there, c)
+
+    smalls = make(0, lambda s, g: sml.at[s], [(lambda p: small, whole)])
+    gats, recs, mlps = [], [], []
+    for h in range(2):
+        pick = (lambda ref: lambda p: ref.at[p]) if h == 0 else (lambda ref: lambda p: ref.at[heads - 1])
+        gats.append(
+            make(
+                1 + h,
+                lambda s, g, h=h: gat.at[h, s],
+                [
+                    (pick(w), lambda r, i=i: r.at[:, pl.ds(i * blk, blk)])
+                    for i, w in enumerate((wr, wig))
+                ],
+            )
+        )
+    for i, w in enumerate((wb, wi, wo)):
+        recs.append(make(3 + i, lambda s, g, i=i: rec.at[0, i, s], [(head_cols(w), whole)]))
+    quarter = rr // 4
+
+    def shared_piece(ref):
+        return lambda p: ref.at[pl.ds(pl.multiple_of(p * quarter, 8), quarter), pl.ds((heads - 1) * blk, blk)]
+
+    def shared_rows(s, g):
+        return rec.at[1, :, s, pl.ds(pl.multiple_of(g * quarter, 8), quarter), :]
+
+    shared = make(
+        6, shared_rows, [(shared_piece(w), lambda r, i=i: r.at[i]) for i, w in enumerate((wb, wi, wo))]
+    )
+    for i, w in enumerate((wg, wu, wd)):
+        for t in range(ff // blk):
+            piece = lambda p, w=w, t=t: w.at[:, pl.ds(pl.multiple_of(p * ff + t * blk, 128), blk)]
+            j = i * (ff // blk) + t
+            mlps.append(make(7 + j, lambda s, g, j=j: o_mlp.at[j, s], [(piece, whole)]))
+    count = len(there)
+    order = [recs[0], gats[0], recs[1], gats[1], shared, recs[2]] + mlps
+    ahead = 2
+
+    def pump(j):
+        if j + ahead < len(order):
+            order[j + ahead].forward_all(False)
+        order[j].forward_all(True)
+        if j + ahead < len(order):
+            order[j + ahead].start(True)
+        if j + 2 * ahead < len(order):
+            order[j + 2 * ahead].start(False)
+
+    smalls.start(True)
+    smalls.start(False)
+    for j in range(2 * ahead):
+        if j < ahead:
+            order[j].start(True)
+        order[j].start(False)
+
+    xin = tok[...].astype(F32)
+    unit = xin * lax.rsqrt(jnp.mean(xin * xin, axis=-1, keepdims=True) + EPS)
+    resid[...] = unit
+    smalls.forward_all(False)
+    smalls.forward_all(True)
+    for j in range(ahead):
+        order[j].forward_all(False)
+    smalls.arrive_all()
+    per_vec, per_gain = blk // 128, width // 128
+    base = (heads - 1) * 16
+    for h in range(2):
+        at = pl.multiple_of(q * 16, 16) if h == 0 else base
+        groups = [jnp.zeros((16, 128), F32)] * per_vec
+        for s in range(n):
+            g = s * rb // 128
+            groups[g] = groups[g] + sml[s, pl.ds(at, 16), :].astype(F32)
+        raw = jnp.concatenate(groups, axis=1)
+        decay = raw[2:3]
+        o_vec[h, 0:2, :] = raw[0:2]
+        o_vec[h, 2:3, :] = jnp.log1p(jnp.exp(-decay))
+        o_vec[h, 3:4, :] = jax.nn.sigmoid(-decay)
+        o_vec[h, 4 : 5 + taps, :] = raw[3 : 4 + taps]
+    groups = [None] * per_gain
+    for s in range(n):
+        g = s * rr // 128
+        v = sml[s, SMALL_ROWS - 16 : SMALL_ROWS, :].astype(F32)
+        groups[g] = v if groups[g] is None else groups[g] + v
+    for g in range(per_gain):
+        o_gain[:, g * 128 : (g + 1) * 128] = groups[g][0:8]
+    for j in range(4):
+        v = sml[dp_at(zh, j // 2, y, j % 2), SMALL_ROWS - 16 : SMALL_ROWS, :].astype(F32)
+        o_ends[j] = jnp.broadcast_to(v[2:3], (8, 128))
+    u_rows = Rows(u_buf, r1, here, c)
+    g_rows = Rows(o_grad, r2, here, c)
+    u_buf[q, c] = (resid[...] * o_gain[0:1, :]).astype(BF)
+    u_rows.start()
+    e3 = o_ends[q][0:1, 3:4]
+    spot = lax.broadcasted_iota(jnp.int32, (half, 1), 0).astype(F32) + (c * half).astype(F32)
+    og[...] = jnp.where(spot < e3, cot[...], 0.0).astype(BF)
+    own_grad = o_grad.at[q, c]
+    place_grad = pltpu.make_async_copy(og, own_grad, fin.at[0])
+    place_grad.start()
+    place_grad.wait()
+    g_rows.start()
+    for j in range(3):
+        pump(j)
+    for k in (1, 2, 3):
+        u_rows.forward(k)
+    for j in range(3, 6):
+        pump(j)
+    for a in gats + recs[:2] + [shared]:
+        a.arrive_all()
+
+    def group_region(g):
+        return rec.at[1, :, :, pl.ds(pl.multiple_of(g * quarter, 8), quarter), :]
+
+    for k in (1, 2, 3):
+        _, d = u_rows.at(k)
+        remote(group_region(q), group_region(q), h_send.at[k], h_recv.at[q], d).start()
+    for h in range(2):
+        if rb % 16 == 0:
+            o_gate[h] = gat[h].reshape(blk, 2 * blk)
+        else:
+            for s in range(n):
+                gfull[s * rb : (s + 1) * rb, :] = gat[h, s].astype(F32)
+            o_gate[h] = gfull[...].astype(BF)
+    for k in range(4):
+        u_rows.arrive(k)
+    recs[2].arrive_all()
+    for k in (1, 2, 3):
+        pq, d = u_rows.at(k)
+        remote(group_region(pq), group_region(pq), h_send.at[k], h_recv.at[pq], d).wait_recv()
+    keep = [pltpu.make_async_copy(rec, o_rec, fin.at[1]), pltpu.make_async_copy(u_buf, o_u, fin.at[2])]
+    for cp in keep:
+        cp.start()
+
+    sums = Sums(part, sibb, got, s1, u_rows)
+
+    def step(i, carry):
+        h = jnp.where(i == 0, 1, 0)
+        k = jnp.maximum(i - 1, 0)
+        pq, _ = u_rows.at(k)
+        at = jnp.where(i == 0, 4, pq)
+        rows = u_buf[pq].reshape(2 * half, width)
+        for j in range(2):
+            w = rec[h, j].reshape(width, blk)
+            pre[at, :, j * blk : (j + 1) * blk] = mm(rows, w)
+        cv, rt, gt, mx = rec_unit(
+            taps, pre[at, :, :blk], pre[at, :, blk:], o_vec[h], o_gate[h], o_ends[pq][0:1, :], state.at[at], a_scr
+        )
+        conv[at], rate[at], gate[at], mixed[at] = cv, rt, gt, mx
+        per = 512 // rr if rr <= 512 else 1
+
+        def cols_out(t, carry):
+            w = rec[h, 2, pl.ds(t * per, per)].reshape(per * rr, blk)
+            tile = mm_t(mx, w)
+            lanes = pl.ds(pl.multiple_of(t * (per * rr), 128), per * rr)
+            tile = tile + jnp.where(i == 1, extra[:, lanes], 0.0)
+
+            @pl.when(i == 0)
+            def _():
+                extra[:, lanes] = tile
+
+            @pl.when(i > 0)
+            def _():
+                part[pq, 0, :, lanes] = tile[:half].astype(BF)
+                part[pq, 1, :, lanes] = tile[half:].astype(BF)
+
+            return carry
+
+        lax.fori_loop(0, width // (per * rr), cols_out, 0)
+
+        @pl.when(i > 0)
+        def _():
+            sums.push(k)
+
+        @pl.when(i == 2)
+        def _():
+            resid[...] = tok[...].astype(F32) + sums.pair(0)
+
+        @pl.when(i > 2)
+        def _():
+            sums.pass_on(k - 1)
+
+        for j, m in ((1, 6), (3, 7)):
+
+            @pl.when(i == j)
+            def _():
+                pump(m)
+
+        return carry
+
+    extra[...] = jnp.zeros_like(extra)
+    lax.fori_loop(0, 5, step, 0)
+    sums.pass_on(3)
+    pump(8)
+    for k in (1, 2, 3):
+        g_rows.forward(k)
+    for k in (1, 2, 3):
+        resid[...] += sums.take(k)
+    total = resid[...]
+    unit = total * lax.rsqrt(jnp.mean(total * total, axis=-1, keepdims=True) + EPS)
+    o_norm[...] = (unit * o_gain[1:2, :]).astype(BF)
+    for j in range(9, len(order)):
+        pump(j)
+    for a in mlps:
+        a.arrive_all()
+    for k in range(4):
+        g_rows.arrive(k)
+    for k in (1, 2, 3):
+        _, d = u_rows.at(k)
+        remote(group_region(q), group_region(q), h_send.at[k], h_recv.at[q], d).wait_send()
+    for a in [smalls, shared] + mlps + gats + recs + [u_rows, g_rows, sums]:
+        a.finish()
+    for cp in keep:
+        cp.wait()
+
+
+def forward(tok, cot, wb, wi, wo, wg, wu, wd, wr, wig, small, n, taps, cid):
+    half, width = tok.shape
+    heads, rb, blk = wr.shape
+    rr = wb.shape[0]
+    length = 2 * half
+    ff = wg.shape[1] // 4
+    vm = pl.BlockSpec(memory_space=pltpu.VMEM)
+    hb = pl.BlockSpec(memory_space=pl.ANY)
+
+    def sds(*shape, t=F32):
+        return jax.ShapeDtypeStruct(shape, t)
+
+    unit = sds(5, length, blk)
+    outs = (
+        (sds(2, 3, n, rr, blk, t=BF), hb),
+        (sds(3 * ff // blk, n, rr, blk, t=BF), hb),
+        (sds(2, blk, 2 * blk, t=BF), vm),
+        (sds(2, 16, blk), vm),
+        (sds(8, width), vm),
+        (sds(4, 8, 128), vm),
+        (sds(4, 2, half, width, t=BF), hb),
+        (sds(4, 2, half, width, t=BF), hb),
+        (sds(5, length, 2 * blk), vm),
+        (unit, vm),
+        (unit, vm),
+        (unit, vm),
+        (unit, vm),
+        (sds(5, length, blk, t=BF), vm),
+        (sds(half, width), vm),
+        (sds(half, width, t=BF), vm),
+    )
+    count = n // 2
+    return pl.pallas_call(
+        functools.partial(forward_kernel, n, taps, heads),
+        out_shape=tuple(o for o, _ in outs),
+        in_specs=[vm, vm] + [hb] * 9,
+        out_specs=[s for _, s in outs],
+        scratch_shapes=[
+            pltpu.VMEM((2, 3, n, rr, blk), BF),
+            pltpu.VMEM((2, n, rb, 2 * blk), BF),
+            pltpu.VMEM((n, SMALL_ROWS, 128), BF),
+            pltpu.VMEM((4, 2, half, width), BF),
+            pltpu.VMEM((half, width), BF),
+            pltpu.VMEM((4, 2, half, width), BF),
+            pltpu.VMEM((4, half, width), BF),
+            pltpu.VMEM((4, half, width), BF),
+            pltpu.VMEM((length, width), F32),
+            pltpu.VMEM((length, blk), F32),
+            pltpu.VMEM((blk, 2 * blk), F32),
+        ]
+        + [
+            pltpu.SemaphoreType.DMA((count,)),
+            pltpu.SemaphoreType.DMA((n,)),
+            pltpu.SemaphoreType.DMA((count,)),
+        ]
+        * 16
+        + row_sems() * 3
+        + [pltpu.SemaphoreType.DMA((3,)), pltpu.SemaphoreType.DMA((4,)), pltpu.SemaphoreType.DMA((4,))],
+        compiler_params=pltpu.CompilerParams(
+            collective_id=cid, has_side_effects=True, vmem_limit_bytes=VMEM_LIMIT
+        ),
+        name="forward",
+    )(tok, cot, wb, wi, wo, wg, wu, wd, wr, wig, small)
+
+
+def mlp_kernel(norm, resid, gain, cot, ends, w_hbm, mg_hbm, g_hbm, o_rec, o_rgrad, o_hid, o_gain,
+               w, nbuf, mg, hg, hu, gbuf, part, sibb, got, wsem, msem, gsem, *sems):
+    zh, zl, y, x, c = place()
+    here = (zh, zl, y, x)
+    q, me = zl * 2 + x, dp_at(zh, zl, y, x)
+    half, width = norm.shape
+    nt, n, rr, blk = w.shape
+    tiles, steps, per = nt // 3, width // blk, blk // rr
+    rows = Rows(nbuf, sems[:4], here, c)
+    sums = Sums(part, sibb, got, sems[4:8], rows)
+    greet([dev(me, 1 - c)] + [rows.at(k)[1] for k in (1, 2, 3)])
+    nbuf[q, c] = norm[...]
+    rows.start()
+    loads = []
+    for t in range(tiles):
+        for i in range(3):
+            j = i * tiles + t
+            loads.append((t, pltpu.make_async_copy(w_hbm.at[j], w.at[j], wsem.at[j])))
+    loads.insert(2, (0, pltpu.make_async_copy(mg_hbm, mg, msem)))
+    for _, cp in loads:
+        cp.start()
+
+    def row(k, carry):
+        pq, _ = rows.at(k)
+        rows.arrive(k)
+
+        def first(t, carry):
+            @pl.when(k == 0)
+            def _():
+                for j, cp in loads:
+
+                    @pl.when(t == j)
+                    def _():
+                        cp.wait()
+
+            a = nbuf[pq].reshape(2 * half, width)
+            gate = mm(a, w[t].reshape(width, blk))
+            up = mm(a, w[tiles + t].reshape(width, blk))
+            grad = mm(mg[pq].reshape(2 * half, width), w[2 * tiles + t].reshape(width, blk))
+            act, der = gelu_parts(gate)
+            o_hid[pq, t] = (act * up).astype(BF)
+            hg[pq, t] = (grad * up * der).astype(BF)
+            hu[pq, t] = (grad * act).astype(BF)
+            return carry
+
+        lax.fori_loop(0, tiles, first, 0)
+
+        @pl.when(k < 3)
+        def _():
+            rows.forward(k + 1)
+
+        @pl.when(k > 1)
+        def _():
+            sums.pass_on(k - 1)
+
+        def second(d, carry):
+            total = jnp.zeros((2 * half, blk), F32)
+            for t in range(tiles):
+                total = total + mm_t(hg[pq, t], w[t, pl.ds(d * per, per)].reshape(blk, blk))
+                total = total + mm_t(hu[pq, t], w[tiles + t, pl.ds(d * per, per)].reshape(blk, blk))
+            lanes = pl.ds(pl.multiple_of(d * blk, 128), blk)
+            part[pq, 0, :, lanes] = total[:half].astype(BF)
+            part[pq, 1, :, lanes] = total[half:].astype(BF)
+            return carry
+
+        lax.fori_loop(0, steps, second, 0)
+        sums.push(k)
+        return carry
+
+    def rows_from(k, carry):
+        return row(k, carry)
+
+    lax.fori_loop(0, 4, rows_from, 0)
+    sums.pass_on(3)
+
+    def out_tile(d):
+        at = pl.ds(d * per, per)
+        return pltpu.make_async_copy(gbuf.at[:, at], g_hbm.at[:, at], gsem.at[d])
+
+    def grads(d, carry):
+        lanes = pl.ds(pl.multiple_of(d * blk, 128), blk)
+        nt_ = nbuf[:, :, :, lanes].reshape(8 * half, blk).T
+        mt_ = mg[:, :, :, lanes].reshape(8 * half, blk).T
+        for i, (left, right) in enumerate(((nt_, hg), (nt_, hu), (mt_, o_hid))):
+            for t in range(tiles):
+                tile = mm(left, right[:, t].reshape(8 * half, blk))
+                gbuf[i * tiles + t, pl.ds(d * per, per)] = tile.astype(BF).reshape(per, rr, blk)
+        out_tile(d).start()
+        return carry
+
+    lax.fori_loop(0, steps, grads, 0)
+    total = sums.pair(0)
+    for k in (1, 2, 3):
+        total = total + sums.take(k)
+    r = resid[...]
+    scale = lax.rsqrt(jnp.mean(r * r, axis=-1, keepdims=True) + EPS)
+    unit = r * scale
+    o_gain[...] = jnp.broadcast_to(jnp.sum(total * unit, axis=0, keepdims=True), o_gain.shape)
+    g2 = total * gain[1:2, :]
+    back = scale * (g2 - unit * jnp.mean(g2 * unit, axis=-1, keepdims=True))
+    e3 = ends[q][0:1, 3:4]
+    spot = lax.broadcasted_iota(jnp.int32, (half, 1), 0).astype(F32) + (c * half).astype(F32)
+    back = back + jnp.where(spot < e3, cot[...], 0.0)
+    o_rgrad[...] = back
+    o_rec[...] = back.astype(BF)
+    for d in range(steps):
+        out_tile(d).wait()
+    rows.finish()
+    sums.finish()
+
+
+def mlp_block(norm, resid, gain, cot, ends, mlp_w, mlp_grad, cid):
+    half, width = norm.shape
+    nt, n, rr, blk = mlp_w.shape
+    tiles = nt // 3
+    vm = pl.BlockSpec(memory_space=pltpu.VMEM)
+    hb = pl.BlockSpec(memory_space=pl.ANY)
+    hid = (4, tiles, 2 * half, blk)
+    return pl.pallas_call(
+        mlp_kernel,
+        out_shape=(
+            jax.ShapeDtypeStruct(mlp_w.shape, BF),
+            jax.ShapeDtypeStruct((half, width), BF),
+            jax.ShapeDtypeStruct((half, width), F32),
+            jax.ShapeDtypeStruct(hid, BF),
+            jax.ShapeDtypeStruct((8, width), F32),
+        ),
+        in_specs=[vm] * 5 + [hb] * 2,
+        out_specs=[hb] + [vm] * 4,
+        scratch_shapes=[
+            pltpu.VMEM(mlp_w.shape, BF),
+            pltpu.VMEM((4, 2, half, width), BF),
+            pltpu.VMEM((4, 2, half, width), BF),
+            pltpu.VMEM(hid, BF),
+            pltpu.VMEM(hid, BF),
+            pltpu.VMEM(mlp_w.shape, BF),
+            pltpu.VMEM((4, 2, half, width), BF),
+            pltpu.VMEM((4, half, width), BF),
+            pltpu.VMEM((4, half, width), BF),
+            pltpu.SemaphoreType.DMA((nt,)),
+            pltpu.SemaphoreType.DMA,
+            pltpu.SemaphoreType.DMA((width // blk,)),
+        ]
+        + row_sems() * 2,
+        compiler_params=pltpu.CompilerParams(
+            collective_id=cid, has_side_effects=True, vmem_limit_bytes=VMEM_LIMIT
+        ),
+        name="mlp_block",
+    )(norm, resid, gain, cot, ends, mlp_w, mlp_grad)
+
+
 def mm(a, b):
     return jnp.dot(a, b, preferred_element_type=F32)
 
@@ -518,73 +1132,41 @@
     rows = w_branch.shape[0]
     ff = w_gate.shape[1] // 4
 
-    def by_head(w):
-        return w.reshape(rows, heads, blk)
-
-    rec_piece = jnp.concatenate([by_head(w_branch), by_head(w_input), by_head(w_output.T)], axis=2)
-    rec_piece = rec_piece.transpose(1, 0, 2)
-
-    def by_quarter(w):
-        return w.reshape(rows, 4, ff)
-
-    mlp_piece = jnp.concatenate([by_quarter(w_gate), by_quarter(w_up), by_quarter(w_down.T)], axis=2)
-    mlp_piece = mlp_piece.transpose(1, 0, 2)
-    gate_piece = jnp.concatenate([w_rgate, w_igate], axis=2)
-    d32 = decay_param.astype(F32)
-    vecs = jnp.stack(
-        [rgate_bias.astype(F32), igate_bias.astype(F32), jax.nn.softplus(-d32), jax.nn.sigmoid(-d32)]
-        + [conv_weight[k].astype(F32) for k in range(taps)]
-        + [conv_bias.astype(F32)]
+    dp = lax.axis_index("dp")
+
+    def lanes(v, per):
+        v = v.astype(BF).reshape(-1, per)
+        at = (dp * per) % 128
+        return lax.dynamic_update_slice(jnp.zeros((v.shape[0], 128), BF), v, (0, at))
+
+    params = jnp.concatenate(
+        [rgate_bias[:, None], igate_bias[:, None], decay_param[:, None], conv_weight.transpose(1, 0, 2), conv_bias[:, None]],
+        axis=1,
     )
-    nv = vecs.shape[0]
-    vecs = jnp.pad(vecs.reshape(nv, heads * rb), ((0, 0), (0, 128 - heads * rb)))
+    params = jnp.pad(params, ((0, 0), (0, 16 - params.shape[1]), (0, 0))).reshape(heads * 16, rb)
     lens = doc_lengths.reshape(4).astype(F32)
     e0 = lens[0]
     e1 = e0 + lens[1]
     e2 = e1 + lens[2]
     e3 = e2 + lens[3]
-    ends_own = jnp.stack([e0, e1, e2, e3])
-
-    def line(v):
-        v = v.astype(F32).reshape(1, -1)
-        return jnp.pad(v, ((0, 0), (0, 128 - v.shape[1])))
-
-    smalls = jnp.concatenate([vecs, line(rec_gain), line(mlp_gain), line(ends_own)], axis=0)
-    smalls = jnp.pad(smalls, ((0, 16 - smalls.shape[0]), (0, 0)))
-
-    recq, rec4, gq, g4, small, mlp = weight_gather(
-        (rec_piece[:4], rec_piece[4], gate_piece[:4], gate_piece[4], smalls, mlp_piece),
-        (True, False, True, False, False, True), n, 1,
+    ends_own = jnp.pad(jnp.stack([e0, e1, e2, e3]).astype(BF)[None], ((0, 13), (0, 124)))
+    small = jnp.concatenate([lanes(params, rb), lanes(jnp.stack([rec_gain, mlp_gain]), rows), ends_own], axis=0)
+    (
+        rec_w, mlp_w, gates, vec, gains_all, group_ends, u, mlp_grad, pre, conv, rate, gate, state, mixed, resid, norm_own,
+    ) = forward(
+        tokens[0], cotangent[0], w_branch, w_input, w_output.T, w_gate, w_up, w_down.T, w_rgate, w_igate, small, n, taps, 1,
     )
-    recq, rec4, mlp = recq.reshape(width, -1), rec4.reshape(width, -1), mlp.reshape(width, -1)
-    gates = jnp.stack([gq.reshape(blk, 2 * blk), g4.reshape(blk, 2 * blk)])
-    vec_all = small[:, :nv, : heads * rb].reshape(n, nv, heads, rb).transpose(2, 1, 0, 3).reshape(heads, nv, blk)
-    vec = jnp.stack([lax.dynamic_index_in_dim(vec_all, q, 0, False), vec_all[4]])
-    vec = jnp.pad(vec, ((0, 0), (0, 16 - nv), (0, 0)))
-    gain1 = small[:, nv, :rows].reshape(1, width)
-    gain2 = small[:, nv + 1, :rows].reshape(1, width)
-    group_ends = small[:, nv + 2].reshape(n // 8, 2, 2, 2, 128)
-    group_ends = lax.dynamic_index_in_dim(group_ends, zh, 0, False)
-    group_ends = lax.dynamic_index_in_dim(group_ends, y, 1, False).reshape(4, 128)
+    rec_w = rec_w.reshape(2, 3, width, blk)
+    recq, rec4 = (jnp.concatenate([rec_w[h, i] for i in range(3)], axis=1) for h in range(2))
+    gain1, gain2 = gains_all[0:1], gains_all[1:2]
     own_ends = lax.dynamic_index_in_dim(group_ends, q, 0, True)
-    ends = jnp.concatenate([group_ends, own_ends], axis=0)[:, None, :]
-    ends = jnp.broadcast_to(ends, (5, 8, 128))
+    ends = jnp.concatenate([group_ends, own_ends], axis=0)
     valid_own = ((lax.broadcasted_iota(jnp.int32, (half, 1), 0) + c * half).astype(F32)) < e3
-
     x_in = tokens[0].astype(F32)
     scale1 = norm_scale(x_in)
     unit1 = x_in * scale1
-    u = act_gather((unit1 * gain1).astype(BF), 2)
     u_all = u.reshape(4 * length, width)
     u_own = lax.dynamic_index_in_dim(u, q, 0, False).reshape(length, width)
-    pre = jnp.concatenate(
-        [
-            mm(u_all, recq[:, : 2 * blk]).reshape(4, length, 2 * blk),
-            mm(u_own, rec4[:, : 2 * blk]).reshape(1, length, 2 * blk),
-        ],
-        axis=0,
-    )
-    mixed, conv, rate, gate, state = rec_forward(taps, pre, gates, vec, ends)
     mixed_a, mixed_b = mixed[:4].reshape(4 * length, blk), mixed[4]
 
     def with_own(a, b):
@@ -595,31 +1177,16 @@
     def by_half(a):
         return a.astype(BF).reshape(4, 2, half, width)
 
-    rec_part = with_own(mm_t(mixed_a, recq[:, 2 * blk :]), mm_t(mixed_b, rec4[:, 2 * blk :]))
-    resid = x_in + act_reduce(by_half(rec_part), 3)
-    scale2 = norm_scale(resid)
-    unit2 = resid * scale2
-    normed = act_gather((unit2 * gain2).astype(BF), 4).reshape(4 * length, width)
-    w_g, w_u, w_d = mlp[:, :ff], mlp[:, ff : 2 * ff], mlp[:, 2 * ff :]
-    gate_pre = mm(normed, w_g)
-    up_pre = mm(normed, w_u)
-    gate_act, gate_back = jax.vjp(gelu_tanh, gate_pre)
-    hidden = (gate_act * up_pre).astype(BF)
+    g_mlp, rec_own, resid_grad, hid, gain2_sum = mlp_block(
+        norm_own, resid, gains_all, cotangent[0], group_ends, mlp_w, mlp_grad, 4
+    )
+    hidden = hid.transpose(0, 2, 1, 3).reshape(4 * length, ff)
+    w_d = mlp_w[2 * ff // blk :].reshape(ff // blk, width, blk).transpose(1, 0, 2).reshape(width, ff)
     mlp_out = act_reduce(by_half(mm_t(hidden, w_d)), 5)
     result = jnp.where(valid_own, resid + mlp_out, 0.0).astype(BF)
-    out_grad = jnp.where(valid_own, cotangent[0], 0.0)
-    mlp_grad = act_gather(out_grad.astype(BF), 6).reshape(4 * length, width)
-    hidden_grad = mm(mlp_grad, w_d)
-    gate_grad = gate_back(hidden_grad * up_pre)[0].astype(BF)
-    up_grad = (hidden_grad * gate_act).astype(BF)
-    normed_grad = act_reduce(by_half(mm_t(gate_grad, w_g) + mm_t(up_grad, w_u)), 7)
-    grad_mlp = jnp.concatenate(
-        [t_mm(normed, gate_grad).astype(BF), t_mm(normed, up_grad).astype(BF), t_mm(mlp_grad, hidden).astype(BF)],
-        axis=1,
-    )
-    gain2_part = jnp.sum(normed_grad * unit2, axis=0)
-    resid_grad = out_grad + norm_back(normed_grad * gain2, unit2, scale2)
-    rg = act_gather(resid_grad.astype(BF), 8)
+    gain2_part = gain2_sum[0]
+    grad_mlp = g_mlp.reshape(3 * ff // blk, width, blk).transpose(1, 0, 2).reshape(width, 3 * ff)
+    rg = act_gather(rec_own, 8)
     rec_grad = rg.reshape(4 * length, width)
     rec_grad_own = lax.dynamic_index_in_dim(rg, q, 0, False).reshape(length, width)
     mixed_grad = jnp.concatenate(

time: 939 us -> 861 us (0.917)
  matrix products: 84.7 us -> 25.4 us
  other arithmetic: 43.7 us -> 16.7 us
  local copies, waits for them, and re-layouts: 69.8 us -> 94.9 us
  Pallas kernels: 725 us -> 705 us
    pallas_call x2, Pallas kernels: 210 us -> 336 us  [the longest x1 269 us: forward(): pl.pallas_call(functools.partial(forward_kernel, n, taps, heads), out_sha...]
    pallas_call x4 -> x1, Pallas kernels: 115 us -> 28.5 us  [act_gather(): pl.pallas_call(act_gather_kernel, out_shape=jax.ShapeDtypeStruct((4, 2, h...]
    pallas_call x4 -> x2, Pallas kernels: 128 us -> 69.2 us  [act_reduce(): pl.pallas_call(act_reduce_kernel, out_shape=jax.ShapeDtypeStruct((half, w...]
    dot_general x7 -> x2, matrix products: 29.7 us -> 4.54 us  [mm(): return jnp.dot(a, b, preferred_element_type=F32)]
    dot_general x7 -> x3, matrix products: 30 us -> 10.9 us  [mm_t(): lax.dot_general(a, b, (((1,), (1,)), ((), ())), preferred_element_type=F32)]
    dot_general x7 -> x4, matrix products: 25 us -> 9.87 us  [t_mm(): lax.dot_general(a, b, (((0,), (0,)), ((), ())), preferred_element_type=F32)]
    reshape x9 -> x2, local copies, waits for them, and re-layouts: 1.8 us -> 16 us  [the longest x1 12.7 us: local(): g_mlp.reshape(3 * ff // blk, width, blk).transpose(1, 0, 2)]
    concatenate x2 -> x1, local copies, waits for them, and re-layouts: 13.2 us -> 0.72 us  [local(): jnp.concatenate([rgate_bias[:, None], igate_bias[:, None], decay_param[:,...]
where the time goes in v2:
time: 861 us; the launch traced here: 850 us
  Pallas kernels  705 us (82%)
  local copies, waits for them, and re-layouts  94.9 us (11%)
  matrix products  25.4 us (3%)
  other arithmetic  16.7 us (2%)
    pallas_call x1, Pallas kernels, forward(): pl.pallas_call(functools.partial(forward_kernel, n, taps, heads), out_sha...  269 us
    pallas_call x1, Pallas kernels, grad_reduce(): pl.pallas_call(functools.partial(grad_reduce_kernel, high, narr, picked),...  257 us
    pallas_call x2, Pallas kernels, act_reduce(): pl.pallas_call(act_reduce_kernel, out_shape=jax.ShapeDtypeStruct((half, w...  69.2 us
    pallas_call x1, Pallas kernels, mlp_block(): pl.pallas_call(mlp_kernel, out_shape=(jax.ShapeDtypeStruct(mlp_w.shape, B...  66.7 us
    pallas_call x1, Pallas kernels, act_gather(): pl.pallas_call(act_gather_kernel, out_shape=jax.ShapeDtypeStruct((4, 2, h...  28.5 us
    unnamed x36, local copies, waits for them, and re-layouts  27.1 us

profile of v2, /device:TPU:0, one launch (start us, length us, event | category | flops | bytes accessed | tf_op | source)
XLA Modules:
  0.0 850.1 jit_solution(15703253254574572192)
XLA Ops:
  2.5 2.3 copy.45
  14.4 268.9 %forward.1 = (bf16[2,3,16,128,256]{4,3,2,1,0:T(8,128)(2,1)}, bf16[9,16,128,256]{3,2,1,0:T(8,128)(2,1)}, bf16[2,256,512]{2,1,0:T(8,128)(2,1)}, f32[2,16,256]{2,1,...) custom-call(bf16[128,2048]{1,0:T(8,128)(2,1)} %bitcast.161, ...), custom_call_target="tpu_custom_call" | custom-call | tf_op jit(solution)/shard_map/forward/pallas_call | solution.py:913
  283.3 66.7 %mlp_block.1 = (bf16[9,16,128,256]{3,2,1,0:T(8,128)(2,1)}, bf16[128,2048]{1,0:T(8,128)(2,1)}, f32[128,2048]{1,0:T(8,128)}, bf16[4,3,256,256]{3,2,1,0:T(8,128)(2,1)}, f32[8,2048]{1,0:T(8,128)}) custom-call(bf16[128,2048]{1,0:T(8,128)(2,1)} %get-tuple-element.47.norm, f32[128,2048]{1,0:T(8,128)} %get-tuple-element.46.resid, f32[8,2048]{1,0:T(8,128)} %get-tuple-element.48.gain, ...), custom_call_target="tpu_custom_call" | custom-call | tf_op jit(solution)/shard_map/mlp_block/pallas_call | solution.py:1064
  350.0 2.7 copy.50
  354.2 2.1 slice.125
  356.3 3.3 copy.51
  359.6 7.8 convolution_convert_fusion
  367.4 37.2 %act_reduce.2 = f32[128,2048]{1,0:T(8,128)} custom-call(bf16[4,2,128,2048]{3,2,1,0:T(8,128)(2,1)} %bitcast.169), custom_call_target="tpu_custom_call" | custom-call | tf_op jit(solution)/shard_map/act_reduce/pallas_call | solution.py:135
  404.7 2.2 fusion.26
  407.5 28.5 %act_gather.1 = bf16[4,2,128,2048]{3,2,1,0:T(8,128)(2,1)} custom-call(bf16[128,2048]{1,0:T(8,128)(2,1)} %get-tuple-element.61.x_ref), custom_call_target="tpu_custom_call" | custom-call | tf_op jit(solution)/shard_map/act_gather/pallas_call | solution.py:85
  435.9 2.9 constant_dynamic-slice_fusion
  438.8 2.1 convolution_bitcast_fusion
  440.9 2.5 fusion.19
  444.5 14.5 %rec_backward.1 = (bf16[5,256,512]{2,1,0:T(8,128)(2,1)}, f32[2,256,512]{2,1,0:T(8,128)}, f32[2,8,256]{2,1,0:T(8,128)}) custom-call(f32[5,256,512]{2,1,0:T(8,128)} %get-tuple-element.54.p_ref, bf16[2,256,512]{2,1,0:T(8,128)(2,1)} %get-tuple-element.55.g_ref, f32[2,16,256]{2,1,0:T(8,128)} %get-tuple-element.56.v_ref, f32[5,8,128]{2,1,0:T(8,128)} %pad_maximum_fusion.5.e_ref, ...), custom_call_target="tpu_custom_call" | custom-call | tf_op jit(solution)/shard_map/rec_backward/pallas_call | solution.py:462
  459.0 2.5 slice_bitcast_fusion.4
  461.6 2.4 fusion.2
  464.9 2.6 convert_element_type.62
  467.6 32.0 %act_reduce.3 = f32[128,2048]{1,0:T(8,128)} custom-call(bf16[4,2,128,2048]{3,2,1,0:T(8,128)(2,1)} %bitcast.156), custom_call_target="tpu_custom_call" | custom-call | tf_op jit(solution)/shard_map/act_reduce/pallas_call | solution.py:135
  502.2 2.6 fusion.15
  504.8 12.7 %copy.52 = bf16[9,2048,256]{1,2,0:T(8,128)(2,1)} copy(bf16[9,2048,256]{2,1,0:T(8,128)(2,1)} %bitcast.160) | data formatting | bytes 18874368 | tf_op jit(solution)/shard_map/reshape | solution.py:1188
  517.5 10.8 %copy.73 = bf16[288,8,16,128]{3,2,1,0:T(8,128)(2,1)} copy(bf16[288,8,16,128]{3,1,2,0:T(8,128)(2,1)} %bitcast.154) | data formatting | bytes 18874368
  528.3 13.1 %copy.57.refs_0_ = bf16[16,128,2304]{2,1,0:T(8,128)(2,1)} copy(bf16[16,128,2304]{1,0,2:T(8,128)(2,1)} %bitcast.155) | data formatting | bytes 18874368 | tf_op jit(solution)/shard_map/reshape;reshape | solution.py:1224
  541.4 3.6 convolution_convert_fusion.4
  545.2 2.5 convolution_convert_fusion.2
  547.9 2.8 copy.53
  554.7 2.8 copy.54
  561.0 3.6 psum.7
  566.0 256.9 %grad_reduce.1 = (f32[4,128,2304]{2,1,0:T(8,128)}, f32[4,128,768]{2,1,0:T(8,128)}, f32[128,768]{1,0:T(8,128)}, f32[4,32,512]{2,1,0:T(8,128)}, f32[32,512]{1,0:T(8,128)}) custom-call(bf16[16,128,2304]{2,1,0:T(8,128)(2,1)} %copy.57.refs_0_, bf16[16,128,768]{2,1,0:T(8,128)(2,1)} %bitcast.158, bf16[16,128,768]{2,1,0:T(8,128)(2,1)} %bitcast.159, ...), custom_call_target="tpu_custom_call" | custom-call | tf_op jit(solution)/shard_map/grad_reduce/pallas_call | solution.py:283
  833.3 4.0 slice_bitcast_fusion
  837.3 3.0 copy.61
  840.3 3.0 copy.66
  845.0 3.0 copy.67
  (86 shorter events, 37.7 us)
Async XLA Ops:
  367.4 37.3 %copy-start.3 = (f32[128,2048]{1,0:T(8,128)S(1)}, f32[128,2048]{1,0:T(8,128)}, u32[]{:S(2)}) copy-start(f32[128,2048]{1,0:T(8,128)} %get-tuple-element.46.resid) | copy-start | bytes 3145732
  367.4 39.4 %copy-start.10 = (f32[4,8,128]{2,1,0:T(8,128)S(1)}, f32[4,8,128]{2,1,0:T(8,128)}, u32[]{:S(2)}) copy-start(f32[4,8,128]{2,1,0:T(8,128)} %get-tuple-element.49.ends) | copy-start | bytes 49156
  435.9 4.9 copy-start.1
  438.8 4.6 copy-start.2
  459.0 2.6 copy-start.4
  467.6 32.0 %copy-start = (bf16[1,128,2048]{2,1,0:T(8,128)(2,1)S(1)}, bf16[1,128,2048]{2,1,0:T(8,128)(2,1)}, u32[]{:S(2)}) copy-start(bf16[1,128,2048]{2,1,0:T(8,128)(2,1)} %param.18) | copy-start | bytes 1572868
  467.6 34.7 %copy-start.6 = (f32[128,2048]{1,0:T(8,128)S(1)}, f32[128,2048]{1,0:T(8,128)}, u32[]{:S(2)}) copy-start(f32[128,2048]{1,0:T(8,128)} %get-tuple-element.53) | copy-start | bytes 3145732
  528.3 13.1 %copy-start.7 = (bf16[5,256,256]{2,1,0:T(8,128)(2,1)S(1)}, bf16[5,256,256]{2,1,0:T(8,128)(2,1)}, u32[]{:S(2)}) copy-start(bf16[5,256,256]{2,1,0:T(8,128)(2,1)} %get-tuple-element.66) | copy-start | bytes 1966084
  541.4 3.7 copy-start.9
  554.7 2.8 copy-start.11
  825.9 2.6 copy-start.5
  825.9 2.6 copy-start.8

commit v3 on v2

--- a/solution.py
+++ b/solution.py
@@ -14,7 +14,7 @@
 DECAY = 8.0
 GC = 0.7978845608028654
 GK = 0.044715
-VMEM_LIMIT = 60 * 1024 * 1024
+VMEM_LIMIT = 62 * 1024 * 1024
 
 
 def dp_at(zh, zl, y, x):
@@ -41,116 +41,6 @@
     return pltpu.make_async_remote_copy(
         src_ref=src, dst_ref=dst, send_sem=ssem, recv_sem=rsem, device_id=d, device_id_type=MESH
     )
-
-
-def peers_of_group(zh, zl, y, x):
-    out = []
-    for kl, kx in ((0, 1), (1, 0), (1, 1)):
-        pz, px = (zl + kl) % 2, (x + kx) % 2
-        out.append((pz * 2 + px, dp_at(zh, pz, y, px)))
-    return out
-
-
-def act_gather_kernel(x_ref, out_ref, send, recv, fsend, frecv, local):
-    zh, zl, y, x, c = place()
-    q, me = zl * 2 + x, dp_at(zh, zl, y, x)
-    sib = dev(me, 1 - c)
-    peers = peers_of_group(zh, zl, y, x)
-    greet([sib] + [dev(d, c) for _, d in peers])
-    own = pltpu.make_async_copy(x_ref, out_ref.at[q, c], local)
-    own.start()
-    copies = []
-    for k, (pq, d) in enumerate(peers):
-        cp = remote(x_ref, out_ref.at[q, c], send.at[k], recv.at[q], dev(d, c))
-        cp.start()
-        copies.append(cp)
-    fwd = [remote(x_ref, out_ref.at[q, c], fsend.at[3], frecv.at[q], sib)]
-    fwd[0].start()
-    for k, (pq, d) in enumerate(peers):
-        land = out_ref.at[pq, c]
-        remote(land, land, send.at[k], recv.at[pq], dev(d, c)).wait_recv()
-        cp = remote(land, land, fsend.at[k], frecv.at[pq], sib)
-        cp.start()
-        fwd.append(cp)
-    for j in range(4):
-        land = out_ref.at[j, 1 - c]
-        remote(land, land, fsend.at[0], frecv.at[j], sib).wait_recv()
-    for cp in copies + fwd:
-        cp.wait_send()
-    own.wait()
-
-
-def act_gather(x, cid):
-    half, width = x.shape
-    return pl.pallas_call(
-        act_gather_kernel,
-        out_shape=jax.ShapeDtypeStruct((4, 2, half, width), x.dtype),
-        in_specs=[pl.BlockSpec(memory_space=pl.ANY)],
-        out_specs=pl.BlockSpec(memory_space=pl.ANY),
-        scratch_shapes=[
-            pltpu.SemaphoreType.DMA((3,)),
-            pltpu.SemaphoreType.DMA((4,)),
-            pltpu.SemaphoreType.DMA((4,)),
-            pltpu.SemaphoreType.DMA((4,)),
-            pltpu.SemaphoreType.DMA,
-        ],
-        compiler_params=pltpu.CompilerParams(collective_id=cid, has_side_effects=True),
-        name="act_gather",
-    )(x)
-
-
-def act_reduce_kernel(p_ref, out_ref, sbuf, tbuf, rbuf, ssend, srecv, send, recv):
-    zh, zl, y, x, c = place()
-    q, me = zl * 2 + x, dp_at(zh, zl, y, x)
-    sib = dev(me, 1 - c)
-    peers = peers_of_group(zh, zl, y, x)
-    greet([sib] + [dev(d, c) for _, d in peers])
-    order = [peers[2], peers[1], peers[0], (q, me)]
-    half = []
-    for k, (pq, d) in enumerate(order):
-        cp = remote(p_ref.at[pq, 1 - c], sbuf.at[pq], ssend.at[k], srecv.at[pq], sib)
-        cp.start()
-        half.append(cp)
-    out = []
-    for k, (pq, d) in enumerate(order):
-        remote(sbuf.at[pq], sbuf.at[pq], ssend.at[k], srecv.at[pq], sib).wait_recv()
-        total = p_ref[pq, c].astype(F32) + sbuf[pq].astype(F32)
-        if k < 3:
-            tbuf[k] = total.astype(BF)
-            cp = remote(tbuf.at[k], rbuf.at[q], send.at[k], recv.at[q], dev(d, c))
-            cp.start()
-            out.append(cp)
-        else:
-            out_ref[...] = total
-    for pq, d in peers:
-        remote(rbuf.at[pq], rbuf.at[pq], send.at[0], recv.at[pq], dev(d, c)).wait_recv()
-        out_ref[...] += rbuf[pq].astype(F32)
-    for cp in half + out:
-        cp.wait_send()
-
-
-def act_reduce(parts, cid):
-    _, _, half, width = parts.shape
-    vm = pl.BlockSpec(memory_space=pltpu.VMEM)
-    return pl.pallas_call(
-        act_reduce_kernel,
-        out_shape=jax.ShapeDtypeStruct((half, width), F32),
-        in_specs=[vm],
-        out_specs=vm,
-        scratch_shapes=[
-            pltpu.VMEM((4, half, width), BF),
-            pltpu.VMEM((3, half, width), BF),
-            pltpu.VMEM((4, half, width), BF),
-            pltpu.SemaphoreType.DMA((4,)),
-            pltpu.SemaphoreType.DMA((4,)),
-            pltpu.SemaphoreType.DMA((3,)),
-            pltpu.SemaphoreType.DMA((4,)),
-        ],
-        compiler_params=pltpu.CompilerParams(
-            collective_id=cid, has_side_effects=True, vmem_limit_bytes=VMEM_LIMIT
-        ),
-        name="act_reduce",
-    )(parts)
 
 
 def plane(zh, zl, y, x, high):
@@ -161,136 +51,6 @@
                 ph, pz, px = (zh + kh) % high, (zl + kl) % 2, (x + kx) % 2
                 out.append((ph, pz, px))
     return out
-
-
-def weight_gather_kernel(high, narr, picked, *refs):
-    src, dst = refs[:narr], refs[narr : 2 * narr]
-    send, recv, fsend, local = refs[2 * narr :]
-    zh, zl, y, x, c = place()
-    me = dp_at(zh, zl, y, x)
-    there = plane(zh, zl, y, x, high)
-    other = dev(dp_at(zh, zl, 1 - y, x), c)
-    greet([dev(dp_at(h, z, y, w), c) for h, z, w in there[1:]] + [other])
-    pend = []
-    for a in range(narr):
-        for k, (h, z, w) in enumerate(there):
-            piece = src[a].at[z * 2 + w] if picked[a] else src[a]
-            if k == 0:
-                cp = pltpu.make_async_copy(piece, dst[a].at[me], local.at[a])
-            else:
-                cp = remote(piece, dst[a].at[me], send.at[a, k], recv.at[a, me], dev(dp_at(h, z, y, w), c))
-            cp.start()
-            pend.append((k, cp))
-    for a in range(narr):
-        for k, (h, z, w) in enumerate(there):
-            s = dp_at(h, z, y, w)
-            land = dst[a].at[s]
-            if k == 0:
-                pend[a * len(there)][1].wait()
-            else:
-                remote(land, land, send.at[a, k], recv.at[a, s], other).wait_recv()
-            cp = remote(land, land, fsend.at[a, k], recv.at[a, s], other)
-            cp.start()
-            pend.append((1, cp))
-    for a in range(narr):
-        for k, (h, z, w) in enumerate(there):
-            s = dp_at(h, z, 1 - y, w)
-            land = dst[a].at[s]
-            remote(land, land, fsend.at[a, k], recv.at[a, s], other).wait_recv()
-    for k, cp in pend:
-        if k:
-            cp.wait_send()
-
-
-def weight_gather(arrays, picked, n, cid):
-    high = n // 8
-    narr = len(arrays)
-    shapes = tuple(
-        jax.ShapeDtypeStruct((n,) + (a.shape[1:] if p else a.shape), a.dtype) for a, p in zip(arrays, picked)
-    )
-    anyspec = pl.BlockSpec(memory_space=pl.ANY)
-    return pl.pallas_call(
-        functools.partial(weight_gather_kernel, high, narr, picked),
-        out_shape=shapes,
-        in_specs=[anyspec] * narr,
-        out_specs=[anyspec] * narr,
-        scratch_shapes=[
-            pltpu.SemaphoreType.DMA((narr, high * 4)),
-            pltpu.SemaphoreType.DMA((narr, n)),
-            pltpu.SemaphoreType.DMA((narr, high * 4)),
-            pltpu.SemaphoreType.DMA((narr,)),
-        ],
-        compiler_params=pltpu.CompilerParams(collective_id=cid, has_side_effects=True),
-        name="weight_gather",
-    )(*arrays)
-
-
-def grad_reduce_kernel(high, narr, picked, *refs):
-    src, dst = refs[:narr], refs[narr : 2 * narr]
-    ybuf, tbuf, rbuf = (refs[(2 + i) * narr : (3 + i) * narr] for i in range(3))
-    ysend, yrecv, send, recv = refs[5 * narr :]
-    zh, zl, y, x, c = place()
-    q = zl * 2 + x
-    there = plane(zh, zl, y, x, high)
-    other = dev(dp_at(zh, zl, 1 - y, x), c)
-    greet([dev(dp_at(h, z, y, w), c) for h, z, w in there[1:]] + [other])
-    mine = zh * 4 + q
-    order = there[1:] + there[:1]
-    pend = []
-    for a in range(narr):
-        for h, z, w in order:
-            j = h * 4 + z * 2 + w
-            cp = remote(src[a].at[dp_at(h, z, 1 - y, w)], ybuf[a].at[j], ysend.at[a, j], yrecv.at[a, j], other)
-            cp.start()
-            pend.append(cp)
-    for a in range(narr):
-        for k, (h, z, w) in enumerate(order):
-            j = h * 4 + z * 2 + w
-            remote(ybuf[a].at[j], ybuf[a].at[j], ysend.at[a, j], yrecv.at[a, j], other).wait_recv()
-            total = src[a][dp_at(h, z, y, w)].astype(F32) + ybuf[a][j].astype(F32)
-            if k < len(order) - 1:
-                tbuf[a][j] = total.astype(tbuf[a].dtype)
-                cp = remote(
-                    tbuf[a].at[j], rbuf[a].at[mine], send.at[a, j], recv.at[a, mine], dev(dp_at(h, z, y, w), c)
-                )
-                cp.start()
-                pend.append(cp)
-            elif picked[a]:
-                dst[a][...] = jnp.zeros(dst[a].shape, F32)
-                dst[a][q] = total
-            else:
-                dst[a][...] = total
-    for a in range(narr):
-        for h, z, w in there[1:]:
-            j = h * 4 + z * 2 + w
-            remote(rbuf[a].at[j], rbuf[a].at[j], send.at[a, j], recv.at[a, j], other).wait_recv()
-            if picked[a]:
-                dst[a][z * 2 + w] += rbuf[a][j].astype(F32)
-            else:
-                dst[a][...] += rbuf[a][j].astype(F32)
-    for cp in pend:
-        cp.wait_send()
-
-
-def grad_reduce(arrays, picked, n, cid):
-    high = n // 8
-    narr = len(arrays)
-    vm = pl.BlockSpec(memory_space=pltpu.VMEM)
-    shapes = tuple(
-        jax.ShapeDtypeStruct(((4,) if p else ()) + a.shape[1:], F32) for a, p in zip(arrays, picked)
-    )
-    bufs = [pltpu.VMEM((high * 4,) + a.shape[1:], a.dtype) for a in arrays]
-    return pl.pallas_call(
-        functools.partial(grad_reduce_kernel, high, narr, picked),
-        out_shape=shapes,
-        in_specs=[vm] * narr,
-        out_specs=[vm] * narr,
-        scratch_shapes=bufs * 3 + [pltpu.SemaphoreType.DMA((narr, high * 4))] * 4,
-        compiler_params=pltpu.CompilerParams(
-            collective_id=cid, has_side_effects=True, vmem_limit_bytes=VMEM_LIMIT
-        ),
-        name="grad_reduce",
-    )(*arrays)
 
 
 def gelu_parts(v):
@@ -348,138 +108,6 @@
     lax.fori_loop(0, blocks, step, jnp.zeros((1, width), F32))
 
 
-def rec_forward_kernel(taps, p_ref, g_ref, v_ref, e_ref, mixed_ref, conv_ref, r_ref, i_ref, state_ref, a_ref):
-    length, two = p_ref.shape[1:]
-    blk = two // 2
-    branch, conv_in = p_ref[0, :, :blk], p_ref[0, :, blk:]
-    vec = v_ref[0]
-    same = segments(e_ref[0, 0:1, :], length, blk, taps)
-    conv = conv_in * vec[4:5] + vec[4 + taps : 5 + taps]
-    for k in range(1, taps):
-        conv = conv + pltpu.roll(conv_in, k, 0) * same[k - 1] * vec[4 + k : 5 + k]
-    pre = jnp.dot(conv.astype(BF), g_ref[0], preferred_element_type=F32)
-    r = jax.nn.sigmoid(pre[:, :blk] + vec[0:1])
-    gate = jax.nn.sigmoid(pre[:, blk:] + vec[1:2])
-    log_a = (-DECAY * r) * vec[2:3]
-    a = jnp.exp(log_a)
-    start = same[0] == 0.0
-    a_eff = jnp.where(start, 0.0, a)
-    mult = jnp.where(start, 1.0, jnp.sqrt(-jnp.tanh(log_a) * (1.0 + a * a)))
-    full_scan(a_eff, mult * gate * conv, state_ref.at[0], a_ref, False)
-    act, _ = gelu_parts(branch)
-    mixed_ref[0] = (state_ref[0] * act).astype(BF)
-    conv_ref[0] = conv
-    r_ref[0] = r
-    i_ref[0] = gate
-
-
-def rec_backward_kernel(
-    taps, p_ref, g_ref, v_ref, e_ref, conv_ref, r_ref, i_ref, state_ref, m_ref,
-    low_ref, gg_ref, vg_ref, carry_ref, a_ref,
-):
-    unit = pl.program_id(0)
-    length, two = p_ref.shape[1:]
-    blk = two // 2
-    branch, conv_in = p_ref[0, :, :blk], p_ref[0, :, blk:]
-    vec = v_ref[0]
-    same = segments(e_ref[0, 0:1, :], length, blk, taps)
-    start = same[0] == 0.0
-    r, gate, conv, state, mg = r_ref[0], i_ref[0], conv_ref[0], state_ref[0], m_ref[0]
-    act, der = gelu_parts(branch)
-    low_ref[0, :, :blk] = (mg * state * der).astype(BF)
-    log_a = (-DECAY * r) * vec[2:3]
-    a = jnp.exp(log_a)
-    a_eff = jnp.where(start, 0.0, a)
-    row = lax.broadcasted_iota(jnp.int32, (length, blk), 0)
-    a_next = jnp.where(row < length - 1, pltpu.roll(a_eff, length - 1, 0), 0.0)
-    full_scan(a_next, mg * act, carry_ref, a_ref, True)
-    carry = carry_ref[...]
-    prev = jnp.where(row > 0, pltpu.roll(state, 1, 0), 0.0)
-    raw = jnp.sqrt(-jnp.tanh(log_a) * (1.0 + a * a))
-    mult = jnp.where(start, 1.0, raw)
-    log_grad = jnp.where(start, 0.0, carry * prev * a - carry * gate * conv * (a * a) / raw)
-    r_grad = log_grad * (-DECAY * vec[2:3]) * (r * (1.0 - r))
-    i_grad = carry * mult * conv * (gate * (1.0 - gate))
-    pre_low = jnp.concatenate([r_grad.astype(BF), i_grad.astype(BF)], axis=1)
-    conv_grad = carry * mult * gate + lax.dot_general(
-        pre_low, g_ref[0], (((1,), (1,)), ((), ())), preferred_element_type=F32
-    )
-    gg = lax.dot_general(conv.astype(BF), pre_low, (((0,), (0,)), ((), ())), preferred_element_type=F32)
-
-    def total(v):
-        return jnp.sum(v, axis=0, keepdims=True)
-
-    rows = [total(r_grad), total(i_grad), total(log_grad * (DECAY * r) * vec[3:4]), total(conv_grad)]
-    inp = conv_grad * vec[4:5]
-    rows.append(total(conv_grad * conv_in))
-    for k in range(1, taps):
-        masked = conv_grad * same[k - 1]
-        rows.append(total(masked * pltpu.roll(conv_in, k, 0)))
-        inp = inp + pltpu.roll(masked, length - k, 0) * vec[4 + k : 5 + k]
-    low_ref[0, :, blk:] = inp.astype(BF)
-    vg = jnp.concatenate(rows, axis=0)
-
-    @pl.when((unit == 0) | (unit == 4))
-    def _():
-        gg_ref[0] = gg
-        vg_ref[0] = vg
-
-    @pl.when((unit != 0) & (unit != 4))
-    def _():
-        gg_ref[0] += gg
-        vg_ref[0] += vg
-
-
-def unit_spec(a):
-    return pl.BlockSpec((1,) + a.shape[1:], lambda u: (u, 0, 0))
-
-
-def head_spec(a):
-    return pl.BlockSpec((1,) + a.shape[1:], lambda u: (u // 4, 0, 0))
-
-
-def rec_forward(taps, pre, gates, vec, ends):
-    units, length, two = pre.shape
-    blk = two // 2
-    block = pl.BlockSpec((1, length, blk), lambda u: (u, 0, 0))
-    f32 = jax.ShapeDtypeStruct((units, length, blk), F32)
-    return pl.pallas_call(
-        functools.partial(rec_forward_kernel, taps),
-        grid=(units,),
-        out_shape=(jax.ShapeDtypeStruct((units, length, blk), BF), f32, f32, f32, f32),
-        in_specs=[unit_spec(pre), head_spec(gates), head_spec(vec), unit_spec(ends)],
-        out_specs=[block] * 5,
-        scratch_shapes=[pltpu.VMEM((length, blk), F32)],
-        compiler_params=pltpu.CompilerParams(vmem_limit_bytes=VMEM_LIMIT),
-        name="rec_forward",
-    )(pre, gates, vec, ends)
-
-
-def rec_backward(taps, pre, gates, vec, ends, conv, r, gate, state, mixed_grad):
-    units, length, two = pre.shape
-    blk = two // 2
-    vrows = 4 + taps
-    return pl.pallas_call(
-        functools.partial(rec_backward_kernel, taps),
-        grid=(units,),
-        out_shape=(
-            jax.ShapeDtypeStruct((units, length, two), BF),
-            jax.ShapeDtypeStruct((2, blk, two), F32),
-            jax.ShapeDtypeStruct((2, vrows, blk), F32),
-        ),
-        in_specs=[unit_spec(pre), head_spec(gates), head_spec(vec), unit_spec(ends)]
-        + [unit_spec(conv)] * 5,
-        out_specs=[
-            unit_spec(pre),
-            pl.BlockSpec((1, blk, two), lambda u: (u // 4, 0, 0)),
-            pl.BlockSpec((1, vrows, blk), lambda u: (u // 4, 0, 0)),
-        ],
-        scratch_shapes=[pltpu.VMEM((length, blk), F32)] * 2,
-        compiler_params=pltpu.CompilerParams(vmem_limit_bytes=VMEM_LIMIT),
-        name="rec_backward",
-    )(pre, gates, vec, ends, conv, r, gate, state, mixed_grad)
-
-
 class Gather:
     def __init__(self, slot, parts, sems, here, there, core):
         self.slot, self.parts, (self.send, self.recv, self.fsend) = slot, parts, sems
@@ -608,6 +236,22 @@
         remote(land, land, self.send.at[k], self.recv.at[pq], r.sib).wait_recv()
         return self.got[pq].astype(F32)
 
+    def ready(self):
+        r = self.rows
+        land = self.sib_buf.at[r.q]
+        remote(land, land, self.ssend.at[0], self.srecv.at[r.q], r.sib).wait_recv()
+        for k in (1, 2, 3):
+            pq, _ = r.at(k)
+            land = self.got.at[pq]
+            remote(land, land, self.send.at[k], self.recv.at[pq], r.sib).wait_recv()
+
+    def own(self, at):
+        r = self.rows
+        total = self.part[r.q, r.core, at].astype(F32) + self.sib_buf[r.q, at].astype(F32)
+        for k in (1, 2, 3):
+            total = total + self.got[r.at(k)[0], at].astype(F32)
+        return total
+
     def finish(self):
         r = self.rows
         land = self.got.at[r.q]
@@ -618,14 +262,7 @@
 
 
 def rec_unit(taps, branch, conv_in, vec, gates, ends, state_ref, a_ref):
-    length, blk = branch.shape
-    same = segments(ends, length, blk, taps)
-    conv = conv_in * vec[4:5] + vec[4 + taps : 5 + taps]
-    for k in range(1, taps):
-        conv = conv + pltpu.roll(conv_in, k, 0) * same[k - 1] * vec[4 + k : 5 + k]
-    pre = jnp.dot(conv.astype(BF), gates, preferred_element_type=F32)
-    r = jax.nn.sigmoid(pre[:, :blk] + vec[0:1])
-    gate = jax.nn.sigmoid(pre[:, blk:] + vec[1:2])
+    same, conv, r, gate = rec_gates(taps, conv_in, vec, gates, ends)
     log_a = (-DECAY * r) * vec[2:3]
     a = jnp.exp(log_a)
     start = same[0] == 0.0
@@ -633,7 +270,7 @@
     mult = jnp.where(start, 1.0, jnp.sqrt(-jnp.tanh(log_a) * (1.0 + a * a)))
     full_scan(a_eff, mult * gate * conv, state_ref, a_ref, False)
     act, _ = gelu_parts(branch)
-    return conv, r, gate, (state_ref[...] * act).astype(BF)
+    return (state_ref[...] * act).astype(BF)
 
 
 SMALL_ROWS = 96
@@ -641,9 +278,9 @@
 
 def forward_kernel(n, taps, heads, *refs):
     (tok, cot, wb, wi, wo, wg, wu, wd, wr, wig, small) = refs[:11]
-    (o_rec, o_mlp, o_gate, o_vec, o_gain, o_ends, o_u, o_grad, pre, conv, rate, gate, state, mixed, resid, o_norm) = refs[11:27]
-    (rec, gat, sml, u_buf, og, part, sibb, got, extra, a_scr, gfull) = refs[27:38]
-    sems = refs[38:]
+    (o_rec, o_mlp, o_gate, o_vec, o_gain, o_ends, o_u, o_grad, pre, state, mixed, resid, o_norm) = refs[11:24]
+    (rec, gat, sml, u_buf, og, part, sibb, got, extra, a_scr, gfull) = refs[24:35]
+    sems = refs[35:]
     g_sems, r1, r2, s1, (fin, h_send, h_recv) = sems[:48], sems[48:52], sems[52:56], sems[56:60], sems[60:]
     zh, zl, y, x, c = place()
     here = (zh, zl, y, x)
@@ -807,10 +444,10 @@
         for j in range(2):
             w = rec[h, j].reshape(width, blk)
             pre[at, :, j * blk : (j + 1) * blk] = mm(rows, w)
-        cv, rt, gt, mx = rec_unit(
+        mx = rec_unit(
             taps, pre[at, :, :blk], pre[at, :, blk:], o_vec[h], o_gate[h], o_ends[pq][0:1, :], state.at[at], a_scr
         )
-        conv[at], rate[at], gate[at], mixed[at] = cv, rt, gt, mx
+        mixed[at] = mx
         per = 512 // rr if rr <= 512 else 1
 
         def cols_out(t, carry):
@@ -901,9 +538,6 @@
         (sds(4, 2, half, width, t=BF), hb),
         (sds(4, 2, half, width, t=BF), hb),
         (sds(5, length, 2 * blk), vm),
-        (unit, vm),
-        (unit, vm),
-        (unit, vm),
         (unit, vm),
         (sds(5, length, blk, t=BF), vm),
         (sds(half, width), vm),
@@ -983,9 +617,9 @@
             up = mm(a, w[tiles + t].reshape(width, blk))
             grad = mm(mg[pq].reshape(2 * half, width), w[2 * tiles + t].reshape(width, blk))
             act, der = gelu_parts(gate)
-            o_hid[pq, t] = (act * up).astype(BF)
-            hg[pq, t] = (grad * up * der).astype(BF)
-            hu[pq, t] = (grad * act).astype(BF)
+            o_hid[t, pq] = (act * up).astype(BF)
+            hg[t, pq] = (grad * up * der).astype(BF)
+            hu[t, pq] = (grad * act).astype(BF)
             return carry
 
         lax.fori_loop(0, tiles, first, 0)
@@ -1001,8 +635,8 @@
         def second(d, carry):
             total = jnp.zeros((2 * half, blk), F32)
             for t in range(tiles):
-                total = total + mm_t(hg[pq, t], w[t, pl.ds(d * per, per)].reshape(blk, blk))
-                total = total + mm_t(hu[pq, t], w[tiles + t, pl.ds(d * per, per)].reshape(blk, blk))
+                total = total + mm_t(hg[t, pq], w[t, pl.ds(d * per, per)].reshape(blk, blk))
+                total = total + mm_t(hu[t, pq], w[tiles + t, pl.ds(d * per, per)].reshape(blk, blk))
             lanes = pl.ds(pl.multiple_of(d * blk, 128), blk)
             part[pq, 0, :, lanes] = total[:half].astype(BF)
             part[pq, 1, :, lanes] = total[half:].astype(BF)
@@ -1028,26 +662,30 @@
         mt_ = mg[:, :, :, lanes].reshape(8 * half, blk).T
         for i, (left, right) in enumerate(((nt_, hg), (nt_, hu), (mt_, o_hid))):
             for t in range(tiles):
-                tile = mm(left, right[:, t].reshape(8 * half, blk))
+                tile = mm(left, right[t].reshape(8 * half, blk))
                 gbuf[i * tiles + t, pl.ds(d * per, per)] = tile.astype(BF).reshape(per, rr, blk)
         out_tile(d).start()
         return carry
 
     lax.fori_loop(0, steps, grads, 0)
-    total = sums.pair(0)
-    for k in (1, 2, 3):
-        total = total + sums.take(k)
-    r = resid[...]
-    scale = lax.rsqrt(jnp.mean(r * r, axis=-1, keepdims=True) + EPS)
-    unit = r * scale
-    o_gain[...] = jnp.broadcast_to(jnp.sum(total * unit, axis=0, keepdims=True), o_gain.shape)
-    g2 = total * gain[1:2, :]
-    back = scale * (g2 - unit * jnp.mean(g2 * unit, axis=-1, keepdims=True))
+    sums.ready()
     e3 = ends[q][0:1, 3:4]
-    spot = lax.broadcasted_iota(jnp.int32, (half, 1), 0).astype(F32) + (c * half).astype(F32)
-    back = back + jnp.where(spot < e3, cot[...], 0.0)
-    o_rgrad[...] = back
-    o_rec[...] = back.astype(BF)
+
+    def finish(i, acc):
+        at = pl.ds(pl.multiple_of(i * 32, 32), 32)
+        total, r = sums.own(at), resid[at, :]
+        scale = lax.rsqrt(jnp.mean(r * r, axis=-1, keepdims=True) + EPS)
+        unit = r * scale
+        g2 = total * gain[1:2, :]
+        back = scale * (g2 - unit * jnp.mean(g2 * unit, axis=-1, keepdims=True))
+        spot = lax.broadcasted_iota(jnp.int32, (32, 1), 0) + (c * half + i * 32)
+        back = back + jnp.where(spot.astype(F32) < e3, cot[at, :], 0.0)
+        o_rgrad[at, :] = back
+        o_rec[at, :] = back.astype(BF)
+        return acc + jnp.sum(total * unit, axis=0, keepdims=True)
+
+    gsum = lax.fori_loop(0, half // 32, finish, jnp.zeros((1, width), F32))
+    o_gain[...] = jnp.broadcast_to(gsum, o_gain.shape)
     for d in range(steps):
         out_tile(d).wait()
     rows.finish()
@@ -1060,7 +698,7 @@
     tiles = nt // 3
     vm = pl.BlockSpec(memory_space=pltpu.VMEM)
     hb = pl.BlockSpec(memory_space=pl.ANY)
-    hid = (4, tiles, 2 * half, blk)
+    hid = (tiles, 4, 2 * half, blk)
     return pl.pallas_call(
         mlp_kernel,
         out_shape=(
@@ -1094,6 +732,478 @@
     )(norm, resid, gain, cot, ends, mlp_w, mlp_grad)
 
 
+class Scatter:
+    def __init__(self, away, mine, pair, landed, sems, here, there, core):
+        self.away, self.mine, self.pair, self.landed = away, mine, pair, landed
+        self.ysend, self.yrecv, self.send, self.recv = sems
+        zh, zl, y, x = here
+        self.core = core
+        self.own = zh * 4 + zl * 2 + x
+        self.places = [
+            (h * 4 + z * 2 + w, dp_at(h, z, y, w), dp_at(h, z, 1 - y, w)) for h, z, w in (*there[1:], there[0])
+        ]
+        self.other = dev(dp_at(zh, zl, 1 - y, x), core)
+
+    def start(self):
+        for j, _, far in self.places:
+            remote(self.away(far), self.pair(j), self.ysend.at[j], self.yrecv.at[j], self.other).start()
+
+    def pass_on(self):
+        last = len(self.places) - 1
+        for i, (j, near, _) in enumerate(self.places):
+            slot = self.pair(j)
+            remote(slot, slot, self.ysend.at[j], self.yrecv.at[j], self.other).wait_recv()
+            slot[...] = (self.mine(near).astype(F32) + slot[...].astype(F32)).astype(slot.dtype)
+            if i == last:
+                pltpu.make_async_copy(slot, self.landed(self.own), self.send.at[j]).start()
+            else:
+                remote(
+                    slot, self.landed(self.own), self.send.at[j], self.recv.at[self.own], dev(near, self.core)
+                ).start()
+
+    def collect(self):
+        last = len(self.places) - 1
+        for i, (j, _, _) in enumerate(self.places):
+            slot, land = self.pair(j), self.landed(j)
+            remote(slot, slot, self.ysend.at[j], self.yrecv.at[j], self.other).wait_send()
+            if i == last:
+                pltpu.make_async_copy(land, land, self.send.at[j]).wait()
+            else:
+                remote(land, land, self.send.at[j], self.recv.at[j], self.other).wait_recv()
+                remote(slot, slot, self.send.at[j], self.recv.at[j], self.other).wait_send()
+
+
+def scatter_sems(high):
+    return [pltpu.SemaphoreType.DMA((high * 4,))] * 4
+
+
+def rec_gates(taps, conv_in, vec, gates, ends):
+    length, blk = conv_in.shape
+    same = segments(ends, length, blk, taps)
+    conv = conv_in * vec[4:5] + vec[4 + taps : 5 + taps]
+    for k in range(1, taps):
+        conv = conv + pltpu.roll(conv_in, k, 0) * same[k - 1] * vec[4 + k : 5 + k]
+    pre = jnp.dot(conv.astype(BF), gates, preferred_element_type=F32)
+    r = jax.nn.sigmoid(pre[:, :blk] + vec[0:1])
+    gate = jax.nn.sigmoid(pre[:, blk:] + vec[1:2])
+    return same, conv, r, gate
+
+
+def rec_unit_back(taps, branch, conv_in, vec, gates, ends, state, mg, carry_ref, a_ref):
+    length, blk = branch.shape
+    same, conv, r, gate = rec_gates(taps, conv_in, vec, gates, ends)
+    start = same[0] == 0.0
+    act, der = gelu_parts(branch)
+    branch_low = (mg * state * der).astype(BF)
+    log_a = (-DECAY * r) * vec[2:3]
+    a = jnp.exp(log_a)
+    a_eff = jnp.where(start, 0.0, a)
+    row = lax.broadcasted_iota(jnp.int32, (length, blk), 0)
+    a_next = jnp.where(row < length - 1, pltpu.roll(a_eff, length - 1, 0), 0.0)
+    full_scan(a_next, mg * act, carry_ref, a_ref, True)
+    carry = carry_ref[...]
+    prev = jnp.where(row > 0, pltpu.roll(state, 1, 0), 0.0)
+    raw = jnp.sqrt(-jnp.tanh(log_a) * (1.0 + a * a))
+    mult = jnp.where(start, 1.0, raw)
+    log_grad = jnp.where(start, 0.0, carry * prev * a - carry * gate * conv * (a * a) / raw)
+    r_grad = log_grad * (-DECAY * vec[2:3]) * (r * (1.0 - r))
+    i_grad = carry * mult * conv * (gate * (1.0 - gate))
+    pre_low = jnp.concatenate([r_grad.astype(BF), i_grad.astype(BF)], axis=1)
+    conv_grad = carry * mult * gate + mm_t(pre_low, gates)
+    gate_grads = t_mm(conv.astype(BF), pre_low)
+
+    def total(v):
+        return jnp.sum(v, axis=0, keepdims=True)
+
+    sums = [total(r_grad), total(i_grad), total(log_grad * (DECAY * r) * vec[3:4]), total(conv_grad)]
+    inp = conv_grad * vec[4:5]
+    sums.append(total(conv_grad * conv_in))
+    for k in range(1, taps):
+        masked = conv_grad * same[k - 1]
+        sums.append(total(masked * pltpu.roll(conv_in, k, 0)))
+        inp = inp + pltpu.roll(masked, length - k, 0) * vec[4 + k : 5 + k]
+    return branch_low, inp.astype(BF), gate_grads, jnp.concatenate(sums, axis=0)
+
+
+def backward_kernel(n, taps, *refs):
+    (tok, rgrad, resid, gain, gsum2, ends, vec, gates, pre, state, mixed) = refs[:11]
+    (rec_own, hid, g_hbm, rec_hbm, mlp_hbm, u_hbm) = refs[11:17]
+    (o_res, o_tok, l_mlp, l_rec, l_sh, l_gate, l_small) = refs[17:24]
+    (rec, ub, rg, part, sib1, got1, sib2, got2, low, grec, gsh, gshin, g_own, y_mlp, y_rec, y_sh, a_scr, c_scr,
+     gg, vg, ggl, y_gate, sml, sml_sib, y_sml) = refs[24:49]
+    sems = refs[49:]
+    zh, zl, y, x, c = place()
+    here = (zh, zl, y, x)
+    q, me = zl * 2 + x, dp_at(zh, zl, y, x)
+    high = n // 8
+    there = plane(zh, zl, y, x, high)
+    half, width = tok.shape
+    length = 2 * half
+    blk = mixed.shape[2]
+    rr = width // n
+    rb = blk // n
+    nt = y_mlp.shape[0]
+    per, steps = blk // rr, width // blk
+    taken = [0]
+
+    def some(k):
+        taken[0] += k
+        return sems[taken[0] - k : taken[0]]
+
+    rows = Rows(rg, some(4), here, c)
+    sums1 = Sums(part, sib1, got1, some(4), rows)
+    sums2 = Sums(part, sib2, got2, some(4), rows)
+    (loads,) = some(1)
+    greet(
+        [dev(dp_at(h, z, y, w), c) for h, z, w in there[1:]]
+        + [dev(dp_at(zh, zl, 1 - y, x), c), dev(me, 1 - c)]
+    )
+    first = pltpu.make_async_copy(rec_own, rg.at[q, c], loads.at[0])
+    first.start()
+    first.wait()
+    rows.start()
+    grab = [
+        pltpu.make_async_copy(rec_hbm, rec, loads.at[0]),
+        pltpu.make_async_copy(u_hbm, ub, loads.at[1]),
+    ]
+    for cp in grab:
+        cp.start()
+
+    def own_part(i):
+        return pltpu.make_async_copy(g_hbm.at[i, :, y], g_own.at[i % 2], loads.at[2 + i % 2])
+
+    own_part(0).start()
+
+    def reduce_chunk(i):
+        own_part(i).wait()
+        if i + 1 < nt:
+            own_part(i + 1).start()
+        mlps[i].pass_on()
+
+    def chunk(i, sem):
+        return Scatter(
+            lambda s: g_hbm.at[i, s // 4, (s // 2) % 2, s % 2],
+            lambda s: g_own[i % 2, s // 4, s % 2],
+            lambda j: y_mlp.at[i, j],
+            lambda j: l_mlp.at[i, j],
+            sem, here, there, c,
+        )
+
+    mlps = [chunk(i, some(4)) for i in range(nt)]
+    for a in mlps:
+        a.start()
+    recs = [
+        Scatter(
+            lambda s, i=i: grec.at[i, s],
+            lambda s, i=i: grec[i, s],
+            lambda j, i=i: y_rec.at[i, j],
+            lambda j, i=i: l_rec.at[i, j],
+            some(4), here, there, c,
+        )
+        for i in range(3)
+    ]
+    part_rows = rr // 2
+
+    def region(ref, h):
+        return ref.at[:, :, pl.ds(pl.multiple_of(h * part_rows, 8), part_rows), :]
+
+    shared = Scatter(
+        lambda s: gshin.at[:, s],
+        lambda s: gshin[:, s],
+        lambda j: y_sh.at[j],
+        lambda j: l_sh.at[j],
+        some(4), here, there, c,
+    )
+    gate_sc = Scatter(
+        lambda s: ggl.at[:, s],
+        lambda s: ggl[:, s],
+        lambda j: y_gate.at[j],
+        lambda j: l_gate.at[j],
+        some(4), here, there, c,
+    )
+    h_send, h_recv, s_send, s_recv, z_send, z_recv, m_send, m_recv = some(8)
+    gg[...] = jnp.zeros_like(gg)
+    vg[...] = jnp.zeros_like(vg)
+    grab[0].wait()
+
+    def step(i, carry):
+        h = jnp.where(i == 1, 1, 0)
+        k = jnp.maximum(i - 1, 0)
+        pq, _ = rows.at(k)
+        at = pq + h * (4 - pq)
+
+        @pl.when(i != 1)
+        def _():
+            rows.arrive(k)
+
+        mg = mm(rg[pq].reshape(length, width), rec[h, 2].reshape(width, blk))
+
+        @pl.when((i > 0) & (i < 4))
+        def _():
+            rows.forward(k + 1)
+
+        b_low, i_low, g_add, v_add = rec_unit_back(
+            taps, pre[at, :, :blk], pre[at, :, blk:], vec[h], gates[h], ends[pq][0:1, :], state[at], mg, c_scr, a_scr,
+        )
+        low[at, :, :blk], low[at, :, blk:] = b_low, i_low
+        gg[h] += g_add
+        vg[h] += v_add
+
+        @pl.when(i > 2)
+        def _():
+            sums1.pass_on(k - 1)
+
+        def cols_out(t, carry):
+            cut = pl.ds(t * per, per)
+            lanes = pl.ds(pl.multiple_of(t * blk, 128), blk)
+
+            def tile_of(left, head):
+                return sum(
+                    mm_t(left[:, j * blk : (j + 1) * blk], rec[head, j, cut].reshape(blk, blk)) for j in range(2)
+                )
+
+            def emit(tile):
+                part[pq, 0, :, lanes] = tile[:half].astype(BF)
+                part[pq, 1, :, lanes] = tile[half:].astype(BF)
+
+            @pl.when(i == 1)
+            def _():
+                emit(tile_of(low[4], 1) + tile_of(low[pq], 0))
+
+            @pl.when(i > 1)
+            def _():
+                emit(tile_of(low[pq], 0))
+
+            return carry
+
+        @pl.when(i > 0)
+        def _():
+            lax.fori_loop(0, steps, cols_out, 0)
+
+        @pl.when(i > 0)
+        def _():
+            sums1.push(k)
+
+        for j in range(5):
+
+            @pl.when(i == j)
+            def _():
+                reduce_chunk(j)
+
+        return carry
+
+    lax.fori_loop(0, 5, step, 0)
+    sums1.pass_on(3)
+    grab[1].wait()
+
+    def grads(d, carry):
+        lanes = pl.ds(pl.multiple_of(d * blk, 128), blk)
+        at = pl.ds(d * per, per)
+        ut = ub[:, :, :, lanes].reshape(4 * length, blk).T
+        rt = rg[:, :, :, lanes].reshape(4 * length, blk).T
+        uo = ub[q, :, :, lanes].reshape(length, blk).T
+        ro = rg[q, :, :, lanes].reshape(length, blk).T
+        for i in range(3):
+            if i < 2:
+                right = low[0:4, :, i * blk : (i + 1) * blk].reshape(4 * length, blk)
+                own = low[4, :, i * blk : (i + 1) * blk]
+            else:
+                right, own = mixed[0:4].reshape(4 * length, blk), mixed[4]
+            grec[i, at] = mm(ut if i < 2 else rt, right).astype(BF).reshape(per, rr, blk)
+            gsh[i, at] = mm(uo if i < 2 else ro, own).astype(BF).reshape(per, rr, blk)
+        return carry
+
+    lax.fori_loop(0, steps, grads, 0)
+    _, beside = rows.at(1)
+    exchange = remote(region(gsh, 1 - x), gshin, h_send, h_recv, beside)
+    exchange.start()
+    for a in recs:
+        a.start()
+    for h in range(2):
+        for s in range(n):
+            ggl[h, s] = gg[h, s * rb : (s + 1) * rb, :].astype(BF)
+    gate_sc.start()
+
+    sums1.ready()
+
+    def finish(i, acc):
+        at = pl.ds(pl.multiple_of(i * 32, 32), 32)
+        total, xin = sums1.own(at), tok[at, :].astype(F32)
+        scale = lax.rsqrt(jnp.mean(xin * xin, axis=-1, keepdims=True) + EPS)
+        unit = xin * scale
+        g1 = total * gain[0:1, :]
+        o_tok[at, :] = rgrad[at, :] + scale * (g1 - unit * jnp.mean(g1 * unit, axis=-1, keepdims=True))
+        return acc + jnp.sum(total * unit, axis=0, keepdims=True)
+
+    gsum1 = lax.fori_loop(0, half // 32, finish, jnp.zeros((1, width), F32))
+    sums1.finish()
+    for h in range(2):
+        sml[8 * h : 8 * h + 8, :] = vg[h]
+    for i in range(steps):
+        sml[16 + i : 17 + i, :] = gsum1[:, i * blk : (i + 1) * blk]
+        sml[16 + steps + i : 17 + steps + i, :] = gsum2[0:1, i * blk : (i + 1) * blk]
+    gain_rows = sml.at[pl.ds(16, 2 * steps)]
+    with_sib = remote(gain_rows, sml_sib, s_send, s_recv, rows.sib)
+    with_sib.start()
+    reduce_chunk(5)
+    exchange.wait()
+    for s in range(n):
+        gshin[:, s] = (
+            gshin[:, s].astype(F32)
+            + gsh[:, s, pl.ds(pl.multiple_of(x * part_rows, 8), part_rows), :].astype(F32)
+        ).astype(BF)
+    shared.start()
+    reduce_chunk(6)
+    with_sib.wait()
+    sml[16 : 16 + 2 * steps, :] += sml_sib[...]
+    with_y = remote(sml, y_sml, z_send, z_recv, dev(dp_at(zh, zl, 1 - y, x), c))
+    with_y.start()
+
+    fetch = pltpu.make_async_copy(mlp_hbm.at[pl.ds(2 * (nt // 3), nt // 3)], rec.at[0], loads.at[0])
+    fetch.start()
+    per_row = length // rr
+    fetch_hid = pltpu.make_async_copy(hid, gsh.at[:, pl.ds(0, 4 * per_row)], loads.at[1])
+    fetch_hid.start()
+    reduce_chunk(7)
+    fetch.wait()
+    fetch_hid.wait()
+
+    def out_rows(i, carry):
+        k = (i + 1) % 4
+        pq, _ = rows.at(k)
+
+        def cols_out(d, carry):
+            tile = jnp.zeros((length, blk), F32)
+            for t in range(nt // 3):
+                left = gsh[t, pl.ds(pq * per_row, per_row)].reshape(length, blk)
+                tile = tile + mm_t(left, rec[0, t, pl.ds(d * per, per)].reshape(blk, blk))
+            lanes = pl.ds(pl.multiple_of(d * blk, 128), blk)
+            part[pq, 0, :, lanes] = tile[:half].astype(BF)
+            part[pq, 1, :, lanes] = tile[half:].astype(BF)
+            return carry
+
+        lax.fori_loop(0, steps, cols_out, 0)
+        sums2.push(k)
+
+        @pl.when(i > 0)
+        def _():
+            sums2.pass_on(i)
+
+        return carry
+
+    lax.fori_loop(0, 4, out_rows, 0)
+    reduce_chunk(8)
+    with_y.wait()
+    sml[...] = sml[...] + y_sml[...]
+    mine = zh * 4 + q
+    small_out = []
+    for i, (h, z, w) in enumerate(there):
+        if i == 0:
+            cp = pltpu.make_async_copy(sml, l_small.at[mine], m_send.at[i])
+        else:
+            cp = remote(sml, l_small.at[mine], m_send.at[i], m_recv.at[mine], dev(dp_at(h, z, y, w), c))
+        cp.start()
+        small_out.append(cp)
+    for a in recs:
+        a.pass_on()
+    gate_sc.pass_on()
+    shared.pass_on()
+    sums2.ready()
+    e3 = ends[q][0:1, 3:4]
+
+    def result(i, carry):
+        at = pl.ds(pl.multiple_of(i * 32, 32), 32)
+        spot = lax.broadcasted_iota(jnp.int32, (32, 1), 0) + (c * half + i * 32)
+        o_res[at, :] = jnp.where(spot.astype(F32) < e3, resid[at, :] + sums2.own(at), 0.0).astype(BF)
+        return carry
+
+    lax.fori_loop(0, half // 32, result, 0)
+    sums2.finish()
+    rows.finish()
+    for a in mlps + recs + [gate_sc, shared]:
+        a.collect()
+    for i, (h, z, w) in enumerate(there):
+        if i == 0:
+            small_out[i].wait()
+        else:
+            j = h * 4 + z * 2 + w
+            land = l_small.at[j]
+            remote(land, land, m_send.at[i], m_recv.at[j], rows.sib).wait_recv()
+            small_out[i].wait_send()
+
+
+def backward(tok, rec_own, rgrad, resid, gain, gsum2, ends, vec, gates, saved, hid, g_mlp, rec_w, mlp_w, u, n, taps, cid):
+    half, width = tok.shape
+    pre, state, mixed = saved
+    blk = mixed.shape[2]
+    length = 2 * half
+    rr, rb, high = width // n, blk // n, n // 8
+    nt = g_mlp.shape[0]
+    slots = high * 4
+    vm = pl.BlockSpec(memory_space=pltpu.VMEM)
+    hb = pl.BlockSpec(memory_space=pl.ANY)
+    g_view = g_mlp.reshape(nt, n // 4, 2, 2, rr, blk)
+    hid = hid.reshape(nt // 3, 4 * length // rr, rr, blk)
+    small_rows = 16 + 2 * (width // blk)
+
+    def sds(*shape, t=BF):
+        return jax.ShapeDtypeStruct(shape, t)
+
+    def v(*shape, t=BF):
+        return pltpu.VMEM(shape, t)
+
+    dma = pltpu.SemaphoreType.DMA
+    return pl.pallas_call(
+        functools.partial(backward_kernel, n, taps),
+        out_shape=(
+            sds(half, width),
+            sds(half, width, t=F32),
+            sds(nt, slots, rr, blk),
+            sds(3, slots, rr, blk),
+            sds(slots, 3, rr // 2, blk),
+            sds(slots, 2, rb, 2 * blk),
+            sds(slots, small_rows, blk, t=F32),
+        ),
+        in_specs=[vm] * 11 + [hb] * 6,
+        out_specs=[vm, vm] + [hb] * 5,
+        scratch_shapes=[
+            v(2, 3, n, rr, blk),
+            v(4, 2, half, width),
+            v(4, 2, half, width),
+            v(4, 2, half, width),
+            v(4, half, width),
+            v(4, half, width),
+            v(4, half, width),
+            v(4, half, width),
+            v(5, length, 2 * blk),
+            v(3, n, rr, blk),
+            v(3, n, rr, blk),
+            v(3, n, rr // 2, blk),
+            v(2, n // 4, 2, rr, blk),
+            v(nt, slots, rr, blk),
+            v(3, slots, rr, blk),
+            v(slots, 3, rr // 2, blk),
+            v(length, blk, t=F32),
+            v(length, blk, t=F32),
+            v(2, blk, 2 * blk, t=F32),
+            v(2, 4 + taps, blk, t=F32),
+            v(2, n, rb, 2 * blk),
+            v(slots, 2, rb, 2 * blk),
+            v(small_rows, blk, t=F32),
+            v(small_rows - 16, blk, t=F32),
+            v(small_rows, blk, t=F32),
+        ]
+        + row_sems() * 3
+        + [dma((4,))]
+        + scatter_sems(high) * (nt + 5)
+        + [dma, dma, dma, dma, dma, dma, dma((slots,)), dma((slots,))],
+        compiler_params=pltpu.CompilerParams(
+            collective_id=cid, has_side_effects=True, vmem_limit_bytes=VMEM_LIMIT
+        ),
+        name="backward",
+    )(tok, rgrad, resid, gain, gsum2, ends, vec, gates, *saved, rec_own, hid, g_view, rec_w, mlp_w, u)
+
+
 def mm(a, b):
     return jnp.dot(a, b, preferred_element_type=F32)
 
@@ -1104,18 +1214,6 @@
 
 def t_mm(a, b):
     return lax.dot_general(a, b, (((0,), (0,)), ((), ())), preferred_element_type=F32)
-
-
-def gelu_tanh(values):
-    return jax.nn.gelu(values, approximate=True)
-
-
-def norm_scale(values):
-    return lax.rsqrt(jnp.mean(values * values, axis=-1, keepdims=True) + EPS)
-
-
-def norm_back(grad, unit, inverse):
-    return inverse * (grad - unit * jnp.mean(grad * unit, axis=-1, keepdims=True))
 
 
 def local(
@@ -1152,110 +1250,55 @@
     ends_own = jnp.pad(jnp.stack([e0, e1, e2, e3]).astype(BF)[None], ((0, 13), (0, 124)))
     small = jnp.concatenate([lanes(params, rb), lanes(jnp.stack([rec_gain, mlp_gain]), rows), ends_own], axis=0)
     (
-        rec_w, mlp_w, gates, vec, gains_all, group_ends, u, mlp_grad, pre, conv, rate, gate, state, mixed, resid, norm_own,
+        rec_w, mlp_w, gates, vec, gains_all, group_ends, u, mlp_grad, pre, state, mixed, resid, norm_own,
     ) = forward(
         tokens[0], cotangent[0], w_branch, w_input, w_output.T, w_gate, w_up, w_down.T, w_rgate, w_igate, small, n, taps, 1,
     )
-    rec_w = rec_w.reshape(2, 3, width, blk)
-    recq, rec4 = (jnp.concatenate([rec_w[h, i] for i in range(3)], axis=1) for h in range(2))
-    gain1, gain2 = gains_all[0:1], gains_all[1:2]
-    own_ends = lax.dynamic_index_in_dim(group_ends, q, 0, True)
-    ends = jnp.concatenate([group_ends, own_ends], axis=0)
-    valid_own = ((lax.broadcasted_iota(jnp.int32, (half, 1), 0) + c * half).astype(F32)) < e3
-    x_in = tokens[0].astype(F32)
-    scale1 = norm_scale(x_in)
-    unit1 = x_in * scale1
-    u_all = u.reshape(4 * length, width)
-    u_own = lax.dynamic_index_in_dim(u, q, 0, False).reshape(length, width)
-    mixed_a, mixed_b = mixed[:4].reshape(4 * length, blk), mixed[4]
-
-    def with_own(a, b):
-        a = a.reshape(4, length, -1)
-        own = lax.dynamic_index_in_dim(a, q, 0, False) + b
-        return lax.dynamic_update_index_in_dim(a, own, q, 0)
-
-    def by_half(a):
-        return a.astype(BF).reshape(4, 2, half, width)
-
     g_mlp, rec_own, resid_grad, hid, gain2_sum = mlp_block(
         norm_own, resid, gains_all, cotangent[0], group_ends, mlp_w, mlp_grad, 4
     )
-    hidden = hid.transpose(0, 2, 1, 3).reshape(4 * length, ff)
-    w_d = mlp_w[2 * ff // blk :].reshape(ff // blk, width, blk).transpose(1, 0, 2).reshape(width, ff)
-    mlp_out = act_reduce(by_half(mm_t(hidden, w_d)), 5)
-    result = jnp.where(valid_own, resid + mlp_out, 0.0).astype(BF)
-    gain2_part = gain2_sum[0]
-    grad_mlp = g_mlp.reshape(3 * ff // blk, width, blk).transpose(1, 0, 2).reshape(width, 3 * ff)
-    rg = act_gather(rec_own, 8)
-    rec_grad = rg.reshape(4 * length, width)
-    rec_grad_own = lax.dynamic_index_in_dim(rg, q, 0, False).reshape(length, width)
-    mixed_grad = jnp.concatenate(
-        [
-            mm(rec_grad, recq[:, 2 * blk :]).reshape(4, length, blk),
-            mm(rec_grad_own, rec4[:, 2 * blk :]).reshape(1, length, blk),
-        ],
-        axis=0,
+    result, token_grad, l_mlp, l_rec, l_sh, l_gate, l_small = backward(
+        tokens[0], rec_own, resid_grad, resid, gains_all, gain2_sum, group_ends, vec, gates,
+        (pre, state, mixed), hid, g_mlp, rec_w, mlp_w, u, n, taps, 5,
     )
-    low, gate_w_grad, vec_grad = rec_backward(taps, pre, gates, vec, ends, conv, rate, gate, state, mixed_grad)
-    low_a, low_b = low[:4].reshape(4 * length, 2 * blk), low[4]
-    u_part = with_own(mm_t(low_a, recq[:, : 2 * blk]), mm_t(low_b, rec4[:, : 2 * blk]))
-    u_grad = act_reduce(by_half(u_part), 9)
-    grad_q = jnp.concatenate([t_mm(u_all, low_a).astype(BF), t_mm(rec_grad, mixed_a).astype(BF)], axis=1)
-    grad_4 = jnp.concatenate([t_mm(u_own, low_b).astype(BF), t_mm(rec_grad_own, mixed_b).astype(BF)], axis=1)
-    gain1_part = jnp.sum(u_grad * unit1, axis=0)
-    token_grad = resid_grad + norm_back(u_grad * gain1, unit1, scale1)
-    gains = lax.psum(jnp.stack([gain1_part, gain2_part]), "tensor")
-
-    nvg = vec_grad.shape[1]
-    depth = -(-(rb + nvg + 2) // 8) * 8
-
-    def small_grads(h, extra):
-        v = vec_grad[h].reshape(nvg, n, rb).transpose(1, 0, 2)
-        v = jnp.pad(v, ((0, 0), (0, 0), (0, 2 * blk - rb)))
-        g = extra.reshape(2, n, rows).transpose(1, 0, 2)
-        g = jnp.pad(g, ((0, 0), (0, 0), (0, 2 * blk - rows)))
-        s = jnp.concatenate([gate_w_grad[h].reshape(n, rb, 2 * blk), v, g], axis=1)
-        return jnp.pad(s, ((0, 0), (0, depth - s.shape[1]), (0, 0)))
-
-    sq = small_grads(0, jnp.zeros_like(gains))
-    s4 = small_grads(1, gains)
-
-    def slots(a):
-        return a.reshape(n, rows, a.shape[1])
-
-    o_mlp, o_q, o_4, o_sq, o_s4 = grad_reduce(
-        (slots(grad_mlp), slots(grad_q), slots(grad_4), sq, s4), (True, True, False, True, False), n, 10
-    )
-    rec_out = jnp.concatenate([o_q, o_4[None]], axis=0)
-    so = jnp.concatenate([o_sq, o_s4[None]], axis=0)
-
-    def heads_cols(a):
-        return a.transpose(1, 0, 2).reshape(rows, heads * blk)
-
-    def quarter_cols(a):
-        return a.transpose(1, 0, 2).reshape(rows, 4 * ff)
-
-    def vec_out(i):
-        return so[:, rb + i, :rb]
-
+    high = n // 8
+
+    def owned(a):
+        return jnp.sum(a.reshape((high, 4) + a.shape[1:]).astype(F32), axis=0)
+
+    tiles = ff // blk
+    o_mlp = jnp.sum(l_mlp.reshape(3, tiles, high, 4, rows, blk).astype(F32), axis=2)
+    o_mlp = o_mlp.transpose(0, 3, 2, 1, 4).reshape(3, rows, 4 * ff)
+    o_q = jnp.sum(l_rec.reshape(3, high, 4, rows, blk).astype(F32), axis=1)
+    o_sh = jnp.sum(l_sh.reshape(high * 2, 2, 3, rows // 2, blk).astype(F32), axis=0)
+    o_sh = o_sh.transpose(1, 0, 2, 3).reshape(3, 1, rows, blk)
+    o_rec = jnp.concatenate([o_q, o_sh], axis=1).transpose(0, 2, 1, 3).reshape(3, rows, heads * blk)
+    o_gate = owned(l_gate)
+    o_gate = jnp.concatenate([o_gate[:, 0], jnp.sum(o_gate[:, 1], axis=0, keepdims=True)], axis=0)
+    o_small = owned(l_small)
+    at = dp * rb
+    o_vec = jnp.concatenate([o_small[:, :8], jnp.sum(o_small[:, 8:16], axis=0, keepdims=True)], axis=0)
+    o_vec = lax.dynamic_slice_in_dim(o_vec, at, rb, 2)
+    o_gain = jnp.sum(o_small[:, 16:], axis=0).reshape(2, width)
+    o_gain = lax.dynamic_slice_in_dim(o_gain, dp * rows, rows, 1)
     return (
         result[None],
         token_grad[None],
-        o_s4[rb + nvg, :rows],
-        heads_cols(rec_out[:, :, :blk]),
-        heads_cols(rec_out[:, :, blk : 2 * blk]),
-        so[:, :rb, :blk],
-        so[:, :rb, blk:],
-        vec_out(0),
-        vec_out(1),
-        vec_out(2),
-        jnp.stack([vec_out(4 + k) for k in range(taps)]),
-        vec_out(3),
-        rec_out[:, :, 2 * blk :].transpose(0, 2, 1).reshape(heads * blk, rows),
-        o_s4[rb + nvg + 1, :rows],
-        quarter_cols(o_mlp[:, :, :ff]),
-        quarter_cols(o_mlp[:, :, ff : 2 * ff]),
-        o_mlp[:, :, 2 * ff :].transpose(0, 2, 1).reshape(4 * ff, rows),
+        o_gain[0],
+        o_rec[0],
+        o_rec[1],
+        o_gate[:, :, :blk],
+        o_gate[:, :, blk:],
+        o_vec[:, 0],
+        o_vec[:, 1],
+        o_vec[:, 2],
+        o_vec[:, 4 : 4 + taps].transpose(1, 0, 2),
+        o_vec[:, 3],
+        o_rec[2].T,
+        o_gain[1],
+        o_mlp[0],
+        o_mlp[1],
+        o_mlp[2].T,
     )
 
 

time: 861 us -> 619 us (0.72); the launches traced: 850 us -> 618 us
  Pallas kernels: 705 us -> 576 us
  local copies, waits for them, and re-layouts: 94.9 us -> 27.5 us
  matrix products: 25.4 us -> 0 us
    pallas_call x5 -> x1, Pallas kernels: 369 us -> 243 us  [backward(): pl.pallas_call(functools.partial(backward_kernel, n, taps), out_shape=(sd...]
    dot_general x9 -> x0, matrix products: 25.4 us -> none  [the longest x3 10.9 us: mm_t(): lax.dot_general(a, b, (((1,), (1,)), ((), ())), preferred_element_type=F32)]
    reshape x2 -> x1, local copies, waits for them, and re-layouts: 16 us -> 0.01 us  [local(): o_gain = jnp.sum(o_small[:, 16:], axis=0).reshape(2, width)]
    transpose x9 -> x2, local copies, waits for them, and re-layouts: 14.4 us -> 0.63 us  [the longest x1 0.6 us: local(): o_vec[:, 4:4 + taps].transpose(1, 0, 2)]
    another operation x5 -> x0, local copies, waits for them, and re-layouts: 13.3 us -> none  [the longest x1 13.1 us: slots(): return a.reshape(n, rows, a.shape[1])]
    unnamed x36 -> x18, local copies, waits for them, and re-layouts: 27.1 us -> 13.9 us
where the time goes in v3:
time: 619 us; the launch traced here: 618 us
  Pallas kernels  576 us (93%)
  local copies, waits for them, and re-layouts  27.5 us (4%)
  other arithmetic  9.62 us (2%)
    pallas_call x1, Pallas kernels, forward(): pl.pallas_call(functools.partial(forward_kernel, n, taps, heads), out_sha...  267 us
    pallas_call x1, Pallas kernels, backward(): pl.pallas_call(functools.partial(backward_kernel, n, taps), out_shape=(sd...  243 us
    pallas_call x1, Pallas kernels, mlp_block(): pl.pallas_call(mlp_kernel, out_shape=(jax.ShapeDtypeStruct(mlp_w.shape, B...  66.8 us
    unnamed x18, local copies, waits for them, and re-layouts  13.9 us

profile of v3, /device:TPU:0, one launch (start us, length us, event | category | flops | bytes accessed | tf_op | source)
XLA Modules:
  0.0 617.8 jit_solution(17381245475975805466)
XLA Ops:
  0.7 0.7 convert_element_type.40
  1.3 0.6 fusion.17
  5.3 0.7 copy.76
  6.0 0.7 copy.77
  6.6 0.7 copy.78
  7.3 0.7 copy.79
  8.0 0.7 concatenate.24
  8.9 1.3 pad_maximum_fusion.1.refs_10_
  10.2 1.9 copy.74
  12.1 2.3 copy.75
  14.4 267.1 %forward.1 = (bf16[2,3,16,128,256]{4,3,2,1,0:T(8,128)(2,1)}, bf16[9,16,128,256]{3,2,1,0:T(8,128)(2,1)}, bf16[2,256,512]{2,1,0:T(8,128)(2,1)}, f32[2,16,256]{2,1,...) custom-call(bf16[128,2048]{1,0:T(8,128)(2,1)} %bitcast.70, ...), custom_call_target="tpu_custom_call" | custom-call | tf_op jit(solution)/shard_map/forward/pallas_call | solution.py:547
  281.5 66.8 %mlp_block.1 = (bf16[9,16,128,256]{3,2,1,0:T(8,128)(2,1)}, bf16[128,2048]{1,0:T(8,128)(2,1)}, f32[128,2048]{1,0:T(8,128)}, bf16[3,4,256,256]{3,2,1,0:T(8,128)(2,1)}, f32[8,2048]{1,0:T(8,128)}) custom-call(bf16[128,2048]{1,0:T(8,128)(2,1)} %get-tuple-element.42.norm, f32[128,2048]{1,0:T(8,128)} %get-tuple-element.43.resid.refs_2_, ...), custom_call_target="tpu_custom_call" | custom-call | tf_op jit(solution)/shard_map/mlp_block/pallas_call | solution.py:702
  348.3 242.6 %backward.1 = (bf16[128,2048]{1,0:T(8,128)(2,1)}, f32[128,2048]{1,0:T(8,128)}, bf16[9,8,128,256]{3,2,1,0:T(8,128)(2,1)}, bf16[3,8,128,256]{3,2,1,0:T(8,128)(2,1)...) custom-call(bf16[128,2048]{1,0:T(8,128)(2,1)} %bitcast.71, ...), custom_call_target="tpu_custom_call" | custom-call | tf_op jit(solution)/shard_map/backward/pallas_call | solution.py:1156
  590.9 1.1 reduce_sum.72
  592.1 0.5 slice_bitcast_fusion.2
  592.6 0.6 slice_bitcast_fusion.1
  593.2 0.6 copy_bitcast_fusion
  593.8 0.6 copy_bitcast_fusion.2
  594.4 1.1 convert_reduce_fusion.3
  595.6 0.7 pad_maximum_fusion
  597.1 1.1 copy.84
  598.4 1.1 copy.89
  599.7 1.1 copy.88
  600.7 4.0 convert_reduce_fusion
  604.8 1.4 fusion.14
  606.2 3.0 copy.87
  609.3 1.6 copy.86
  610.9 3.0 copy.91
  613.9 0.5 copy.85
  614.4 1.6 copy.90
  616.0 0.8 copy.103
  616.8 1.0 copy.104
  (26 shorter events, 1.6 us)
Async XLA Ops:
  590.9 5.4 copy-start.2
  594.4 2.0 copy-start
  614.4 1.6 copy-start.3
  614.4 2.4 copy-start.1

commit v4 on v3

--- a/solution.py
+++ b/solution.py
@@ -173,17 +173,28 @@
         pz, px = (zl + k // 2) % 2, (x + k % 2) % 2
         return pz * 2 + px, dev(dp_at(zh, pz, y, px), self.core)
 
-    def start(self):
-        own = self.buf.at[self.q, self.core]
-        remote(own, own, self.fsend.at[0], self.frecv.at[self.q], self.sib).start()
-        for k in (1, 2, 3):
+    def start(self, piece=0, pieces=1):
+        per = self.buf.shape[2] // pieces
+        own = self.buf.at[self.q, self.core, pl.ds(piece * per, per)]
+        for k in (1, 2):
             _, d = self.at(k)
             remote(own, own, self.send.at[k], self.recv.at[self.q], d).start()
+        remote(own, own, self.fsend.at[0], self.frecv.at[self.q], self.sib).start()
 
     def forward(self, k):
         pq, d = self.at(k)
         land = self.buf.at[pq, self.core]
         remote(land, land, self.send.at[k], self.recv.at[pq], d).wait_recv()
+
+        def relay():
+            _, beside = self.at(1)
+            remote(land, land, self.send.at[3], self.recv.at[pq], beside).start()
+
+        if isinstance(k, int):
+            if k == 2:
+                relay()
+        else:
+            pl.when(k == 2)(relay)
         remote(land, land, self.fsend.at[k], self.frecv.at[pq], self.sib).start()
 
     def arrive(self, k):
@@ -321,13 +332,15 @@
         )
     for i, w in enumerate((wb, wi, wo)):
         recs.append(make(3 + i, lambda s, g, i=i: rec.at[0, i, s], [(head_cols(w), whole)]))
-    quarter = rr // 4
+    part_rows = rr // 2
 
     def shared_piece(ref):
-        return lambda p: ref.at[pl.ds(pl.multiple_of(p * quarter, 8), quarter), pl.ds((heads - 1) * blk, blk)]
+        return lambda p: ref.at[
+            pl.ds(pl.multiple_of((p % 2) * part_rows, 8), part_rows), pl.ds((heads - 1) * blk, blk)
+        ]
 
     def shared_rows(s, g):
-        return rec.at[1, :, s, pl.ds(pl.multiple_of(g * quarter, 8), quarter), :]
+        return rec.at[1, :, s, pl.ds(pl.multiple_of((g % 2) * part_rows, 8), part_rows), :]
 
     shared = make(
         6, shared_rows, [(shared_piece(w), lambda r, i=i: r.at[i]) for i, w in enumerate((wb, wi, wo))]
@@ -345,6 +358,9 @@
         if j + ahead < len(order):
             order[j + ahead].forward_all(False)
         order[j].forward_all(True)
+        for _ in range(2 if j < 4 else 1):
+            if trickle:
+                trickle.pop(0)()
         if j + ahead < len(order):
             order[j + ahead].start(True)
         if j + 2 * ahead < len(order):
@@ -392,7 +408,7 @@
     u_rows = Rows(u_buf, r1, here, c)
     g_rows = Rows(o_grad, r2, here, c)
     u_buf[q, c] = (resid[...] * o_gain[0:1, :]).astype(BF)
-    u_rows.start()
+    trickle = [functools.partial(r.start, p, 8) for r in (u_rows, g_rows) for p in range(8)]
     e3 = o_ends[q][0:1, 3:4]
     spot = lax.broadcasted_iota(jnp.int32, (half, 1), 0).astype(F32) + (c * half).astype(F32)
     og[...] = jnp.where(spot < e3, cot[...], 0.0).astype(BF)
@@ -400,22 +416,28 @@
     place_grad = pltpu.make_async_copy(og, own_grad, fin.at[0])
     place_grad.start()
     place_grad.wait()
-    g_rows.start()
-    for j in range(3):
+    for j in range(5):
         pump(j)
-    for k in (1, 2, 3):
+    for k in (1, 2):
         u_rows.forward(k)
-    for j in range(3, 6):
-        pump(j)
-    for a in gats + recs[:2] + [shared]:
+    pump(5)
+    u_rows.forward(3)
+
+    _, beside = u_rows.at(1)
+
+    def exchange(g, first, many):
+        rows = rec.at[
+            1, :, pl.ds(first, many), pl.ds(pl.multiple_of((g % 2) * part_rows, 8), part_rows), :
+        ]
+        return remote(rows, rows, h_send, h_recv, beside)
+
+    shared.arrive_all()
+    eighth = n // 8
+    for p in range(4):
+        exchange(q, p * eighth, eighth).start()
+    trickle[:0] = [exchange(q, p * eighth, eighth).start for p in range(4, 8)]
+    for a in gats + recs:
         a.arrive_all()
-
-    def group_region(g):
-        return rec.at[1, :, :, pl.ds(pl.multiple_of(g * quarter, 8), quarter), :]
-
-    for k in (1, 2, 3):
-        _, d = u_rows.at(k)
-        remote(group_region(q), group_region(q), h_send.at[k], h_recv.at[q], d).start()
     for h in range(2):
         if rb % 16 == 0:
             o_gate[h] = gat[h].reshape(blk, 2 * blk)
@@ -425,21 +447,22 @@
             o_gate[h] = gfull[...].astype(BF)
     for k in range(4):
         u_rows.arrive(k)
-    recs[2].arrive_all()
-    for k in (1, 2, 3):
-        pq, d = u_rows.at(k)
-        remote(group_region(pq), group_region(pq), h_send.at[k], h_recv.at[pq], d).wait_recv()
     keep = [pltpu.make_async_copy(rec, o_rec, fin.at[1]), pltpu.make_async_copy(u_buf, o_u, fin.at[2])]
-    for cp in keep:
-        cp.start()
+    keep[1].start()
 
     sums = Sums(part, sibb, got, s1, u_rows)
 
     def step(i, carry):
-        h = jnp.where(i == 0, 1, 0)
-        k = jnp.maximum(i - 1, 0)
+        h = i // 4
+        k = ((i + 1) % 4) * ((7 - i) // 4)
         pq, _ = u_rows.at(k)
-        at = jnp.where(i == 0, 4, pq)
+        at = pq + h * (4 - pq)
+
+        @pl.when(i == 4)
+        def _():
+            exchange(q + 1, 0, n).wait_recv()
+            keep[0].start()
+
         rows = u_buf[pq].reshape(2 * half, width)
         for j in range(2):
             w = rec[h, j].reshape(width, blk)
@@ -454,13 +477,13 @@
             w = rec[h, 2, pl.ds(t * per, per)].reshape(per * rr, blk)
             tile = mm_t(mx, w)
             lanes = pl.ds(pl.multiple_of(t * (per * rr), 128), per * rr)
-            tile = tile + jnp.where(i == 1, extra[:, lanes], 0.0)
-
-            @pl.when(i == 0)
+            tile = tile + jnp.where(i == 4, extra[:, lanes], 0.0)
+
+            @pl.when(i == 3)
             def _():
                 extra[:, lanes] = tile
 
-            @pl.when(i > 0)
+            @pl.when(i != 3)
             def _():
                 part[pq, 0, :, lanes] = tile[:half].astype(BF)
                 part[pq, 1, :, lanes] = tile[half:].astype(BF)
@@ -469,46 +492,51 @@
 
         lax.fori_loop(0, width // (per * rr), cols_out, 0)
 
-        @pl.when(i > 0)
+        @pl.when(i != 3)
         def _():
             sums.push(k)
 
-        @pl.when(i == 2)
+        @pl.when((i > 0) & (i < 4))
         def _():
-            resid[...] = tok[...].astype(F32) + sums.pair(0)
-
-        @pl.when(i > 2)
-        def _():
-            sums.pass_on(k - 1)
-
-        for j, m in ((1, 6), (3, 7)):
+            sums.pass_on(i)
+
+        for j in range(4):
 
             @pl.when(i == j)
             def _():
-                pump(m)
+                pump(6 + j)
 
         return carry
 
     extra[...] = jnp.zeros_like(extra)
     lax.fori_loop(0, 5, step, 0)
-    sums.pass_on(3)
-    pump(8)
-    for k in (1, 2, 3):
+    sums.ready()
+
+    def finish(i, carry):
+        at = pl.ds(pl.multiple_of(i * 32, 32), 32)
+        total = tok[at, :].astype(F32) + sums.own(at)
+        resid[at, :] = total
+        unit = total * lax.rsqrt(jnp.mean(total * total, axis=-1, keepdims=True) + EPS)
+        o_norm[at, :] = (unit * o_gain[1:2, :]).astype(BF)
+        return carry
+
+    pump(10)
+    lax.fori_loop(0, half // 32, finish, 0)
+    pump(11)
+    while trickle:
+        trickle.pop(0)()
+    pump(12)
+    for k in (1, 2):
         g_rows.forward(k)
-    for k in (1, 2, 3):
-        resid[...] += sums.take(k)
-    total = resid[...]
-    unit = total * lax.rsqrt(jnp.mean(total * total, axis=-1, keepdims=True) + EPS)
-    o_norm[...] = (unit * o_gain[1:2, :]).astype(BF)
-    for j in range(9, len(order)):
+    pump(13)
+    g_rows.forward(3)
+    for j in range(14, len(order)):
         pump(j)
     for a in mlps:
         a.arrive_all()
     for k in range(4):
         g_rows.arrive(k)
-    for k in (1, 2, 3):
-        _, d = u_rows.at(k)
-        remote(group_region(q), group_region(q), h_send.at[k], h_recv.at[q], d).wait_send()
+    exchange(q, 0, n).wait_send()
     for a in [smalls, shared] + mlps + gats + recs + [u_rows, g_rows, sums]:
         a.finish()
     for cp in keep:
@@ -569,7 +597,7 @@
         ]
         * 16
         + row_sems() * 3
-        + [pltpu.SemaphoreType.DMA((3,)), pltpu.SemaphoreType.DMA((4,)), pltpu.SemaphoreType.DMA((4,))],
+        + [pltpu.SemaphoreType.DMA((3,)), pltpu.SemaphoreType.DMA, pltpu.SemaphoreType.DMA],
         compiler_params=pltpu.CompilerParams(
             collective_id=cid, has_side_effects=True, vmem_limit_bytes=VMEM_LIMIT
         ),
@@ -869,49 +897,45 @@
     for cp in grab:
         cp.start()
 
+    tiles = nt // 3
+
+    def cols_at(i):
+        return pl.ds(pl.multiple_of(i * blk, 128), blk)
+
     def own_part(i):
         return pltpu.make_async_copy(g_hbm.at[i, :, y], g_own.at[i % 2], loads.at[2 + i % 2])
 
     own_part(0).start()
-
-    def reduce_chunk(i):
-        own_part(i).wait()
-        if i + 1 < nt:
-            own_part(i + 1).start()
-        mlps[i].pass_on()
 
     def chunk(i, sem):
         return Scatter(
             lambda s: g_hbm.at[i, s // 4, (s // 2) % 2, s % 2],
             lambda s: g_own[i % 2, s // 4, s % 2],
             lambda j: y_mlp.at[i, j],
-            lambda j: l_mlp.at[i, j],
+            lambda j: l_mlp.at[j // 4, i // tiles, :, cols_at((j % 4) * tiles + i % tiles)],
             sem, here, there, c,
         )
 
     mlps = [chunk(i, some(4)) for i in range(nt)]
-    for a in mlps:
+    for a in mlps[:3]:
         a.start()
     recs = [
         Scatter(
             lambda s, i=i: grec.at[i, s],
             lambda s, i=i: grec[i, s],
             lambda j, i=i: y_rec.at[i, j],
-            lambda j, i=i: l_rec.at[i, j],
+            lambda j, i=i: l_rec.at[j // 4, i, :, cols_at(j % 4)],
             some(4), here, there, c,
         )
         for i in range(3)
     ]
     part_rows = rr // 2
 
-    def region(ref, h):
-        return ref.at[:, :, pl.ds(pl.multiple_of(h * part_rows, 8), part_rows), :]
-
     shared = Scatter(
         lambda s: gshin.at[:, s],
         lambda s: gshin[:, s],
         lambda j: y_sh.at[j],
-        lambda j: l_sh.at[j],
+        lambda j: l_sh.at[j // 2, :, pl.ds(pl.multiple_of((j % 2) * part_rows, 8), part_rows), :],
         some(4), here, there, c,
     )
     gate_sc = Scatter(
@@ -922,6 +946,21 @@
         some(4), here, there, c,
     )
     h_send, h_recv, s_send, s_recv, z_send, z_recv, m_send, m_recv = some(8)
+    order = mlps + recs + [gate_sc]
+    trickle = []
+
+    def pump(j):
+        if j < nt:
+            own_part(j).wait()
+            if j + 1 < nt:
+                own_part(j + 1).start()
+        order[j].pass_on()
+        for _ in range(2):
+            if trickle:
+                trickle.pop(0)()
+        if j + 3 < len(order):
+            order[j + 3].start()
+
     gg[...] = jnp.zeros_like(gg)
     vg[...] = jnp.zeros_like(vg)
     grab[0].wait()
@@ -988,12 +1027,16 @@
 
             @pl.when(i == j)
             def _():
-                reduce_chunk(j)
+                pump(j)
 
         return carry
 
     lax.fori_loop(0, 5, step, 0)
     sums1.pass_on(3)
+    for h in range(2):
+        for s in range(n):
+            ggl[h, s] = gg[h, s * rb : (s + 1) * rb, :].astype(BF)
+    pump(5)
     grab[1].wait()
 
     def grads(d, carry):
@@ -1015,14 +1058,15 @@
 
     lax.fori_loop(0, steps, grads, 0)
     _, beside = rows.at(1)
-    exchange = remote(region(gsh, 1 - x), gshin, h_send, h_recv, beside)
-    exchange.start()
-    for a in recs:
-        a.start()
-    for h in range(2):
-        for s in range(n):
-            ggl[h, s] = gg[h, s * rb : (s + 1) * rb, :].astype(BF)
-    gate_sc.start()
+
+    def exchange(first, many):
+        there_rows = pl.ds(pl.multiple_of((1 - x) * part_rows, 8), part_rows)
+        cut = pl.ds(first, many)
+        return remote(gsh.at[:, cut, there_rows, :], gshin.at[:, cut], h_send, h_recv, beside)
+
+    eighth = n // 8
+    trickle += [exchange(p * eighth, eighth).start for p in range(8)]
+    pump(6)
 
     sums1.ready()
 
@@ -1045,26 +1089,26 @@
     gain_rows = sml.at[pl.ds(16, 2 * steps)]
     with_sib = remote(gain_rows, sml_sib, s_send, s_recv, rows.sib)
     with_sib.start()
-    reduce_chunk(5)
-    exchange.wait()
+    pump(7)
+    with_sib.wait()
+    sml[16 : 16 + 2 * steps, :] += sml_sib[...]
+    with_y = remote(sml, y_sml, z_send, z_recv, dev(dp_at(zh, zl, 1 - y, x), c))
+    with_y.start()
+    pump(8)
+    pump(9)
+    exchange(0, n).wait()
     for s in range(n):
         gshin[:, s] = (
             gshin[:, s].astype(F32)
             + gsh[:, s, pl.ds(pl.multiple_of(x * part_rows, 8), part_rows), :].astype(F32)
         ).astype(BF)
     shared.start()
-    reduce_chunk(6)
-    with_sib.wait()
-    sml[16 : 16 + 2 * steps, :] += sml_sib[...]
-    with_y = remote(sml, y_sml, z_send, z_recv, dev(dp_at(zh, zl, 1 - y, x), c))
-    with_y.start()
-
     fetch = pltpu.make_async_copy(mlp_hbm.at[pl.ds(2 * (nt // 3), nt // 3)], rec.at[0], loads.at[0])
     fetch.start()
     per_row = length // rr
     fetch_hid = pltpu.make_async_copy(hid, gsh.at[:, pl.ds(0, 4 * per_row)], loads.at[1])
     fetch_hid.start()
-    reduce_chunk(7)
+    pump(10)
     fetch.wait()
     fetch_hid.wait()
 
@@ -1089,10 +1133,15 @@
         def _():
             sums2.pass_on(i)
 
+        for j in range(2):
+
+            @pl.when(i == 1 + 2 * j)
+            def _():
+                pump(11 + j)
+
         return carry
 
     lax.fori_loop(0, 4, out_rows, 0)
-    reduce_chunk(8)
     with_y.wait()
     sml[...] = sml[...] + y_sml[...]
     mine = zh * 4 + q
@@ -1104,9 +1153,6 @@
             cp = remote(sml, l_small.at[mine], m_send.at[i], m_recv.at[mine], dev(dp_at(h, z, y, w), c))
         cp.start()
         small_out.append(cp)
-    for a in recs:
-        a.pass_on()
-    gate_sc.pass_on()
     shared.pass_on()
     sums2.ready()
     e3 = ends[q][0:1, 3:4]
@@ -1158,9 +1204,9 @@
         out_shape=(
             sds(half, width),
             sds(half, width, t=F32),
-            sds(nt, slots, rr, blk),
-            sds(3, slots, rr, blk),
-            sds(slots, 3, rr // 2, blk),
+            sds(high, 3, rr, 4 * (nt // 3) * blk),
+            sds(high, 3, rr, 4 * blk),
+            sds(slots // 2, 3, rr, blk),
             sds(slots, 2, rb, 2 * blk),
             sds(slots, small_rows, blk, t=F32),
         ),
@@ -1266,13 +1312,11 @@
     def owned(a):
         return jnp.sum(a.reshape((high, 4) + a.shape[1:]).astype(F32), axis=0)
 
-    tiles = ff // blk
-    o_mlp = jnp.sum(l_mlp.reshape(3, tiles, high, 4, rows, blk).astype(F32), axis=2)
-    o_mlp = o_mlp.transpose(0, 3, 2, 1, 4).reshape(3, rows, 4 * ff)
-    o_q = jnp.sum(l_rec.reshape(3, high, 4, rows, blk).astype(F32), axis=1)
-    o_sh = jnp.sum(l_sh.reshape(high * 2, 2, 3, rows // 2, blk).astype(F32), axis=0)
-    o_sh = o_sh.transpose(1, 0, 2, 3).reshape(3, 1, rows, blk)
-    o_rec = jnp.concatenate([o_q, o_sh], axis=1).transpose(0, 2, 1, 3).reshape(3, rows, heads * blk)
+    def add(a):
+        return jnp.sum(a.astype(F32), axis=0)
+
+    o_mlp = [add(l_mlp[:, i]) for i in range(3)]
+    o_rec = [jnp.concatenate([add(l_rec[:, i]), add(l_sh[:, i])], axis=1) for i in range(3)]
     o_gate = owned(l_gate)
     o_gate = jnp.concatenate([o_gate[:, 0], jnp.sum(o_gate[:, 1], axis=0, keepdims=True)], axis=0)
     o_small = owned(l_small)

time: 619 us -> 561 us (0.906)
  Pallas kernels: 576 us -> 529 us
  local copies, waits for them, and re-layouts: 27.5 us -> 15.2 us
    pallas_call x1, Pallas kernels: 267 us -> 233 us  [forward(): pl.pallas_call(functools.partial(forward_kernel, n, taps, heads), out_sha...]
    pallas_call x1, Pallas kernels: 243 us -> 226 us  [backward(): pl.pallas_call(functools.partial(backward_kernel, n, taps), out_shape=(sd...]
    slice x8 -> x0, local copies, waits for them, and re-layouts: 8.18 us -> none  [the longest x2 4.47 us: local(): o_mlp[2]]
    unnamed x18 -> x16, local copies, waits for them, and re-layouts: 13.9 us -> 9.82 us
where the time goes in v4:
time: 561 us; the launch traced here: 560 us
  Pallas kernels  529 us (94%)
  local copies, waits for them, and re-layouts  15.2 us (3%)
  other arithmetic  12.1 us (2%)
    pallas_call x1, Pallas kernels, forward(): pl.pallas_call(functools.partial(forward_kernel, n, taps, heads), out_sha...  233 us
    pallas_call x1, Pallas kernels, backward(): pl.pallas_call(functools.partial(backward_kernel, n, taps), out_shape=(sd...  226 us
    pallas_call x1, Pallas kernels, mlp_block(): pl.pallas_call(mlp_kernel, out_shape=(jax.ShapeDtypeStruct(mlp_w.shape, B...  69.9 us

profile of v4, /device:TPU:0, one launch (start us, length us, event | category | flops | bytes accessed | tf_op | source)
XLA Modules:
  0.0 560.1 jit_solution(15959703990084087317)
XLA Ops:
  0.7 0.7 convert_element_type.58
  1.3 0.6 fusion.15
  5.2 0.1 fusion.10
  5.3 0.7 copy.44
  6.0 0.7 copy.45
  6.6 0.7 copy.46
  7.3 0.7 copy.47
  8.0 0.7 concatenate.30
  8.8 0.2 dynamic_update_slice.4
  8.9 1.3 pad_maximum_fusion.3.refs_10_
  10.2 1.9 copy.42
  12.1 2.3 copy.43
  14.4 233.2 %forward.1 = (bf16[2,3,16,128,256]{4,3,2,1,0:T(8,128)(2,1)}, bf16[9,16,128,256]{3,2,1,0:T(8,128)(2,1)}, bf16[2,256,512]{2,1,0:T(8,128)(2,1)}, f32[2,16,256]{2,1,...) custom-call(bf16[128,2048]{1,0:T(8,128)(2,1)} %bitcast.45, ...), custom_call_target="tpu_custom_call" | custom-call | tf_op jit(solution)/shard_map/forward/pallas_call | solution.py:575
  247.6 69.9 %mlp_block.1 = (bf16[9,16,128,256]{3,2,1,0:T(8,128)(2,1)}, bf16[128,2048]{1,0:T(8,128)(2,1)}, f32[128,2048]{1,0:T(8,128)}, bf16[3,4,256,256]{3,2,1,0:T(8,128)(2,1)}, f32[8,2048]{1,0:T(8,128)}) custom-call(bf16[128,2048]{1,0:T(8,128)(2,1)} %get-tuple-element.42.norm, f32[128,2048]{1,0:T(8,128)} %get-tuple-element.43.resid.refs_2_, ...), custom_call_target="tpu_custom_call" | custom-call | tf_op jit(solution)/shard_map/mlp_block/pallas_call | solution.py:730
  317.5 225.6 %backward.1 = (bf16[128,2048]{1,0:T(8,128)(2,1)}, f32[128,2048]{1,0:T(8,128)}, bf16[2,3,128,3072]{3,2,1,0:T(8,128)(2,1)}, bf16[2,3,128,1024]{3,2,1,0:T(8,128)(2,...) custom-call(bf16[128,2048]{1,0:T(8,128)(2,1)} %bitcast.46, ...), custom_call_target="tpu_custom_call" | custom-call | tf_op jit(solution)/shard_map/backward/pallas_call | solution.py:1202
  543.1 0.0 copy-start.2
  543.1 1.1 reduce_sum.126
  544.3 0.1 fusion.1
  544.4 0.5 slice_bitcast_fusion.2
  544.9 0.6 slice_bitcast_fusion.1
  545.5 0.6 copy_bitcast_fusion
  546.1 0.6 copy_bitcast_fusion.2
  546.7 1.0 convert_reduce_fusion.6
  547.8 0.7 pad_maximum_fusion.2
  548.5 0.1 convert_reduce_fusion.7
  548.6 0.3 convert_reduce_fusion.3
  549.0 1.1 copy.48
  550.0 1.1 pad_maximum_fusion
  551.2 5.5 convert_reduce_fusion
  556.7 1.6 copy.49
  558.3 0.8 copy.61
  559.1 1.0 copy.62
  (16 shorter events, 0.1 us)
Async XLA Ops:
  543.1 5.4 copy-start.2
  543.1 5.5 copy-start
  556.7 1.6 copy-start.3
  556.7 2.4 copy-start.1

commit v5 on v4

--- a/solution.py
+++ b/solution.py
@@ -351,14 +351,15 @@
             j = i * (ff // blk) + t
             mlps.append(make(7 + j, lambda s, g, j=j: o_mlp.at[j, s], [(piece, whole)]))
     count = len(there)
-    order = [recs[0], gats[0], recs[1], gats[1], shared, recs[2]] + mlps
-    ahead = 2
+    order = [shared, recs[0], gats[0], recs[1], gats[1], recs[2]] + mlps
+    ahead = 3
+    trickle = []
 
     def pump(j):
         if j + ahead < len(order):
             order[j + ahead].forward_all(False)
         order[j].forward_all(True)
-        for _ in range(2 if j < 4 else 1):
+        for _ in range(3 if j < 6 else 2):
             if trickle:
                 trickle.pop(0)()
         if j + ahead < len(order):
@@ -377,9 +378,10 @@
     unit = xin * lax.rsqrt(jnp.mean(xin * xin, axis=-1, keepdims=True) + EPS)
     resid[...] = unit
     smalls.forward_all(False)
-    smalls.forward_all(True)
     for j in range(ahead):
         order[j].forward_all(False)
+    smalls.forward_all(True)
+    pump(0)
     smalls.arrive_all()
     per_vec, per_gain = blk // 128, width // 128
     base = (heads - 1) * 16
@@ -404,11 +406,16 @@
         o_gain[:, g * 128 : (g + 1) * 128] = groups[g][0:8]
     for j in range(4):
         v = sml[dp_at(zh, j // 2, y, j % 2), SMALL_ROWS - 16 : SMALL_ROWS, :].astype(F32)
-        o_ends[j] = jnp.broadcast_to(v[2:3], (8, 128))
+        row = jnp.broadcast_to(v[2:3], (8, 128))
+        lane = lax.broadcasted_iota(jnp.int32, (8, 128), 1)
+        ends = jnp.zeros((8, 128), F32)
+        for i in range(4):
+            ends = ends + jnp.where(lane >= i, row[:, i : i + 1], 0.0)
+        o_ends[j] = ends
     u_rows = Rows(u_buf, r1, here, c)
     g_rows = Rows(o_grad, r2, here, c)
     u_buf[q, c] = (resid[...] * o_gain[0:1, :]).astype(BF)
-    trickle = [functools.partial(r.start, p, 8) for r in (u_rows, g_rows) for p in range(8)]
+    trickle += [functools.partial(u_rows.start, p, 8) for p in range(8)]
     e3 = o_ends[q][0:1, 3:4]
     spot = lax.broadcasted_iota(jnp.int32, (half, 1), 0).astype(F32) + (c * half).astype(F32)
     og[...] = jnp.where(spot < e3, cot[...], 0.0).astype(BF)
@@ -416,13 +423,6 @@
     place_grad = pltpu.make_async_copy(og, own_grad, fin.at[0])
     place_grad.start()
     place_grad.wait()
-    for j in range(5):
-        pump(j)
-    for k in (1, 2):
-        u_rows.forward(k)
-    pump(5)
-    u_rows.forward(3)
-
     _, beside = u_rows.at(1)
 
     def exchange(g, first, many):
@@ -431,11 +431,19 @@
         ]
         return remote(rows, rows, h_send, h_recv, beside)
 
+    pump(1)
     shared.arrive_all()
     eighth = n // 8
-    for p in range(4):
-        exchange(q, p * eighth, eighth).start()
-    trickle[:0] = [exchange(q, p * eighth, eighth).start for p in range(4, 8)]
+    trickle += [exchange(q, p * eighth, eighth).start for p in range(8)]
+    for j in range(2, 5):
+        pump(j)
+    for k in (1, 2):
+        u_rows.forward(k)
+    pump(5)
+    while trickle:
+        trickle.pop(0)()
+    trickle += [functools.partial(g_rows.start, p, 8) for p in range(8)]
+    u_rows.forward(3)
     for a in gats + recs:
         a.arrive_all()
     for h in range(2):
@@ -510,6 +518,10 @@
 
     extra[...] = jnp.zeros_like(extra)
     lax.fori_loop(0, 5, step, 0)
+    pump(10)
+    pump(11)
+    for k in (1, 2):
+        g_rows.forward(k)
     sums.ready()
 
     def finish(i, carry):
@@ -520,14 +532,8 @@
         o_norm[at, :] = (unit * o_gain[1:2, :]).astype(BF)
         return carry
 
-    pump(10)
     lax.fori_loop(0, half // 32, finish, 0)
-    pump(11)
-    while trickle:
-        trickle.pop(0)()
     pump(12)
-    for k in (1, 2):
-        g_rows.forward(k)
     pump(13)
     g_rows.forward(3)
     for j in range(14, len(order)):
@@ -761,26 +767,23 @@
 
 
 class Scatter:
-    def __init__(self, away, mine, pair, landed, sems, here, there, core):
-        self.away, self.mine, self.pair, self.landed = away, mine, pair, landed
+    def __init__(self, away, both, mine, pair, landed, sems, here, there, core):
+        self.away, self.both, self.mine, self.pair, self.landed = away, both, mine, pair, landed
         self.ysend, self.yrecv, self.send, self.recv = sems
         zh, zl, y, x = here
         self.core = core
         self.own = zh * 4 + zl * 2 + x
-        self.places = [
-            (h * 4 + z * 2 + w, dp_at(h, z, y, w), dp_at(h, z, 1 - y, w)) for h, z, w in (*there[1:], there[0])
-        ]
+        self.places = [(h * 4 + z * 2 + w, dp_at(h, z, y, w)) for h, z, w in (*there[4:], *there[1:4], there[0])]
         self.other = dev(dp_at(zh, zl, 1 - y, x), core)
 
     def start(self):
-        for j, _, far in self.places:
-            remote(self.away(far), self.pair(j), self.ysend.at[j], self.yrecv.at[j], self.other).start()
+        remote(self.away, self.both, self.ysend, self.yrecv, self.other).start()
 
     def pass_on(self):
         last = len(self.places) - 1
-        for i, (j, near, _) in enumerate(self.places):
+        remote(self.away, self.both, self.ysend, self.yrecv, self.other).wait_recv()
+        for i, (j, near) in enumerate(self.places):
             slot = self.pair(j)
-            remote(slot, slot, self.ysend.at[j], self.yrecv.at[j], self.other).wait_recv()
             slot[...] = (self.mine(near).astype(F32) + slot[...].astype(F32)).astype(slot.dtype)
             if i == last:
                 pltpu.make_async_copy(slot, self.landed(self.own), self.send.at[j]).start()
@@ -791,9 +794,9 @@
 
     def collect(self):
         last = len(self.places) - 1
-        for i, (j, _, _) in enumerate(self.places):
+        remote(self.away, self.both, self.ysend, self.yrecv, self.other).wait_send()
+        for i, (j, _) in enumerate(self.places):
             slot, land = self.pair(j), self.landed(j)
-            remote(slot, slot, self.ysend.at[j], self.yrecv.at[j], self.other).wait_send()
             if i == last:
                 pltpu.make_async_copy(land, land, self.send.at[j]).wait()
             else:
@@ -802,7 +805,7 @@
 
 
 def scatter_sems(high):
-    return [pltpu.SemaphoreType.DMA((high * 4,))] * 4
+    return [pltpu.SemaphoreType.DMA, pltpu.SemaphoreType.DMA] + [pltpu.SemaphoreType.DMA((high * 4,))] * 2
 
 
 def rec_gates(taps, conv_in, vec, gates, ends):
@@ -857,9 +860,9 @@
     (tok, rgrad, resid, gain, gsum2, ends, vec, gates, pre, state, mixed) = refs[:11]
     (rec_own, hid, g_hbm, rec_hbm, mlp_hbm, u_hbm) = refs[11:17]
     (o_res, o_tok, l_mlp, l_rec, l_sh, l_gate, l_small) = refs[17:24]
-    (rec, ub, rg, part, sib1, got1, sib2, got2, low, grec, gsh, gshin, g_own, y_mlp, y_rec, y_sh, a_scr, c_scr,
-     gg, vg, ggl, y_gate, sml, sml_sib, y_sml) = refs[24:49]
-    sems = refs[49:]
+    (rec, ub, rg, part, sib1, got1, low, grec, gsh, gshin, g_own, y_mlp, y_rec, y_sh, a_scr, c_scr,
+     gg, vg, ggl, y_gate, sml, sml_sib, y_sml) = refs[24:47]
+    sems = refs[47:]
     zh, zl, y, x, c = place()
     here = (zh, zl, y, x)
     q, me = zl * 2 + x, dp_at(zh, zl, y, x)
@@ -870,7 +873,7 @@
     blk = mixed.shape[2]
     rr = width // n
     rb = blk // n
-    nt = y_mlp.shape[0]
+    nt = g_own.shape[0]
     per, steps = blk // rr, width // blk
     taken = [0]
 
@@ -880,7 +883,7 @@
 
     rows = Rows(rg, some(4), here, c)
     sums1 = Sums(part, sib1, got1, some(4), rows)
-    sums2 = Sums(part, sib2, got2, some(4), rows)
+    sums2 = Sums(part, sib1, got1, some(4), rows)
     (loads,) = some(1)
     greet(
         [dev(dp_at(h, z, y, w), c) for h, z, w in there[1:]]
@@ -893,6 +896,7 @@
     grab = [
         pltpu.make_async_copy(rec_hbm, rec, loads.at[0]),
         pltpu.make_async_copy(u_hbm, ub, loads.at[1]),
+        pltpu.make_async_copy(g_hbm.at[:, :, y], g_own, loads.at[2]),
     ]
     for cp in grab:
         cp.start()
@@ -902,16 +906,12 @@
     def cols_at(i):
         return pl.ds(pl.multiple_of(i * blk, 128), blk)
 
-    def own_part(i):
-        return pltpu.make_async_copy(g_hbm.at[i, :, y], g_own.at[i % 2], loads.at[2 + i % 2])
-
-    own_part(0).start()
-
     def chunk(i, sem):
         return Scatter(
-            lambda s: g_hbm.at[i, s // 4, (s // 2) % 2, s % 2],
-            lambda s: g_own[i % 2, s // 4, s % 2],
-            lambda j: y_mlp.at[i, j],
+            g_hbm.at[i, :, 1 - y],
+            y_mlp.at[i],
+            lambda s: g_own[i, s // 4, s % 2],
+            lambda j: y_mlp.at[i, j // 2, j % 2],
             lambda j: l_mlp.at[j // 4, i // tiles, :, cols_at((j % 4) * tiles + i % tiles)],
             sem, here, there, c,
         )
@@ -921,9 +921,10 @@
         a.start()
     recs = [
         Scatter(
-            lambda s, i=i: grec.at[i, s],
-            lambda s, i=i: grec[i, s],
-            lambda j, i=i: y_rec.at[i, j],
+            grec.at[i, :, 1 - y],
+            y_rec.at[i],
+            lambda s, i=i: grec[i, s // 4, (s // 2) % 2, s % 2],
+            lambda j, i=i: y_rec.at[i, j // 2, j % 2],
             lambda j, i=i: l_rec.at[j // 4, i, :, cols_at(j % 4)],
             some(4), here, there, c,
         )
@@ -932,30 +933,30 @@
     part_rows = rr // 2
 
     shared = Scatter(
-        lambda s: gshin.at[:, s],
-        lambda s: gshin[:, s],
-        lambda j: y_sh.at[j],
+        gshin.at[:, :, 1 - y],
+        y_sh,
+        lambda s: gshin[:, s // 4, (s // 2) % 2, s % 2],
+        lambda j: y_sh.at[:, j // 2, j % 2],
         lambda j: l_sh.at[j // 2, :, pl.ds(pl.multiple_of((j % 2) * part_rows, 8), part_rows), :],
         some(4), here, there, c,
     )
     gate_sc = Scatter(
-        lambda s: ggl.at[:, s],
-        lambda s: ggl[:, s],
-        lambda j: y_gate.at[j],
+        ggl.at[:, :, 1 - y],
+        y_gate,
+        lambda s: ggl[:, s // 4, (s // 2) % 2, s % 2],
+        lambda j: y_gate.at[:, j // 2, j % 2],
         lambda j: l_gate.at[j],
         some(4), here, there, c,
     )
-    h_send, h_recv, s_send, s_recv, z_send, z_recv, m_send, m_recv = some(8)
-    order = mlps + recs + [gate_sc]
+    h_send, h_recv, s_send, s_recv, z_send, z_recv, m_send, m_recv, again = some(9)
+    order = mlps + [shared] + recs + [gate_sc]
     trickle = []
+    _, beside = rows.at(1)
+    eighth = n // 16
 
     def pump(j):
-        if j < nt:
-            own_part(j).wait()
-            if j + 1 < nt:
-                own_part(j + 1).start()
         order[j].pass_on()
-        for _ in range(2):
+        for _ in range(2 if j else 0):
             if trickle:
                 trickle.pop(0)()
         if j + 3 < len(order):
@@ -964,6 +965,29 @@
     gg[...] = jnp.zeros_like(gg)
     vg[...] = jnp.zeros_like(vg)
     grab[0].wait()
+
+    def exchange(first, many):
+        there_rows = pl.ds(pl.multiple_of((1 - x) * part_rows, 8), part_rows)
+        cut = pl.ds(first, many)
+        return remote(gsh.at[:, cut, :, :, there_rows, :], gshin.at[:, cut], h_send, h_recv, beside)
+
+    def store(ref, i, d, tile):
+        tile = tile.astype(BF)
+        if per == 2:
+            ref[i, d // 2, d % 2] = tile.reshape(2, rr, blk)
+        else:
+            ref[i, pl.ds(d * (per // 4), per // 4)] = tile.reshape(per // 4, 2, 2, rr, blk)
+
+    def shared_grads(d, carry):
+        lanes = pl.ds(pl.multiple_of(d * blk, 128), blk)
+        uo = ub[q, :, :, lanes].reshape(length, blk).T
+        ro = rg[q, :, :, lanes].reshape(length, blk).T
+        for i in range(3):
+            own = low[4, :, i * blk : (i + 1) * blk] if i < 2 else mixed[4]
+            store(gsh, i, d, mm(uo if i < 2 else ro, own))
+        return carry
+
+    trickle += [exchange(p * eighth, eighth).start for p in range(4)]
 
     def step(i, carry):
         h = jnp.where(i == 1, 1, 0)
@@ -1027,6 +1051,11 @@
 
             @pl.when(i == j)
             def _():
+                if j == 0:
+                    grab[2].wait()
+                if j == 1:
+                    grab[1].wait()
+                    lax.fori_loop(0, steps, shared_grads, 0)
                 pump(j)
 
         return carry
@@ -1035,37 +1064,33 @@
     sums1.pass_on(3)
     for h in range(2):
         for s in range(n):
-            ggl[h, s] = gg[h, s * rb : (s + 1) * rb, :].astype(BF)
+            ggl[h, s // 4, (s // 2) % 2, s % 2] = gg[h, s * rb : (s + 1) * rb, :].astype(BF)
+    fetch = pltpu.make_async_copy(mlp_hbm.at[pl.ds(2 * (nt // 3), nt // 3)], rec.at[0], loads.at[0])
+    fetch.start()
     pump(5)
-    grab[1].wait()
 
     def grads(d, carry):
         lanes = pl.ds(pl.multiple_of(d * blk, 128), blk)
-        at = pl.ds(d * per, per)
         ut = ub[:, :, :, lanes].reshape(4 * length, blk).T
         rt = rg[:, :, :, lanes].reshape(4 * length, blk).T
-        uo = ub[q, :, :, lanes].reshape(length, blk).T
-        ro = rg[q, :, :, lanes].reshape(length, blk).T
         for i in range(3):
             if i < 2:
                 right = low[0:4, :, i * blk : (i + 1) * blk].reshape(4 * length, blk)
-                own = low[4, :, i * blk : (i + 1) * blk]
             else:
-                right, own = mixed[0:4].reshape(4 * length, blk), mixed[4]
-            grec[i, at] = mm(ut if i < 2 else rt, right).astype(BF).reshape(per, rr, blk)
-            gsh[i, at] = mm(uo if i < 2 else ro, own).astype(BF).reshape(per, rr, blk)
+                right = mixed[0:4].reshape(4 * length, blk)
+            store(grec, i, d, mm(ut if i < 2 else rt, right))
         return carry
 
     lax.fori_loop(0, steps, grads, 0)
-    _, beside = rows.at(1)
-
-    def exchange(first, many):
-        there_rows = pl.ds(pl.multiple_of((1 - x) * part_rows, 8), part_rows)
-        cut = pl.ds(first, many)
-        return remote(gsh.at[:, cut, there_rows, :], gshin.at[:, cut], h_send, h_recv, beside)
-
-    eighth = n // 8
-    trickle += [exchange(p * eighth, eighth).start for p in range(8)]
+    exchange(0, n // 4).wait()
+    for s in range(n // 4):
+        gshin[:, s] = (
+            gshin[:, s].astype(F32)
+            + gsh[:, s, :, :, pl.ds(pl.multiple_of(x * part_rows, 8), part_rows), :].astype(F32)
+        ).astype(BF)
+    per_row = length // rr
+    fetch_hid = pltpu.make_async_copy(hid, gsh.at[:, pl.ds(0, per_row)], loads.at[1])
+    fetch_hid.start()
     pump(6)
 
     sums1.ready()
@@ -1081,6 +1106,8 @@
 
     gsum1 = lax.fori_loop(0, half // 32, finish, jnp.zeros((1, width), F32))
     sums1.finish()
+    for d in [rows.sib] + [rows.at(k)[1] for k in (1, 2, 3)]:
+        pl.semaphore_signal(again, inc=1, device_id=d, device_id_type=MESH)
     for h in range(2):
         sml[8 * h : 8 * h + 8, :] = vg[h]
     for i in range(steps):
@@ -1090,27 +1117,16 @@
     with_sib = remote(gain_rows, sml_sib, s_send, s_recv, rows.sib)
     with_sib.start()
     pump(7)
-    with_sib.wait()
-    sml[16 : 16 + 2 * steps, :] += sml_sib[...]
-    with_y = remote(sml, y_sml, z_send, z_recv, dev(dp_at(zh, zl, 1 - y, x), c))
-    with_y.start()
-    pump(8)
-    pump(9)
-    exchange(0, n).wait()
-    for s in range(n):
-        gshin[:, s] = (
-            gshin[:, s].astype(F32)
-            + gsh[:, s, pl.ds(pl.multiple_of(x * part_rows, 8), part_rows), :].astype(F32)
-        ).astype(BF)
-    shared.start()
-    fetch = pltpu.make_async_copy(mlp_hbm.at[pl.ds(2 * (nt // 3), nt // 3)], rec.at[0], loads.at[0])
-    fetch.start()
-    per_row = length // rr
-    fetch_hid = pltpu.make_async_copy(hid, gsh.at[:, pl.ds(0, 4 * per_row)], loads.at[1])
-    fetch_hid.start()
-    pump(10)
+
     fetch.wait()
     fetch_hid.wait()
+
+    pl.semaphore_wait(again, 4)
+
+    def hid_rows(t, row):
+        if per_row == 2:
+            return gsh[t, row // 2, row % 2].reshape(length, blk)
+        return gsh[t, pl.ds(row * (per_row // 4), per_row // 4)].reshape(length, blk)
 
     def out_rows(i, carry):
         k = (i + 1) % 4
@@ -1119,7 +1135,7 @@
         def cols_out(d, carry):
             tile = jnp.zeros((length, blk), F32)
             for t in range(nt // 3):
-                left = gsh[t, pl.ds(pq * per_row, per_row)].reshape(length, blk)
+                left = hid_rows(t, pq)
                 tile = tile + mm_t(left, rec[0, t, pl.ds(d * per, per)].reshape(blk, blk))
             lanes = pl.ds(pl.multiple_of(d * blk, 128), blk)
             part[pq, 0, :, lanes] = tile[:half].astype(BF)
@@ -1133,15 +1149,16 @@
         def _():
             sums2.pass_on(i)
 
-        for j in range(2):
-
-            @pl.when(i == 1 + 2 * j)
-            def _():
-                pump(11 + j)
-
         return carry
 
     lax.fori_loop(0, 4, out_rows, 0)
+    pump(8)
+    with_sib.wait()
+    sml[16 : 16 + 2 * steps, :] += sml_sib[...]
+    with_y = remote(sml, y_sml, z_send, z_recv, dev(dp_at(zh, zl, 1 - y, x), c))
+    with_y.start()
+    pump(9)
+    pump(10)
     with_y.wait()
     sml[...] = sml[...] + y_sml[...]
     mine = zh * 4 + q
@@ -1153,7 +1170,7 @@
             cp = remote(sml, l_small.at[mine], m_send.at[i], m_recv.at[mine], dev(dp_at(h, z, y, w), c))
         cp.start()
         small_out.append(cp)
-    shared.pass_on()
+    pump(11)
     sums2.ready()
     e3 = ends[q][0:1, 3:4]
 
@@ -1165,6 +1182,8 @@
 
     lax.fori_loop(0, half // 32, result, 0)
     sums2.finish()
+    pump(12)
+    pump(13)
     rows.finish()
     for a in mlps + recs + [gate_sc, shared]:
         a.collect()
@@ -1189,7 +1208,7 @@
     vm = pl.BlockSpec(memory_space=pltpu.VMEM)
     hb = pl.BlockSpec(memory_space=pl.ANY)
     g_view = g_mlp.reshape(nt, n // 4, 2, 2, rr, blk)
-    hid = hid.reshape(nt // 3, 4 * length // rr, rr, blk)
+    hid = hid.reshape(nt // 3, length // rr, 2, 2, rr, blk)
     small_rows = 16 + 2 * (width // blk)
 
     def sds(*shape, t=BF):
@@ -1219,22 +1238,20 @@
             v(4, 2, half, width),
             v(4, half, width),
             v(4, half, width),
-            v(4, half, width),
-            v(4, half, width),
             v(5, length, 2 * blk),
-            v(3, n, rr, blk),
-            v(3, n, rr, blk),
-            v(3, n, rr // 2, blk),
-            v(2, n // 4, 2, rr, blk),
-            v(nt, slots, rr, blk),
-            v(3, slots, rr, blk),
-            v(slots, 3, rr // 2, blk),
+            v(3, n // 4, 2, 2, rr, blk),
+            v(3, n // 4, 2, 2, rr, blk),
+            v(3, n // 4, 2, 2, rr // 2, blk),
+            v(nt, n // 4, 2, rr, blk),
+            v(nt, n // 4, 2, rr, blk),
+            v(3, n // 4, 2, rr, blk),
+            v(3, n // 4, 2, rr // 2, blk),
             v(length, blk, t=F32),
             v(length, blk, t=F32),
             v(2, blk, 2 * blk, t=F32),
             v(2, 4 + taps, blk, t=F32),
-            v(2, n, rb, 2 * blk),
-            v(slots, 2, rb, 2 * blk),
+            v(2, n // 4, 2, 2, rb, 2 * blk),
+            v(2, n // 4, 2, rb, 2 * blk),
             v(small_rows, blk, t=F32),
             v(small_rows - 16, blk, t=F32),
             v(small_rows, blk, t=F32),
@@ -1242,7 +1259,7 @@
         + row_sems() * 3
         + [dma((4,))]
         + scatter_sems(high) * (nt + 5)
-        + [dma, dma, dma, dma, dma, dma, dma((slots,)), dma((slots,))],
+        + [dma, dma, dma, dma, dma, dma, dma((slots,)), dma((slots,)), pltpu.SemaphoreType.REGULAR],
         compiler_params=pltpu.CompilerParams(
             collective_id=cid, has_side_effects=True, vmem_limit_bytes=VMEM_LIMIT
         ),
@@ -1284,17 +1301,11 @@
         return lax.dynamic_update_slice(jnp.zeros((v.shape[0], 128), BF), v, (0, at))
 
     params = jnp.concatenate(
-        [rgate_bias[:, None], igate_bias[:, None], decay_param[:, None], conv_weight.transpose(1, 0, 2), conv_bias[:, None]],
-        axis=1,
-    )
+        [rgate_bias[None], igate_bias[None], decay_param[None], conv_weight, conv_bias[None]], axis=0
+    ).transpose(1, 0, 2)
     params = jnp.pad(params, ((0, 0), (0, 16 - params.shape[1]), (0, 0))).reshape(heads * 16, rb)
-    lens = doc_lengths.reshape(4).astype(F32)
-    e0 = lens[0]
-    e1 = e0 + lens[1]
-    e2 = e1 + lens[2]
-    e3 = e2 + lens[3]
-    ends_own = jnp.pad(jnp.stack([e0, e1, e2, e3]).astype(BF)[None], ((0, 13), (0, 124)))
-    small = jnp.concatenate([lanes(params, rb), lanes(jnp.stack([rec_gain, mlp_gain]), rows), ends_own], axis=0)
+    lens_own = jnp.pad(doc_lengths.astype(BF), ((0, 13), (0, 124)))
+    small = jnp.concatenate([lanes(params, rb), lanes(jnp.stack([rec_gain, mlp_gain]), rows), lens_own], axis=0)
     (
         rec_w, mlp_w, gates, vec, gains_all, group_ends, u, mlp_grad, pre, state, mixed, resid, norm_own,
     ) = forward(

time: 561 us -> 549 us (0.979)
  Pallas kernels: 529 us -> 521 us
    pallas_call x1, Pallas kernels: 233 us -> 224 us  [forward(): pl.pallas_call(functools.partial(forward_kernel, n, taps, heads), out_sha...]
where the time goes in v5:
time: 549 us; the launch traced here: 548 us
  Pallas kernels  521 us (95%)
  local copies, waits for them, and re-layouts  14.6 us (3%)
  other arithmetic  12.1 us (2%)
    pallas_call x1, Pallas kernels, backward(): pl.pallas_call(functools.partial(backward_kernel, n, taps), out_shape=(sd...  227 us
    pallas_call x1, Pallas kernels, forward(): pl.pallas_call(functools.partial(forward_kernel, n, taps, heads), out_sha...  224 us
    pallas_call x1, Pallas kernels, mlp_block(): pl.pallas_call(mlp_kernel, out_shape=(jax.ShapeDtypeStruct(mlp_w.shape, B...  69.8 us

profile of v5, /device:TPU:0, one launch (start us, length us, event | category | flops | bytes accessed | tf_op | source)
XLA Modules:
  0.0 548.4 jit_solution(12285943966713841982)
XLA Ops:
  0.7 0.7 convert_element_type.49
  1.3 0.7 copy.44
  2.0 0.7 copy.45
  2.7 0.7 copy.46
  3.4 0.7 copy.47
  4.1 0.7 concatenate.22
  4.8 0.2 dynamic_update_slice.4
  5.0 1.3 fusion.2.refs_10_
  6.3 1.9 copy.42
  8.2 2.3 copy.43
  10.5 224.0 %forward.1 = (bf16[2,3,16,128,256]{4,3,2,1,0:T(8,128)(2,1)}, bf16[9,16,128,256]{3,2,1,0:T(8,128)(2,1)}, bf16[2,256,512]{2,1,0:T(8,128)(2,1)}, f32[2,16,256]{2,1,...) custom-call(bf16[128,2048]{1,0:T(8,128)(2,1)} %bitcast.45, ...), custom_call_target="tpu_custom_call" | custom-call | tf_op jit(solution)/shard_map/forward/pallas_call | solution.py:581
  234.5 69.8 %mlp_block.1 = (bf16[9,16,128,256]{3,2,1,0:T(8,128)(2,1)}, bf16[128,2048]{1,0:T(8,128)(2,1)}, f32[128,2048]{1,0:T(8,128)}, bf16[3,4,256,256]{3,2,1,0:T(8,128)(2,1)}, f32[8,2048]{1,0:T(8,128)}) custom-call(bf16[128,2048]{1,0:T(8,128)(2,1)} %get-tuple-element.42.norm, f32[128,2048]{1,0:T(8,128)} %get-tuple-element.43.resid.refs_2_, ...), custom_call_target="tpu_custom_call" | custom-call | tf_op jit(solution)/shard_map/mlp_block/pallas_call | solution.py:736
  304.3 227.0 %backward.1 = (bf16[128,2048]{1,0:T(8,128)(2,1)}, f32[128,2048]{1,0:T(8,128)}, bf16[2,3,128,3072]{3,2,1,0:T(8,128)(2,1)}, bf16[2,3,128,1024]{3,2,1,0:T(8,128)(2,...) custom-call(bf16[128,2048]{1,0:T(8,128)(2,1)} %bitcast.46, ...), custom_call_target="tpu_custom_call" | custom-call | tf_op jit(solution)/shard_map/backward/pallas_call | solution.py:1221
  531.3 0.0 copy-start.2
  531.4 0.0 copy-start
  531.4 1.1 reduce_sum.126
  532.5 0.1 fusion.3
  532.6 0.5 slice_bitcast_fusion.2
  533.2 0.6 slice_bitcast_fusion.1
  533.8 0.6 copy_bitcast_fusion
  534.4 0.6 copy_bitcast_fusion.2
  535.0 1.0 convert_reduce_fusion.6
  536.0 0.7 pad_maximum_fusion.2
  536.7 0.0 copy-done.2
  536.7 0.1 convert_reduce_fusion.7
  536.8 0.3 convert_reduce_fusion.3
  537.2 1.1 copy.48
  538.3 1.1 pad_maximum_fusion
  539.4 5.5 %convert_reduce_fusion = (f32[128,3072]{1,0:T(8,128)S(1)}, f32[128,3072]{1,0:T(8,128)}, f32[128,3072]{1,0:T(8,128)}) fusion(bf16[2,3,128,3072]{3,2,1,0:T(8,128)(2,1)} %get-tuple-element.66), kind=kLoop, calls=%fused_computation | loop fusion | flops 3538944 | bytes 9437184 | tf_op jit(solution)/shard_map/reduce_sum | solution.py:1327
  545.0 1.6 copy.49
  546.6 0.8 copy.61
  547.4 1.0 copy.62
  (14 shorter events, 0.1 us)
Async XLA Ops:
  531.3 5.4 copy-start.2
  531.4 5.5 copy-start
  545.0 1.6 copy-start.3
  545.0 2.4 copy-start.1

commit v6 on v5

--- a/solution.py
+++ b/solution.py
@@ -287,11 +287,13 @@
 SMALL_ROWS = 96
 
 
-def forward_kernel(n, taps, heads, *refs):
+def forward_kernel(n, taps, heads, turn, *refs):
     (tok, cot, wb, wi, wo, wg, wu, wd, wr, wig, small) = refs[:11]
     (o_rec, o_mlp, o_gate, o_vec, o_gain, o_ends, o_u, o_grad, pre, state, mixed, resid, o_norm) = refs[11:24]
     (rec, gat, sml, u_buf, og, part, sibb, got, extra, a_scr, gfull) = refs[24:35]
     sems = refs[35:]
+    if turn:
+        sems, wo_in, wd_in, (wo, wd) = refs[35:-2], wo, wd, refs[-2:]
     g_sems, r1, r2, s1, (fin, h_send, h_recv) = sems[:48], sems[48:52], sems[52:56], sems[56:60], sems[60:]
     zh, zl, y, x, c = place()
     here = (zh, zl, y, x)
@@ -367,13 +369,21 @@
         if j + 2 * ahead < len(order):
             order[j + 2 * ahead].start(False)
 
+    def turn_over(src, dst):
+        for i in range(0, src.shape[0], 128):
+            dst[:, i : i + 128] = src[i : i + 128, :].T
+
     smalls.start(True)
     smalls.start(False)
+    if turn:
+        turn_over(wo_in, wo)
     for j in range(2 * ahead):
         if j < ahead:
             order[j].start(True)
         order[j].start(False)
 
+    if turn:
+        turn_over(wd_in, wd)
     xin = tok[...].astype(F32)
     unit = xin * lax.rsqrt(jnp.mean(xin * xin, axis=-1, keepdims=True) + EPS)
     resid[...] = unit
@@ -555,6 +565,9 @@
     rr = wb.shape[0]
     length = 2 * half
     ff = wg.shape[1] // 4
+    turn = rr % 128 == 0
+    if not turn:
+        wo, wd = wo.T, wd.T
     vm = pl.BlockSpec(memory_space=pltpu.VMEM)
     hb = pl.BlockSpec(memory_space=pl.ANY)
 
@@ -579,9 +592,9 @@
     )
     count = n // 2
     return pl.pallas_call(
-        functools.partial(forward_kernel, n, taps, heads),
+        functools.partial(forward_kernel, n, taps, heads, turn),
         out_shape=tuple(o for o, _ in outs),
-        in_specs=[vm, vm] + [hb] * 9,
+        in_specs=[vm, vm, hb, hb, vm if turn else hb, hb, hb, vm if turn else hb, hb, hb, hb],
         out_specs=[s for _, s in outs],
         scratch_shapes=[
             pltpu.VMEM((2, 3, n, rr, blk), BF),
@@ -603,7 +616,8 @@
         ]
         * 16
         + row_sems() * 3
-        + [pltpu.SemaphoreType.DMA((3,)), pltpu.SemaphoreType.DMA, pltpu.SemaphoreType.DMA],
+        + [pltpu.SemaphoreType.DMA((3,)), pltpu.SemaphoreType.DMA, pltpu.SemaphoreType.DMA]
+        + ([pltpu.VMEM((rr, heads * blk), BF), pltpu.VMEM((rr, 4 * ff), BF)] if turn else []),
         compiler_params=pltpu.CompilerParams(
             collective_id=cid, has_side_effects=True, vmem_limit_bytes=VMEM_LIMIT
         ),
@@ -1309,7 +1323,7 @@
     (
         rec_w, mlp_w, gates, vec, gains_all, group_ends, u, mlp_grad, pre, state, mixed, resid, norm_own,
     ) = forward(
-        tokens[0], cotangent[0], w_branch, w_input, w_output.T, w_gate, w_up, w_down.T, w_rgate, w_igate, small, n, taps, 1,
+        tokens[0], cotangent[0], w_branch, w_input, w_output, w_gate, w_up, w_down, w_rgate, w_igate, small, n, taps, 1,
     )
     g_mlp, rec_own, resid_grad, hid, gain2_sum = mlp_block(
         norm_own, resid, gains_all, cotangent[0], group_ends, mlp_w, mlp_grad, 4

time: 549 us -> 545 us (level)
  no operation moved by 1% of the time
where the time goes in v6:
time: 545 us; the launch traced here: 544 us
  Pallas kernels  521 us (96%)
  other arithmetic  12.1 us (2%)
  local copies, waits for them, and re-layouts  10.5 us (2%)
    pallas_call x1, Pallas kernels, backward(): pl.pallas_call(functools.partial(backward_kernel, n, taps), out_shape=(sd...  227 us
    pallas_call x1, Pallas kernels, forward(): pl.pallas_call(functools.partial(forward_kernel, n, taps, heads, turn), o...  224 us
    pallas_call x1, Pallas kernels, mlp_block(): pl.pallas_call(mlp_kernel, out_shape=(jax.ShapeDtypeStruct(mlp_w.shape, B...  69.8 us

profile of v6, /device:TPU:0, one launch (start us, length us, event | category | flops | bytes accessed | tf_op | source)
XLA Modules:
  0.0 544.5 jit_solution(17870864283121585291)
XLA Ops:
  0.7 0.7 convert_element_type.49
  1.3 0.7 copy.40
  2.0 0.7 copy.41
  2.7 0.7 copy.42
  3.4 0.7 copy.43
  4.1 0.7 concatenate.22
  4.8 0.2 dynamic_update_slice.4
  5.0 1.3 fusion.2.refs_10_
  6.3 224.3 %forward.1 = (bf16[2,3,16,128,256]{4,3,2,1,0:T(8,128)(2,1)}, bf16[9,16,128,256]{3,2,1,0:T(8,128)(2,1)}, bf16[2,256,512]{2,1,0:T(8,128)(2,1)}, f32[2,16,256]{2,1,...) custom-call(bf16[128,2048]{1,0:T(8,128)(2,1)} %bitcast.42, ...), custom_call_target="tpu_custom_call" | custom-call | tf_op jit(solution)/shard_map/forward/pallas_call | solution.py:594
  230.6 69.8 %mlp_block.1 = (bf16[9,16,128,256]{3,2,1,0:T(8,128)(2,1)}, bf16[128,2048]{1,0:T(8,128)(2,1)}, f32[128,2048]{1,0:T(8,128)}, bf16[3,4,256,256]{3,2,1,0:T(8,128)(2,1)}, f32[8,2048]{1,0:T(8,128)}) custom-call(bf16[128,2048]{1,0:T(8,128)(2,1)} %get-tuple-element.42.norm, f32[128,2048]{1,0:T(8,128)} %get-tuple-element.43.resid.refs_2_, ...), custom_call_target="tpu_custom_call" | custom-call | tf_op jit(solution)/shard_map/mlp_block/pallas_call | solution.py:750
  300.5 227.0 %backward.1 = (bf16[128,2048]{1,0:T(8,128)(2,1)}, f32[128,2048]{1,0:T(8,128)}, bf16[2,3,128,3072]{3,2,1,0:T(8,128)(2,1)}, bf16[2,3,128,1024]{3,2,1,0:T(8,128)(2,...) custom-call(bf16[128,2048]{1,0:T(8,128)(2,1)} %bitcast.43, ...), custom_call_target="tpu_custom_call" | custom-call | tf_op jit(solution)/shard_map/backward/pallas_call | solution.py:1235
  527.4 0.0 copy-start.2
  527.5 0.0 copy-start
  527.5 1.1 reduce_sum.126
  528.6 0.1 fusion.3
  528.8 0.5 slice_bitcast_fusion.2
  529.3 0.6 slice_bitcast_fusion.1
  529.9 0.6 copy_bitcast_fusion
  530.5 0.6 copy_bitcast_fusion.2
  531.1 1.0 convert_reduce_fusion.6
  532.1 0.7 pad_maximum_fusion.2
  532.8 0.0 copy-done.2
  532.8 0.1 convert_reduce_fusion.7
  532.9 0.3 convert_reduce_fusion.3
  533.3 1.1 copy.44
  534.4 1.1 pad_maximum_fusion
  535.6 5.5 %convert_reduce_fusion = (f32[128,3072]{1,0:T(8,128)S(1)}, f32[128,3072]{1,0:T(8,128)}, f32[128,3072]{1,0:T(8,128)}) fusion(bf16[2,3,128,3072]{3,2,1,0:T(8,128)(2,1)} %get-tuple-element.66), kind=kLoop, calls=%fused_computation | loop fusion | flops 3538944 | bytes 9437184 | tf_op jit(solution)/shard_map/reduce_sum | solution.py:1341
  541.1 1.6 copy.45
  542.7 0.0 copy-done.3
  542.7 0.8 copy.57
  543.5 0.0 copy-done.1
  543.5 1.0 copy.58
  (12 shorter events, 0.1 us)
Async XLA Ops:
  527.4 5.4 copy-start.2
  527.5 5.5 %copy-start = (bf16[2,3,128,1024]{3,2,1,0:T(8,128)(2,1)S(1)}, bf16[2,3,128,1024]{3,2,1,0:T(8,128)(2,1)}, u32[]{:S(2)}) copy-start(bf16[2,3,128,1024]{3,2,1,0:T(8,128)(2,1)} %get-tuple-element.63) | copy-start | bytes 4718596
  541.1 1.6 copy-start.3
  541.1 2.4 copy-start.1

commit v7 on v6

--- a/solution.py
+++ b/solution.py
@@ -681,10 +681,11 @@
             sums.pass_on(k - 1)
 
         def second(d, carry):
-            total = jnp.zeros((2 * half, blk), F32)
-            for t in range(tiles):
-                total = total + mm_t(hg[t, pq], w[t, pl.ds(d * per, per)].reshape(blk, blk))
-                total = total + mm_t(hu[t, pq], w[tiles + t, pl.ds(d * per, per)].reshape(blk, blk))
+            left = jnp.concatenate([a[t, pq] for a in (hg, hu) for t in range(tiles)], axis=1)
+            right = jnp.concatenate(
+                [w[t, pl.ds(d * per, per)].reshape(blk, blk) for t in range(2 * tiles)], axis=1
+            )
+            total = mm_t(left, right)
             lanes = pl.ds(pl.multiple_of(d * blk, 128), blk)
             part[pq, 0, :, lanes] = total[:half].astype(BF)
             part[pq, 1, :, lanes] = total[half:].astype(BF)
@@ -1035,9 +1036,7 @@
             lanes = pl.ds(pl.multiple_of(t * blk, 128), blk)
 
             def tile_of(left, head):
-                return sum(
-                    mm_t(left[:, j * blk : (j + 1) * blk], rec[head, j, cut].reshape(blk, blk)) for j in range(2)
-                )
+                return mm_t(left, jnp.concatenate([rec[head, j, cut].reshape(blk, blk) for j in range(2)], axis=1))
 
             def emit(tile):
                 part[pq, 0, :, lanes] = tile[:half].astype(BF)

time: 545 us -> 545 us (level)
  no operation moved by 1% of the time
where the time goes in v7:
time: 545 us; the launch traced here: 544 us
  Pallas kernels  521 us (96%)
  other arithmetic  12.1 us (2%)
  local copies, waits for them, and re-layouts  10.5 us (2%)
    pallas_call x1, Pallas kernels, backward(): pl.pallas_call(functools.partial(backward_kernel, n, taps), out_shape=(sd...  227 us
    pallas_call x1, Pallas kernels, forward(): pl.pallas_call(functools.partial(forward_kernel, n, taps, heads, turn), o...  224 us
    pallas_call x1, Pallas kernels, mlp_block(): pl.pallas_call(mlp_kernel, out_shape=(jax.ShapeDtypeStruct(mlp_w.shape, B...  69.8 us

profile of v7, /device:TPU:0, one launch (start us, length us, event | category | flops | bytes accessed | tf_op | source)
XLA Modules:
  0.0 544.5 jit_solution(194978067275086390)
XLA Ops:
  0.7 0.7 convert_element_type.49
  1.3 0.7 copy.40
  2.0 0.7 copy.41
  2.7 0.7 copy.42
  3.4 0.7 copy.43
  4.1 0.7 concatenate.22
  4.8 0.2 dynamic_update_slice.4
  5.0 1.3 fusion.2.refs_10_
  6.3 224.3 %forward.1 = (bf16[2,3,16,128,256]{4,3,2,1,0:T(8,128)(2,1)}, bf16[9,16,128,256]{3,2,1,0:T(8,128)(2,1)}, bf16[2,256,512]{2,1,0:T(8,128)(2,1)}, f32[2,16,256]{2,1,...) custom-call(bf16[128,2048]{1,0:T(8,128)(2,1)} %bitcast.42, ...), custom_call_target="tpu_custom_call" | custom-call | tf_op jit(solution)/shard_map/forward/pallas_call | solution.py:594
  230.6 69.8 %mlp_block.1 = (bf16[9,16,128,256]{3,2,1,0:T(8,128)(2,1)}, bf16[128,2048]{1,0:T(8,128)(2,1)}, f32[128,2048]{1,0:T(8,128)}, bf16[3,4,256,256]{3,2,1,0:T(8,128)(2,1)}, f32[8,2048]{1,0:T(8,128)}) custom-call(bf16[128,2048]{1,0:T(8,128)(2,1)} %get-tuple-element.42.norm, f32[128,2048]{1,0:T(8,128)} %get-tuple-element.43.resid.refs_2_, ...), custom_call_target="tpu_custom_call" | custom-call | tf_op jit(solution)/shard_map/mlp_block/pallas_call | solution.py:751
  300.5 227.0 %backward.1 = (bf16[128,2048]{1,0:T(8,128)(2,1)}, f32[128,2048]{1,0:T(8,128)}, bf16[2,3,128,3072]{3,2,1,0:T(8,128)(2,1)}, bf16[2,3,128,1024]{3,2,1,0:T(8,128)(2,...) custom-call(bf16[128,2048]{1,0:T(8,128)(2,1)} %bitcast.43, ...), custom_call_target="tpu_custom_call" | custom-call | tf_op jit(solution)/shard_map/backward/pallas_call | solution.py:1234
  527.4 0.0 copy-start.2
  527.5 0.0 copy-start
  527.5 1.1 reduce_sum.126
  528.6 0.1 fusion.3
  528.8 0.5 slice_bitcast_fusion.2
  529.3 0.6 slice_bitcast_fusion.1
  529.9 0.6 copy_bitcast_fusion
  530.5 0.6 copy_bitcast_fusion.2
  531.1 1.0 convert_reduce_fusion.6
  532.1 0.7 pad_maximum_fusion.2
  532.8 0.0 copy-done.2
  532.8 0.1 convert_reduce_fusion.7
  532.9 0.3 convert_reduce_fusion.3
  533.3 1.1 copy.44
  534.4 1.1 pad_maximum_fusion
  535.6 5.5 %convert_reduce_fusion = (f32[128,3072]{1,0:T(8,128)S(1)}, f32[128,3072]{1,0:T(8,128)}, f32[128,3072]{1,0:T(8,128)}) fusion(bf16[2,3,128,3072]{3,2,1,0:T(8,128)(2,1)} %get-tuple-element.66), kind=kLoop, calls=%fused_computation | loop fusion | flops 3538944 | bytes 9437184 | tf_op jit(solution)/shard_map/reduce_sum | solution.py:1340
  541.1 1.6 copy.45
  542.7 0.0 copy-done.3
  542.7 0.8 copy.57
  543.5 0.0 copy-done.1
  543.5 1.0 copy.58
  (12 shorter events, 0.1 us)
Async XLA Ops:
  527.4 5.4 copy-start.2
  527.5 5.5 %copy-start = (bf16[2,3,128,1024]{3,2,1,0:T(8,128)(2,1)S(1)}, bf16[2,3,128,1024]{3,2,1,0:T(8,128)(2,1)}, u32[]{:S(2)}) copy-start(bf16[2,3,128,1024]{3,2,1,0:T(8,128)(2,1)} %get-tuple-element.63) | copy-start | bytes 4718596
  541.1 1.6 copy-start.3
  541.1 2.4 copy-start.1
